TPU v7x, 32 devices: a whole 2x2x4 slice. The times are simulated.
32 devices in a mesh: group: 2 (over x), tok: 16 (over z, y, core).
Axes of the slice: x: 2, y: 2, z: 4, core: 2. Of those that a mesh axis runs over, the one named last changes fastest.
Arguments:
- activations: bfloat16 [32768, 1024], P(('group', 'tok')), parts along dimension 0, may hold values from -14 to 14
- view_id: int32 [32768], P(('group', 'tok')), parts along dimension 0, may hold values from 0 to 15, as said below
- window_lengths: int32 [32, 3], P(('group', 'tok')), parts along dimension 0, may hold values from 1 to 512, 1024 in all within a row
- project_weight: bfloat16 [1024, 3072], replicated, may hold values from -0.1875 to 0.1875
- rate_weight: bfloat16 [1024, 4], replicated, may hold values from -0.1875 to 0.1875
- fast_start: float32 [256, 3, 4, 256], replicated, may hold values from -0.375 to 0.375
- momentum: float32 [512, 3, 4, 256], P(('group', 'tok')), parts along dimension 0, may hold values from -0.1875 to 0.1875
- norm_gain: float32 [4, 256], replicated, may hold values from 0.1 to 1.9
- output_weight: bfloat16 [1024, 1024], replicated, may hold values from -0.1875 to 0.1875
Outputs:
- mixed_views: bfloat16 [32, 1024, 1024], P(('group', 'tok')), parts along dimension 0
- momentum_next: float32 [512, 3, 4, 256], P(('group', 'tok')), parts along dimension 0
There are 2 independent parts, one for each index of `group`. A program takes and returns all parts, laid end to end along the dimension named above; an argument that names none is the same for every part. Nothing has to cross between parts.
Inputs may be any that keep to these rules, and one draw needn't show every extreme that they name: `view_id`: each block of 1024 consecutive tokens holds exactly 64 tokens of every view.
All inputs are finite; a program needn't handle non-finite values.
Results may differ from a plain program's by a relative error of at most 0.012.
The roundings to bfloat16 on the way count: a program that leaves them out, or rounds other values in their place, can miss the bound.
Values may be sent and summed in bfloat16 or wider, within the bound.
No kernel may reach another device: no remote copies, remote signals or barrier semaphores. Data moves between devices by JAX's collectives and lax.ppermute only.
A program may use at most 128 MiB of HBM per device.

v0:
```python
import math

import jax
import jax.numpy as jnp
from jax import lax
from jax.sharding import PartitionSpec as P


def unit_rms(values):
    return values * lax.rsqrt(jnp.mean(values * values, axis=-1, keepdims=True) + 1e-06)


def window_attention(arrived, lengths, head_count):
    row_total = arrived.shape[0]
    model_width = arrived.shape[1] // 3
    head_size = model_width // head_count
    queries = arrived[:, :model_width].reshape(row_total, head_count, head_size)
    keys_all = arrived[:, model_width : 2 * model_width].reshape(row_total, head_count, head_size)
    values_all = arrived[:, 2 * model_width :].reshape(row_total, head_count, head_size)
    bounds = jnp.cumsum(lengths)
    window_of = jnp.sum(jnp.arange(row_total)[:, None] >= bounds[None, :], axis=1)
    block_rows = min(512, row_total)
    block_total = row_total // block_rows
    scale_factor = 1.0 / math.sqrt(head_size)

    def attend(pieces):
        query_block, window_block = pieces
        scores = (
            jnp.einsum("qhd,khd->hqk", query_block, keys_all, preferred_element_type=jnp.float32)
            * scale_factor
        )
        same = window_block[:, None] == window_of[None, :]
        scores = jnp.where(same[None], scores, -1e30)
        highest = jnp.max(scores, axis=-1, keepdims=True)
        expo = jnp.exp(scores - highest)
        probs = (expo / jnp.sum(expo, axis=-1, keepdims=True)).astype(jnp.bfloat16)
        return jnp.einsum("hqk,khd->qhd", probs, values_all, preferred_element_type=jnp.float32)

    attended = lax.map(
        attend,
        (
            queries.reshape(block_total, block_rows, head_count, head_size),
            window_of.reshape(block_total, block_rows),
        ),
    )
    return attended.reshape(row_total, model_width)


def body(
    activations,
    view_id,
    window_lengths,
    project_weight,
    rate_weight,
    fast_start,
    momentum,
    norm_gain,
    output_weight,
):
    f32 = jnp.float32
    bf16 = jnp.bfloat16
    tok_dev, model_width = activations.shape
    shards = lax.axis_size("tok")
    head_count = rate_weight.shape[1]
    head_size = model_width // head_count
    per_view = tok_dev // shards
    shard_rows = head_size // shards
    onehot = (view_id[:, None] == jnp.arange(shards, dtype=jnp.int32)[None, :]).astype(jnp.int32)
    rank_in_view = jnp.sum(jnp.cumsum(onehot, axis=0) * onehot, axis=1) - 1
    slot_index = view_id * per_view + rank_in_view
    ordering = jnp.argsort(slot_index)
    projected = jnp.dot(activations, project_weight, preferred_element_type=f32).astype(bf16)
    sent = projected[ordering].reshape(shards, per_view, 3 * model_width)
    arrived = lax.all_to_all(sent, "tok", split_axis=0, concat_axis=0, tiled=True).reshape(
        tok_dev, 3 * model_width
    )
    queries = projected[:, :model_width].astype(f32).reshape(tok_dev, head_count, head_size)
    keys_all = (
        projected[:, model_width : 2 * model_width]
        .astype(f32)
        .reshape(tok_dev, head_count, head_size)
    )
    values_all = projected[:, 2 * model_width :].astype(f32).reshape(tok_dev, head_count, head_size)
    rate = jax.nn.softplus(jnp.dot(activations, rate_weight, preferred_element_type=f32)) * (
        0.1 / math.sqrt(tok_dev * shards)
    )
    key_unit = unit_rms(keys_all).astype(bf16)
    fast_round = fast_start.astype(bf16)
    pre_gate = jnp.einsum("thd,dhf->thf", key_unit, fast_round[:, 0], preferred_element_type=f32)
    pre_up = jnp.einsum("thd,dhf->thf", key_unit, fast_round[:, 1], preferred_element_type=f32)
    gate_sig = jax.nn.sigmoid(pre_gate)
    hidden = (pre_gate * gate_sig * pre_up).astype(bf16)
    back_out = (-rate[:, :, None] * values_all).astype(bf16)
    back_hidden = jnp.einsum("thd,dhf->thf", back_out, fast_round[:, 2], preferred_element_type=f32)
    back_gate = (back_hidden * pre_up * gate_sig * (1.0 + pre_gate * (1.0 - gate_sig))).astype(bf16)
    back_up = (back_hidden * pre_gate * gate_sig).astype(bf16)
    first_row = lax.axis_index("tok") * shard_rows
    grad_gate = jnp.einsum("thr,thf->rhf", key_unit, back_gate, preferred_element_type=f32)
    grad_up = jnp.einsum("thr,thf->rhf", key_unit, back_up, preferred_element_type=f32)
    grad_down = jnp.einsum("thr,thf->rhf", back_out, hidden, preferred_element_type=f32)
    total = lax.psum(jnp.stack([grad_gate, grad_up, grad_down], axis=1), "tok")
    gradient = lax.dynamic_slice_in_dim(total, first_row, shard_rows, 0)
    momentum_next = 0.9 * momentum + gradient
    own_start = lax.dynamic_slice_in_dim(fast_start, first_row, shard_rows, 0)
    moved = own_start - momentum_next
    factor = jnp.sqrt(jnp.sum(own_start * own_start, axis=-1, keepdims=True)) / jnp.sqrt(
        jnp.sum(moved * moved, axis=-1, keepdims=True) + 1e-06
    )
    fast_share = (moved * factor).astype(bf16)
    fast_full = lax.all_gather(fast_share, "tok", axis=0, tiled=True)
    query_unit = unit_rms(queries).astype(bf16)
    query_gate = jnp.einsum("thd,dhf->thf", query_unit, fast_full[:, 0], preferred_element_type=f32)
    query_up = jnp.einsum("thd,dhf->thf", query_unit, fast_full[:, 1], preferred_element_type=f32)
    query_hidden = (query_gate * jax.nn.sigmoid(query_gate) * query_up).astype(bf16)
    fast_out = jnp.einsum("thf,dhf->thd", query_hidden, fast_full[:, 2], preferred_element_type=f32)
    normed = (unit_rms(fast_out) * norm_gain[None]).reshape(tok_dev, model_width).astype(bf16)
    normed_sent = normed[ordering].reshape(shards, per_view, model_width)
    normed_views = lax.all_to_all(
        normed_sent, "tok", split_axis=0, concat_axis=0, tiled=True
    ).reshape(tok_dev, model_width)
    attended = window_attention(arrived, window_lengths[0], head_count)
    combined = (normed_views.astype(f32) + attended).astype(bf16)
    mixed = jnp.dot(combined, output_weight, preferred_element_type=f32).astype(bf16)
    return (mixed[None], momentum_next)


def solution(mesh):
    in_specs = (
        P(("group", "tok"), None),
        P(("group", "tok")),
        P(("group", "tok"), None),
        P(),
        P(),
        P(),
        P(("group", "tok"), None, None, None),
        P(),
        P(),
    )
    out_specs = (P(("group", "tok"), None, None), P(("group", "tok"), None, None, None))
    return jax.shard_map(body, mesh=mesh, in_specs=in_specs, out_specs=out_specs, check_vma=False)
```

profile of v0, /device:TPU:0, one launch (start us, length us, event | category | flops | bytes accessed | tf_op | source)
XLA Modules:
  0.0 413.4 jit_solution(2239238047977006569)
XLA Ops:
  7.2 0.8 fusion.66
  8.0 4.5 %reduce-window.18 = s32[16,8,128]{2,1,0:T(8,128)S(1)} reduce-window(s32[16,8,128]{2,1,0:T(8,128)S(1)} %fusion.66, s32[]{:T(128)} %copy.294), window={size=1x1x128 pad=0_0x0_0x127_0}, to_apply=%region_6.7 | reduce-window | flops 2080768 | bytes 131076 | tf_op jit(solution)/shard_map/reduce-window
  12.9 0.7 fusion.65
  13.7 0.7 add_add_fusion
  14.3 4.4 %sort.17 = (s32[1024]{0:T(1024)}, s32[1024]{0:T(1024)S(1)}) sort(s32[1024]{0:T(1024)S(1)} %add_add_fusion, s32[1024]{0:T(1024)S(1)} %iota.16), dimensions={0}, to_apply=%region_9.10 | sort | flops 10240 | bytes 16384 | tf_op jit(solution)/shard_map/jit(argsort)/sort | solution.py:71
  18.7 11.3 %convolution_convert_fusion = bf16[1024,3072]{1,0:T(8,128)(2,1)} fusion(bf16[1024,1024]{1,0:T(8,128)(2,1)S(1)} %copy-done, bf16[1024,3072]{1,0:T(8,128)(2,1)} %param.14), kind=kOutput, calls=%fused_computation.20 | convolution fusion | flops 6445596672 | bytes 14680064 | tf_op jit(solution)/shard_map/dot_general | solution.py:72
  30.0 15.8 %gather_fusion.1 = bf16[1024,3072]{1,0:T(8,128)(2,1)} fusion(bf16[1024,3072]{1,0:T(8,128)(2,1)} %convolution_convert_fusion, s32[1024]{0:T(1024)S(1)} %fusion.69), kind=kCustom, calls=%fused_computation.1 | custom fusion | bytes 12587008 | tf_op jit(solution)/shard_map/gather | solution.py:73
  45.8 7.4 %all-to-all-start.1 = ((bf16[16,64,3072]{2,1,0:T(8,128)(2,1)}), bf16[16,64,3072]{2,1,0:T(8,128)(2,1)}, u32[]{:S(2)}, u32[]{:S(2)}) async-start(bf16[16,64,3072]{2,1,0:T(8,128)(2,1)} %bitcast.200), calls=%async_computation.1 | async-start | bytes 12582912 | tf_op jit(solution)/shard_map/all_to_all | solution.py:74
  53.5 7.9 %slice_convert_fusion.2 = (f32[1024,1024]{1,0:T(8,128)}, f32[1024,1024]{1,0:T(8,128)}, f32[1024,1024]{1,0:T(8,128)}) fusion(bf16[1024,3072]{1,0:T(8,128)(2,1)} %convolution_convert_fusion), kind=kLoop, calls=%fused_computation.61 | loop fusion | flops 3145728 | bytes 18874368 | tf_op jit(solution)/shard_map/reshape | solution.py:83
  61.4 5.4 %copy.203 = f32[1024,1024]{0,1:T(8,128)} copy(f32[1024,1024]{1,0:T(8,128)} %get-tuple-element.128) | data formatting | bytes 8388608 | tf_op jit(solution)/shard_map/reshape | solution.py:81
  66.8 2.7 multiply_reduce_fusion.1
  69.5 5.4 %copy.206 = f32[1024,4,256]{2,0,1:T(8,128)} copy(f32[1024,4,256]{0,2,1:T(8,128)} %bitcast.199) | data formatting | bytes 8388608 | tf_op jit(solution)/shard_map/reshape | solution.py:81
  74.9 2.5 copy.276
  77.4 0.6 copy-done.4
  78.0 0.7 multiply_convert_fusion.1
  78.7 0.7 fusion.58
  79.5 0.7 fusion.68
  80.2 0.7 fusion.59
  80.9 0.8 copy-done.5
  81.7 1.4 fusion.56
  83.1 1.6 fusion.49
  84.7 3.0 fusion.52
  87.7 2.4 fusion.46
  90.1 2.0 pad_maximum_fusion
  92.3 4.1 copy.199
  96.4 171.1 %all-reduce.2.cloned.1.call-done = f32[256,3,4,256]{3,0,2,1:T(8,128)} async-done(((f32[256,3,4,256]{3,0,2,1:T(8,128)}), f32[256,3,4,256]{3,0,2,1:T(8,128)}) %all-reduce.2.cloned.1.call-update) | async-done | bytes 3145744 | tf_op jit(solution)/shard_map/psum | solution.py:101
  267.6 1.2 multiply_reduce_fusion.3
  268.8 1.0 multiply_convert_fusion.2
  269.8 0.7 copy.213
  270.5 5.6 %reshape.180 = f32[1024,4,256]{2,1,0:T(4,128)} reshape(f32[1024,1024]{1,0:T(8,128)} %get-tuple-element.127) | data formatting | bytes 8388608 | tf_op jit(solution)/shard_map/reshape | solution.py:77
  276.4 3.6 multiply_reduce_fusion
  280.1 1.4 multiply_convert_fusion
  281.5 0.8 copy.232
  282.3 27.2 %all-gather.2.cloned.1.call-done = bf16[256,3,4,256]{3,2,1,0:T(4,128)(2,1)} async-done(((bf16[16,3,4,256]{3,2,1,0:T(4,128)(2,1)}), bf16[256,3,4,256]{3,2,1,0:T(4,128)(2,1)}) %all-gather.2.cloned.1.call-update) | async-done | bytes 1572880 | tf_op jit(solution)/shard_map/all_gather | solution.py:110
  309.5 2.7 fusion.77
  312.2 1.1 copy.246
  313.3 0.3 copy.247
  313.6 3.8 fusion.41
  317.4 5.0 %fusion.12 = (f32[1024,4]{0,1:T(4,128)S(1)}, f32[4,256,1024]{2,1,0:T(8,128)}) fusion(f32[4,256,1024]{1,2,0:T(8,128)} %fusion.41, bf16[1024,4,256]{2,1,0:T(4,128)(2,1)S(1)} %multiply_convert_fusion, bf16[256,1,4,256]{0,3,2,1:T(8,128)(2,1)S(1)} %copy.247, bf16[256,1,4,256]{3,2,1,0:T(4,128)(2,1)S(1)} %copy-done.7), kind=kOutput, calls=%fused_computation.27 | convolution fusion | flops 1082126336 | bytes 11550720 | tf_op jit(solution)/shard_map/thf,dhf->thd/dot_general | solution.py:115
  322.4 3.9 fusion.14
  326.4 2.9 copy.225
  329.2 5.4 %gather_fusion = bf16[1024,1024]{1,0:T(8,128)(2,1)} fusion(bf16[1024,1024]{1,0:T(8,128)(2,1)S(1)} %copy.225, s32[1024]{0:T(1024)S(1)} %fusion.69), kind=kCustom, calls=%fused_computation | custom fusion | bytes 4198400 | tf_op jit(solution)/shard_map/gather | solution.py:117
  334.6 4.7 %all-to-all-start = ((bf16[16,64,1024]{2,1,0:T(8,128)(2,1)}), bf16[16,64,1024]{2,1,0:T(8,128)(2,1)}, u32[]{:S(2)}, u32[]{:S(2)}) async-start(bf16[16,64,1024]{2,1,0:T(8,128)(2,1)} %bitcast.203), calls=%async_computation | async-start | bytes 4194304 | tf_op jit(solution)/shard_map/all_to_all | solution.py:118
  339.3 5.8 %fusion.76 = (bf16[1024,1024]{1,0:T(8,128)(2,1)}, bf16[1024,1024]{1,0:T(8,128)(2,1)}, bf16[1024,1024]{1,0:T(8,128)(2,1)}) fusion(bf16[1024,3072]{1,0:T(8,128)(2,1)} %bitcast.32), kind=kLoop, calls=%fused_computation.113 | loop fusion | bytes 12582912 | tf_op jit(solution)/shard_map/slice | solution.py:19
  345.1 2.9 copy.226
  347.9 2.6 copy.229
  350.5 2.9 copy.227
  353.4 2.6 copy.230
  356.0 4.5 %reshape_reshape.3 = bf16[2,512,4,256]{3,2,1,0:T(4,128)(2,1)} reshape(bf16[1024,1024]{1,0:T(8,128)(2,1)} %get-tuple-element.131) | data formatting | bytes 4194304 | tf_op jit(solution)/shard_map/reshape;reshape | solution.py:42
  360.5 33.8 %while.10 = (s32[]{:T(128)}, f32[2,512,4,256]{3,2,1,0:T(4,128)}, s32[2,512]{1,0:T(2,128)S(1)}, s32[1024]{0:T(1024)S(1)}, bf16[2,512,4,256]{3,2,1,0:T(4,128)(2,1)...) while((s32[]{:T(128)}, f32[2,512,4,256]{3,2,1,0:T(4,128)}, ...), condition=%wide.region_15.16_spmd, body=%wide.region_12.15_spmd.sunk | while | flops 2164786176 | bytes 65038996 | solution.py:39
  360.5 1.7 constant_dynamic-slice_fusion.4
  362.4 1.3 fusion.100
  363.7 0.4 broadcast_compare_fusion.2
  364.1 5.8 %fusion.101 = (f32[4,512]{1,0:T(4,128)S(1)}, f32[4,512,1024]{2,1,0:T(8,128)}) fusion(f32[4,512,1024]{2,1,0:T(8,128)S(1)} %fusion.100, pred[512,1024]{1,0:T(8,128)(4,1)S(1)} %broadcast_compare_fusion.2), kind=kOutput, calls=%fused_computation.112.clone.1 | output fusion | flops 12583935 | bytes 17309696 | tf_op jit(solution)/shard_map/while/body/eval_jaxpr/sub | solution.py:35
  369.9 4.7 %fusion.102 = f32[1,512,4,256]{3,1,2,0:T(8,128)S(1)} fusion(bf16[1024,4,256]{2,0,1:T(8,128)(2,1)S(1)} %copy-done.6, f32[4,512,1024]{2,1,0:T(8,128)} %get-tuple-element.182, f32[4,512]{1,0:T(4,128)S(1)} %get-tuple-element.183), kind=kOutput, calls=%fused_computation.12.clone.1 | convolution fusion | flops 1077936128 | bytes 12591104 | tf_op jit(solution)/shard_map/while/body/eval_jaxpr/hqk,khd->qhd/dot_general | solution.py:37
  374.7 2.7 copy_dynamic-update-slice_fusion.2
  377.4 1.7 constant_dynamic-slice_fusion.4
  379.3 1.3 fusion.100
  380.6 0.4 broadcast_compare_fusion.2
  381.0 5.8 %fusion.101 = (f32[4,512]{1,0:T(4,128)S(1)}, f32[4,512,1024]{2,1,0:T(8,128)}) fusion(f32[4,512,1024]{2,1,0:T(8,128)S(1)} %fusion.100, pred[512,1024]{1,0:T(8,128)(4,1)S(1)} %broadcast_compare_fusion.2), kind=kOutput, calls=%fused_computation.112.clone.1 | output fusion | flops 12583935 | bytes 17309696 | tf_op jit(solution)/shard_map/while/body/eval_jaxpr/sub | solution.py:35
  386.8 4.7 %fusion.102 = f32[1,512,4,256]{3,1,2,0:T(8,128)S(1)} fusion(bf16[1024,4,256]{2,0,1:T(8,128)(2,1)S(1)} %copy-done.6, f32[4,512,1024]{2,1,0:T(8,128)} %get-tuple-element.182, f32[4,512]{1,0:T(4,128)S(1)} %get-tuple-element.183), kind=kOutput, calls=%fused_computation.12.clone.1 | convolution fusion | flops 1077936128 | bytes 12591104 | tf_op jit(solution)/shard_map/while/body/eval_jaxpr/hqk,khd->qhd/dot_general | solution.py:37
  391.6 2.7 copy_dynamic-update-slice_fusion.2
  394.2 5.1 %copy.255 = f32[128,8,4,256]{3,1,2,0:T(8,128)} copy(f32[128,8,4,256]{3,2,1,0:T(4,128)} %bitcast.46) | data formatting | bytes 8388608
  399.4 7.2 %convert_bitcast_fusion = bf16[1,1024,1024]{2,1,0:T(8,128)(2,1)} fusion(bf16[1024,1024]{1,0:T(8,128)(2,1)} %param.19, f32[1024,1024]{1,0:T(8,128)} %bitcast.207, bf16[1024,1024]{1,0:T(8,128)(2,1)} %bitcast.40), kind=kOutput, calls=%fused_computation.62 | convolution fusion | flops 2151677952 | bytes 10485760 | tf_op jit(solution)/shard_map/dot_general | solution.py:123
  (50 shorter events, 1.7 us)
Async XLA Ops:
  7.2 11.6 %copy-start = (bf16[1024,1024]{1,0:T(8,128)(2,1)S(1)}, bf16[1024,1024]{1,0:T(8,128)(2,1)}, u32[]{:S(2)}) copy-start(bf16[1024,1024]{1,0:T(8,128)(2,1)} %param.11) | copy-start | bytes 6291460
  45.8 288.8 %all-to-all-start.1 = ((bf16[16,64,3072]{2,1,0:T(8,128)(2,1)}), bf16[16,64,3072]{2,1,0:T(8,128)(2,1)}, u32[]{:S(2)}, u32[]{:S(2)}) async-start(bf16[16,64,3072]{2,1,0:T(8,128)(2,1)} %bitcast.200), calls=%async_computation.1 | async-start | bytes 12582912 | tf_op jit(solution)/shard_map/all_to_all | solution.py:74
  53.2 214.3 %all-reduce.2.cloned.1.call-start = ((), (), s32[]{:S(2)}) async-start(), calls=%async_computation.2 | async-start | bytes 6291456 | tf_op jit(solution)/shard_map/psum | solution.py:101
  74.9 3.1 copy-start.4
  78.7 0.7 copy-start.9
  79.5 2.2 copy-start.5
  92.0 175.5 %copy-start.8 = (f32[16,3,4,256]{3,2,1,0:T(4,128)S(1)}, f32[16,3,4,256]{3,2,1,0:T(4,128)}, u32[]{:S(2)}) copy-start(f32[16,3,4,256]{3,2,1,0:T(4,128)} %param.17) | copy-start | bytes 589828
  92.1 217.4 %all-gather.2.cloned.1.call-start = ((), (), s32[]{:S(2)}) async-start(), calls=%async_computation.3 | async-start | bytes 1671168 | tf_op jit(solution)/shard_map/all_gather | solution.py:110
  270.5 5.6 %copy-start.11 = (s32[1,3]{1,0:T(1,128)S(1)}, s32[1,3]{1,0:T(1,128)}, u32[]{:S(2)}) copy-start(s32[1,3]{1,0:T(1,128)} %param.13) | copy-start | bytes 40
  276.4 3.7 copy-start.3
  313.6 3.8 copy-start.7
  317.4 5.0 %copy-start.10 = (f32[4,256]{1,0:T(4,128)S(1)}, f32[4,256]{1,0:T(4,128)}, u32[]{:S(2)}) copy-start(f32[4,256]{1,0:T(4,128)} %param.18) | copy-start | bytes 12292
  334.6 64.8 %all-to-all-start = ((bf16[16,64,1024]{2,1,0:T(8,128)(2,1)}), bf16[16,64,1024]{2,1,0:T(8,128)(2,1)}, u32[]{:S(2)}, u32[]{:S(2)}) async-start(bf16[16,64,1024]{2,1,0:T(8,128)(2,1)} %bitcast.203), calls=%async_computation | async-start | bytes 4194304 | tf_op jit(solution)/shard_map/all_to_all | solution.py:118
  360.5 1.9 copy-start.2
  364.1 5.8 %copy-start.6 = (bf16[1024,4,256]{2,0,1:T(8,128)(2,1)S(1)}, bf16[1024,4,256]{2,0,1:T(8,128)(2,1)}, u32[]{:S(2)}) copy-start(bf16[1024,4,256]{2,0,1:T(8,128)(2,1)} %get-tuple-element.206) | copy-start | bytes 6291460 | tf_op jit(solution)/shard_map/while
  377.4 1.9 copy-start.2
  381.0 5.8 %copy-start.6 = (bf16[1024,4,256]{2,0,1:T(8,128)(2,1)S(1)}, bf16[1024,4,256]{2,0,1:T(8,128)(2,1)}, u32[]{:S(2)}) copy-start(bf16[1024,4,256]{2,0,1:T(8,128)(2,1)} %get-tuple-element.206) | copy-start | bytes 6291460 | tf_op jit(solution)/shard_map/while
  399.4 7.2 %copy-start.1 = (bf16[1024,1024]{1,0:T(8,128)(2,1)S(1)}, bf16[1024,1024]{1,0:T(8,128)(2,1)}, u32[]{:S(2)}) copy-start(bf16[1024,1024]{1,0:T(8,128)(2,1)} %param.11) | copy-start | bytes 6291460
Sparse Core Ops, SparseCore 0:
  92.2 175.3 all-reduce.1
  270.6 38.8 all-gather.1
where the time goes:
time: 415 us; the launch traced here: 413 us
  waiting for transfers between devices  198 us (48%)
  local copies, waits for them, and re-layouts  89.9 us (22%)
  matrix products  49.8 us (12%)
  other arithmetic  48.4 us (12%)
  between operations  14.3 us (3%)
  starting transfers between devices  12.6 us (3%)
    psum x1, waiting for transfers between devices, body(): total = lax.psum(jnp.stack([grad_gate, grad_up, grad_down], axis=1), 'tok')  171 us
    all_gather x1, waiting for transfers between devices, body(): fast_full = lax.all_gather(fast_share, 'tok', axis=0, tiled=True)  27.2 us
    gather x1, local copies, waits for them, and re-layouts, body(): sent = projected[ordering].reshape(shards, per_view, 3 * model_width)  15.8 us
    unnamed x26, local copies, waits for them, and re-layouts  15.4 us
    sub x2, other arithmetic, attend(): expo = jnp.exp(scores - highest)  11.7 us
    dot_general x1, matrix products, body(): jnp.dot(activations, project_weight, preferred_element_type=f32)  11.3 us
    reshape x2, local copies, waits for them, and re-layouts, body(): keys_all = projected[:, model_width:2 * model_width].astype(f32).reshape(...  10.8 us
    dot_general x2, matrix products, attend(): jnp.einsum('hqk,khd->qhd', probs, values_all, preferred_element_type=jnp....  9.47 us
  transfers between devices with their start and end apart: 4, of which 2 were waited for; matrix products, arithmetic and copies ran while one was open for 34% of the time, Pallas kernels for 0%

commit v1 on v0

v1 whole, which is shorter than its diff:
```python
import math

import jax
import jax.numpy as jnp
from jax import lax
from jax.experimental import pallas as pl
from jax.experimental.pallas import tpu as pltpu
from jax.sharding import PartitionSpec as P

F32 = jnp.float32
BF16 = jnp.bfloat16
VMEM_LIMIT = 60 * 1024 * 1024


def dot(a, b):
    return jnp.dot(a, b, preferred_element_type=F32)


def dot_tn(a, b):
    return lax.dot_general(a, b, (((0,), (0,)), ((), ())), preferred_element_type=F32)


def dot_nt(a, b):
    return lax.dot_general(a, b, (((1,), (1,)), ((), ())), preferred_element_type=F32)


def bit_reverse(value, width):
    out = 0
    for bit in range(width):
        out |= ((value >> bit) & 1) << (width - 1 - bit)
    return out


def params(grid_rank=1):
    return pltpu.CompilerParams(
        dimension_semantics=("arbitrary",) * grid_rank, vmem_limit_bytes=VMEM_LIMIT
    )


def cost(flops, nbytes, transcendentals=0):
    return pl.CostEstimate(
        flops=int(flops), bytes_accessed=int(nbytes), transcendentals=int(transcendentals)
    )


def group_by_view(view_id, activations, shards):
    tok_dev, width = activations.shape
    per_view = tok_dev // shards
    chunk = 256
    tile = 256

    def kernel(view_ref, act_ref, out_ref, slot_ref):
        @pl.when(pl.program_id(0) == 0)
        def _():
            rows = lax.broadcasted_iota(jnp.int32, (chunk, chunk), 0)
            cols = lax.broadcasted_iota(jnp.int32, (chunk, chunk), 1)
            upper = jnp.where(rows < cols, 1.0, 0.0).astype(BF16)
            views = lax.broadcasted_iota(jnp.int32, (shards, chunk), 0)
            before = jnp.zeros((shards, 1), F32)
            for start in range(0, tok_dev, chunk):
                member = views == view_ref[:, start : start + chunk]
                hot = jnp.where(member, 1.0, 0.0)
                rank = dot(hot.astype(BF16), upper) + before
                slot = jnp.where(member, rank + (views * per_view).astype(F32), 0.0)
                slot_ref[:, start : start + chunk] = jnp.sum(slot, axis=0, keepdims=True).astype(
                    jnp.int32
                )
                before = before + jnp.sum(hot, axis=1, keepdims=True)

        target = lax.broadcasted_iota(jnp.int32, (tile, tok_dev), 0) + pl.program_id(0) * tile
        pick = jnp.where(target == slot_ref[...], 1.0, 0.0).astype(BF16)
        out_ref[...] = dot(pick, act_ref[...]).astype(BF16)

    return pl.pallas_call(
        kernel,
        grid=(tok_dev // tile,),
        in_specs=[
            pl.BlockSpec((1, tok_dev), lambda i: (0, 0)),
            pl.BlockSpec((tok_dev, width), lambda i: (0, 0)),
        ],
        out_specs=pl.BlockSpec((tile, width), lambda i: (i, 0)),
        out_shape=jax.ShapeDtypeStruct((tok_dev, width), BF16),
        scratch_shapes=[pltpu.VMEM((1, tok_dev), jnp.int32)],
        compiler_params=params(),
        cost_estimate=cost(2 * tok_dev * tok_dev * width, 4 * tok_dev * width),
        name="group_by_view",
    )(view_id.reshape(1, tok_dev), activations)


def fast_gradient(position, activations, project_weight, rate_weight, fast_round, shards):
    tok_dev, width = activations.shape
    heads = rate_weight.shape[1]
    size = width // heads
    slab = size // shards
    stages = shards.bit_length() - 1
    tile = 256
    scale = 0.1 / math.sqrt(tok_dev * shards)
    half = size // 2

    def kernel(pos_ref, act_ref, wk_ref, wv_ref, rate_w_ref, fast_ref, keep_ref, send_ref,
               rate_ref, key_ref, out_ref, hid_ref, gate_ref, grad_ref):
        head = pl.program_id(0)

        @pl.when(head == 0)
        def _():
            raw = dot(act_ref[...], rate_w_ref[...])
            rate_ref[...] = (jnp.maximum(raw, 0.0) + jnp.log1p(jnp.exp(-jnp.abs(raw)))) * scale

        w_gate = fast_ref[:, 0:size]
        w_up = fast_ref[:, size : 2 * size]
        w_down = fast_ref[:, 2 * size : 3 * size]
        for start in range(0, tok_dev, tile):
            rows = slice(start, start + tile)
            act = act_ref[rows, :]
            keys = dot(act, wk_ref[...]).astype(BF16).astype(F32)
            values = dot(act, wv_ref[...]).astype(BF16).astype(F32)
            key_unit = (
                keys * lax.rsqrt(jnp.mean(keys * keys, axis=-1, keepdims=True) + 1e-06)
            ).astype(BF16)
            lanes = lax.broadcasted_iota(jnp.int32, (tile, heads), 1)
            rate = jnp.sum(
                jnp.where(lanes == head, rate_ref[rows, :], 0.0), axis=1, keepdims=True
            )
            back_out = (-rate * values).astype(BF16)
            pre_gate = dot(key_unit, w_gate)
            pre_up = dot(key_unit, w_up)
            back_hidden = dot(back_out, w_down)
            sig = jax.nn.sigmoid(pre_gate)
            act_gate = pre_gate * sig
            key_ref[rows, :] = key_unit
            out_ref[rows, :] = back_out
            hid_ref[rows, :] = (act_gate * pre_up).astype(BF16)
            gate_ref[rows, 0:size] = (
                back_hidden * pre_up * sig * (1.0 + pre_gate * (1.0 - sig))
            ).astype(BF16)
            gate_ref[rows, size : 2 * size] = (back_hidden * act_gate).astype(BF16)
        grad_ref[:, 0 : 2 * size] = dot_tn(key_ref[...], gate_ref[...])
        grad_ref[:, 2 * size : 3 * size] = dot_tn(out_ref[...], hid_ref[...])
        for place in range(shards):
            owner = pos_ref[0] ^ bit_reverse(place, stages)
            rows = grad_ref[pl.ds(pl.multiple_of(owner * slab, slab), slab), :]
            if place < shards // 2:
                keep_ref[place * slab : (place + 1) * slab, :] = rows
            else:
                low = place * slab - half
                send_ref[low : low + slab, :] = rows.astype(BF16)

    return pl.pallas_call(
        kernel,
        grid_spec=pltpu.PrefetchScalarGridSpec(
            num_scalar_prefetch=1,
            grid=(heads,),
            in_specs=[
                pl.BlockSpec((tok_dev, width), lambda h, p: (0, 0)),
                pl.BlockSpec((width, size), lambda h, p: (0, heads + h)),
                pl.BlockSpec((width, size), lambda h, p: (0, 2 * heads + h)),
                pl.BlockSpec((width, heads), lambda h, p: (0, 0)),
                pl.BlockSpec((size, 3 * size), lambda h, p: (0, h)),
            ],
            out_specs=[
                pl.BlockSpec((half, 3 * size), lambda h, p: (0, h)),
                pl.BlockSpec((half, 3 * size), lambda h, p: (0, h)),
            ],
            scratch_shapes=[
                pltpu.VMEM((tok_dev, heads), F32),
                pltpu.VMEM((tok_dev, size), BF16),
                pltpu.VMEM((tok_dev, size), BF16),
                pltpu.VMEM((tok_dev, size), BF16),
                pltpu.VMEM((tok_dev, 2 * size), BF16),
                pltpu.VMEM((size, 3 * size), F32),
            ],
        ),
        out_shape=[
            jax.ShapeDtypeStruct((half, 3 * width), F32),
            jax.ShapeDtypeStruct((half, 3 * width), BF16),
        ],
        compiler_params=params(),
        cost_estimate=cost(
            2 * tok_dev * width * (2 * width + 6 * size),
            2 * tok_dev * width + 4 * width * width + 6 * size * width + 9 * size * width,
            4 * tok_dev * width,
        ),
        name="fast_gradient",
    )(position, activations, project_weight, project_weight, rate_weight, fast_round)


def add_and_halve(keep, received):
    rows, width = keep.shape
    half = rows // 2
    cols = width // 4

    def kernel(keep_ref, got_ref, stay_ref, go_ref):
        total = keep_ref[...] + got_ref[...].astype(F32)
        stay_ref[...] = total[:half]
        go_ref[...] = total[half:].astype(BF16)

    return pl.pallas_call(
        kernel,
        grid=(4,),
        in_specs=[pl.BlockSpec((rows, cols), lambda i: (0, i))] * 2,
        out_specs=[pl.BlockSpec((half, cols), lambda i: (0, i))] * 2,
        out_shape=[
            jax.ShapeDtypeStruct((half, width), F32),
            jax.ShapeDtypeStruct((half, width), BF16),
        ],
        compiler_params=params(),
        cost_estimate=cost(rows * width, 9 * rows * width),
        name="add_and_halve",
    )(keep, received)


def update_rows(keep, received, momentum, own_start, size):
    rows, width = keep.shape

    def kernel(keep_ref, got_ref, mom_ref, start_ref, next_ref, share_ref):
        for low in range(0, width, size):
            cols = slice(low, low + size)
            moment = 0.9 * mom_ref[:, cols] + (keep_ref[:, cols] + got_ref[:, cols].astype(F32))
            next_ref[:, cols] = moment
            start = start_ref[:, cols]
            moved = start - moment
            factor = jnp.sqrt(jnp.sum(start * start, axis=-1, keepdims=True)) / jnp.sqrt(
                jnp.sum(moved * moved, axis=-1, keepdims=True) + 1e-06
            )
            share_ref[:, cols] = (moved * factor).astype(BF16)

    return pl.pallas_call(
        kernel,
        out_shape=[
            jax.ShapeDtypeStruct((rows, width), F32),
            jax.ShapeDtypeStruct((rows, width), BF16),
        ],
        cost_estimate=cost(8 * rows * width, 20 * rows * width),
        name="update_rows",
    )(keep, received, momentum, own_start)


def project_and_attend(window_ends, arrived, project_weight, heads):
    tok_dev, width = arrived.shape
    size = width // heads
    windows = window_ends.shape[0]
    tile = 256
    scale = 1.0 / math.sqrt(size)

    def kernel(ends_ref, x_ref, wq_ref, wk_ref, wv_ref, unit_ref, att_ref):
        x = x_ref[...]
        queries = dot(x, wq_ref[...]).astype(BF16)
        keys = dot(x, wk_ref[...]).astype(BF16)
        values = dot(x, wv_ref[...]).astype(BF16)
        wide = queries.astype(F32)
        unit_ref[...] = (
            wide * lax.rsqrt(jnp.mean(wide * wide, axis=-1, keepdims=True) + 1e-06)
        ).astype(BF16)
        key_place = lax.broadcasted_iota(jnp.int32, (1, tok_dev), 1)
        key_window = jnp.zeros((1, tok_dev), jnp.int32)
        for w in range(windows):
            key_window += (key_place >= ends_ref[w]).astype(jnp.int32)
        for start in range(0, tok_dev, tile):
            place = lax.broadcasted_iota(jnp.int32, (tile, 1), 0) + start
            window = jnp.zeros((tile, 1), jnp.int32)
            for w in range(windows):
                window += (place >= ends_ref[w]).astype(jnp.int32)
            scores = dot_nt(queries[start : start + tile], keys) * scale
            scores = jnp.where(window == key_window, scores, -1e30)
            highest = jnp.max(scores, axis=-1, keepdims=True)
            expo = jnp.exp(scores - highest)
            total = jnp.sum(expo, axis=-1, keepdims=True)
            att_ref[start : start + tile, :] = dot(expo.astype(BF16), values) / total

    return pl.pallas_call(
        kernel,
        grid_spec=pltpu.PrefetchScalarGridSpec(
            num_scalar_prefetch=1,
            grid=(heads,),
            in_specs=[
                pl.BlockSpec((tok_dev, width), lambda h, e: (0, 0)),
                pl.BlockSpec((width, size), lambda h, e: (0, h)),
                pl.BlockSpec((width, size), lambda h, e: (0, heads + h)),
                pl.BlockSpec((width, size), lambda h, e: (0, 2 * heads + h)),
            ],
            out_specs=[
                pl.BlockSpec((tok_dev, size), lambda h, e: (0, h)),
                pl.BlockSpec((tok_dev, size), lambda h, e: (0, h)),
            ],
        ),
        out_shape=[
            jax.ShapeDtypeStruct((tok_dev, width), BF16),
            jax.ShapeDtypeStruct((tok_dev, width), F32),
        ],
        compiler_params=params(),
        cost_estimate=cost(
            2 * tok_dev * width * (3 * width + 2 * tok_dev),
            8 * tok_dev * width + 6 * width * width,
            heads * tok_dev * tok_dev,
        ),
        name="project_and_attend",
    )(window_ends, arrived, project_weight, project_weight, project_weight)


def apply_fast(position, gathered, unit, attended, norm_gain, output_weight, shards):
    tok_dev, width = unit.shape
    heads, size = norm_gain.shape
    slab = size // shards
    stages = shards.bit_length() - 1
    tile = 256
    parts = len(gathered)
    part_rows = size // parts

    def kernel(pos_ref, *refs):
        part_refs = refs[:parts]
        unit_ref, att_ref, gain_ref, ow_ref, mix_ref, wide_ref, fast_ref = refs[parts:]

        @pl.when(pl.program_id(0) == 0)
        def _():
            for place in range(shards):
                owner = pos_ref[0] ^ bit_reverse(place, stages)
                low = (place * slab) % part_rows
                rows = part_refs[place * slab // part_rows][low : low + slab, :]
                wide_ref[pl.ds(pl.multiple_of(owner * slab, slab), slab), :] = rows.astype(F32)
            fast_ref[...] = wide_ref[...].astype(BF16)

        pieces = []
        for head in range(heads):
            low = head * 3 * size
            cols = slice(head * size, (head + 1) * size)
            query = unit_ref[:, cols]
            gate = dot(query, fast_ref[:, low : low + size])
            up = dot(query, fast_ref[:, low + size : low + 2 * size])
            hidden = (gate * jax.nn.sigmoid(gate) * up).astype(BF16)
            out = dot_nt(hidden, fast_ref[:, low + 2 * size : low + 3 * size])
            out = out * lax.rsqrt(jnp.mean(out * out, axis=-1, keepdims=True) + 1e-06)
            normed = (out * gain_ref[head : head + 1, :]).astype(BF16).astype(F32)
            pieces.append((normed + att_ref[:, cols]).astype(BF16))
        combined = jnp.concatenate(pieces, axis=1)
        mix_ref[...] = dot(combined, ow_ref[...]).astype(BF16)

    return pl.pallas_call(
        kernel,
        grid_spec=pltpu.PrefetchScalarGridSpec(
            num_scalar_prefetch=1,
            grid=(tok_dev // tile,),
            in_specs=[pl.BlockSpec((part_rows, 3 * width), lambda i, p: (0, 0))] * parts
            + [
                pl.BlockSpec((tile, width), lambda i, p: (i, 0)),
                pl.BlockSpec((tile, width), lambda i, p: (i, 0)),
                pl.BlockSpec((heads, size), lambda i, p: (0, 0)),
                pl.BlockSpec((width, width), lambda i, p: (0, 0)),
            ],
            out_specs=pl.BlockSpec((tile, width), lambda i, p: (i, 0)),
            scratch_shapes=[
                pltpu.VMEM((size, 3 * width), F32),
                pltpu.VMEM((size, 3 * width), BF16),
            ],
        ),
        out_shape=jax.ShapeDtypeStruct((tok_dev, width), BF16),
        compiler_params=params(),
        cost_estimate=cost(
            2 * tok_dev * width * (width + 3 * size),
            8 * tok_dev * width + 2 * width * width + 6 * size * width,
            tok_dev * width,
        ),
        name="apply_fast",
    )(position, *gathered, unit, attended, norm_gain, output_weight)


def body(
    activations,
    view_id,
    window_lengths,
    project_weight,
    rate_weight,
    fast_start,
    momentum,
    norm_gain,
    output_weight,
):
    tok_dev, width = activations.shape
    shards = lax.axis_size("tok")
    index = lax.axis_index("tok")
    position = index.reshape(1).astype(jnp.int32)
    heads = rate_weight.shape[1]
    size = width // heads
    slab = size // shards

    def swap(array, bit):
        return lax.ppermute(array, "tok", [(i, i ^ bit) for i in range(shards)])

    def flat(array):
        return jnp.swapaxes(array, 1, 2).reshape(array.shape[0], 3 * width)

    sent = group_by_view(view_id, activations, shards)
    arrived = lax.all_to_all(
        sent.reshape(shards, tok_dev // shards, width), "tok", split_axis=0, concat_axis=0, tiled=True
    ).reshape(tok_dev, width)

    fast_round = flat(fast_start.astype(BF16))
    own_start = flat(lax.dynamic_slice_in_dim(fast_start, index * slab, slab, 0))
    keep, send = fast_gradient(
        position, activations, project_weight, rate_weight, fast_round, shards
    )
    bit = 1
    while bit < shards:
        received = swap(send, bit)
        bit *= 2
        if bit < shards:
            keep, send = add_and_halve(keep, received)
    moment, share = update_rows(keep, received, flat(momentum), own_start, size)
    momentum_next = jnp.swapaxes(moment.reshape(slab, heads, 3, size), 1, 2)

    unit, attended = project_and_attend(
        jnp.cumsum(window_lengths[0]), arrived, project_weight, heads
    )

    bit = shards // 2
    block = share
    while bit > 1:
        block = jnp.concatenate([block, swap(block, bit)], axis=0)
        bit //= 2
    gathered = [block, swap(block, 1)]
    mixed = apply_fast(position, gathered, unit, attended, norm_gain, output_weight, shards)
    return (mixed[None], momentum_next)


def solution(mesh):
    in_specs = (
        P(("group", "tok"), None),
        P(("group", "tok")),
        P(("group", "tok"), None),
        P(),
        P(),
        P(),
        P(("group", "tok"), None, None, None),
        P(),
        P(),
    )
    out_specs = (P(("group", "tok"), None, None), P(("group", "tok"), None, None, None))
    return jax.shard_map(body, mesh=mesh, in_specs=in_specs, out_specs=out_specs, check_vma=False)
```

time: 415 us -> 138 us (0.33)
  waiting for transfers between devices: 198 us -> 40.8 us
  local copies, waits for them, and re-layouts: 89.9 us -> 14.8 us
  Pallas kernels: 0 us -> 64.3 us
  matrix products: 49.8 us -> 0 us
  other arithmetic: 48.4 us -> 2.58 us
  between operations: 14.3 us -> 0.76 us
    psum x1 -> x0, waiting for transfers between devices: 171 us -> none  [body(): total = lax.psum(jnp.stack([grad_gate, grad_up, grad_down], axis=1), 'tok')]
    pallas_call x0 -> x8, Pallas kernels: none -> 64.3 us  [the longest x1 20.8 us: project_and_attend(): pl.pallas_call(kernel, grid_spec=pltpu.PrefetchScalarGridSpec(num_scalar_...]
    dot_general x15 -> x0, matrix products: 49.8 us -> none  [the longest x1 11.3 us: body(): jnp.dot(activations, project_weight, preferred_element_type=f32)]
    ppermute x0 -> x8, waiting for transfers between devices: none -> 40.8 us  [swap(): return lax.ppermute(array, 'tok', [(i, i ^ bit) for i in range(shards)])]
    all_gather x1 -> x0, waiting for transfers between devices: 27.2 us -> none  [body(): fast_full = lax.all_gather(fast_share, 'tok', axis=0, tiled=True)]
    gather x2 -> x0, local copies, waits for them, and re-layouts: 21.1 us -> none  [the longest x1 15.8 us: body(): sent = projected[ordering].reshape(shards, per_view, 3 * model_width)]
    slice x6 -> x0, local copies, waits for them, and re-layouts: 14.4 us -> none  [the longest x2 8.63 us: window_attention(): arrived[:, 2 * model_width:].reshape(row_total, head_count, head_size)]
    reshape x4, local copies, waits for them, and re-layouts: 16.4 us -> 4.44 us  [the longest x3 3.37 us: flat(): return jnp.swapaxes(array, 1, 2).reshape(array.shape[0], 3 * width)]
  transfers between devices with their start and end apart: 4 -> 9, of which waited for: 2 -> 7; matrix products, arithmetic and copies ran while one was open for 34% -> 10% of each run, Pallas kernels for 0% -> 36%
where the time goes in v1:
time: 138 us; the launch traced here: 137 us
  Pallas kernels  64.3 us (47%)
  waiting for transfers between devices  40.8 us (30%)
  local copies, waits for them, and re-layouts  14.8 us (11%)
  starting transfers between devices  13.6 us (10%)
  other arithmetic  2.58 us (2%)
    ppermute x8, waiting for transfers between devices, swap(): return lax.ppermute(array, 'tok', [(i, i ^ bit) for i in range(shards)])  40.8 us
    pallas_call x1, Pallas kernels, project_and_attend(): pl.pallas_call(kernel, grid_spec=pltpu.PrefetchScalarGridSpec(num_scalar_...  20.8 us
    pallas_call x1, Pallas kernels, fast_gradient(): pl.pallas_call(kernel, grid_spec=pltpu.PrefetchScalarGridSpec(num_scalar_...  15.9 us
    pallas_call x3, Pallas kernels, add_and_halve(): pl.pallas_call(kernel, grid=(4,), in_specs=[pl.BlockSpec((rows, cols), la...  10.1 us
    pallas_call x1, Pallas kernels, apply_fast(): pl.pallas_call(kernel, grid_spec=pltpu.PrefetchScalarGridSpec(num_scalar_...  9.87 us
    unnamed x24, local copies, waits for them, and re-layouts  9.3 us
    all_to_all x1, starting transfers between devices, body(): lax.all_to_all(sent.reshape(shards, tok_dev // shards, width), 'tok', spl...  7.57 us
    ppermute x8, starting transfers between devices, swap(): return lax.ppermute(array, 'tok', [(i, i ^ bit) for i in range(shards)])  5.99 us
  transfers between devices with their start and end apart: 9, of which 7 were waited for; matrix products, arithmetic and copies ran while one was open for 10% of the time, Pallas kernels for 36%

profile of v1, /device:TPU:0, one launch (start us, length us, event | category | flops | bytes accessed | tf_op | source)
XLA Modules:
  0.0 136.8 jit_solution(12146511741137888142)
XLA Ops:
  0.6 5.6 %group_by_view.1 = bf16[1024,1024]{1,0:T(8,128)(2,1)} custom-call(s32[1,1024]{1,0:T(1,128)} %bitcast.18, bf16[1024,1024]{1,0:T(8,128)(2,1)} %act_ref.3), custom_call_target="tpu_custom_call" | custom-call | flops 2147483648 | bytes 4194304 | tf_op jit(solution)/shard_map/group_by_view/pallas_call | solution.py:74
  6.2 0.0 copy-start.6
  6.2 7.6 %all-to-all-start = ((bf16[16,64,1024]{2,1,0:T(8,128)(2,1)}), bf16[16,64,1024]{2,1,0:T(8,128)(2,1)}, u32[]{:S(2)}, u32[]{:S(2)}) async-start(bf16[16,64,1024]{2,1,0:T(8,128)(2,1)} %bitcast.15), calls=%async_computation | async-start | bytes 4194304 | tf_op jit(solution)/shard_map/all_to_all | solution.py:392
  13.8 0.0 copy-done.6
  13.8 0.9 copy.17.rate_w_ref
  14.7 2.9 %copy.16 = bf16[256,3,4,256]{0,3,1,2:T(8,128)(2,1)S(1)} copy(f32[256,3,4,256]{3,2,1,0:T(4,128)} %param.14) | data formatting | bytes 4718592 | tf_op args[5]
  17.6 1.8 %copy.18.fast_ref = bf16[256,3072]{1,0:T(8,128)(2,1)} copy(bf16[256,3072]{0,1:T(8,128)(2,1)S(1)} %bitcast.14) | data formatting | bytes 3145728 | tf_op jit(solution)/shard_map/reshape | solution.py:389
  19.4 15.9 %fast_gradient.1 = (f32[128,3072]{1,0:T(8,128)}, bf16[128,3072]{1,0:T(8,128)(2,1)}) custom-call(s32[1]{0:T(128)} %bitcast.pos_ref, bf16[1024,1024]{1,0:T(8,128)(2,1)} %act_ref.3, bf16[1024,3072]{1,0:T(8,128)(2,1)} %wv_ref.3, bf16[1024,3072]{1,0:T(8,128)(2,1)} %wv_ref.3, bf16[1024,4]{1,0:T(8,128)(2,1)} %copy.17.rate_w_ref, bf16[256,3072]{1,0:T(8,128)(2,1)} %copy.18.fast_ref), custom_call_target="tpu_custom_call" | custom-call | flops 7516192768 | bytes 10223616 | tf_op jit(solution)/shard_map/fast_gradient/pallas_call | solution.py:148
  35.3 0.3 collective-permute-start
  35.6 2.1 %collective-permute-done.got_ref = bf16[128,3072]{1,0:T(8,128)(2,1)S(1)} collective-permute-done((bf16[128,3072]{1,0:T(8,128)(2,1)}, bf16[128,3072]{1,0:T(8,128)(2,1)S(1)}, u32[]{:S(2)}, u32[]{:S(2)}) %collective-permute-start) | collective-permute-done | bytes 786464 | tf_op jit(solution)/shard_map/ppermute | solution.py:386
  37.8 0.0 copy-start
  37.8 0.9 copy-done
  38.7 3.7 %add_and_halve.3 = (f32[64,3072]{1,0:T(8,128)}, bf16[64,3072]{1,0:T(8,128)(2,1)}) custom-call(f32[128,3072]{1,0:T(8,128)} %get-tuple-element.14.keep_ref, bf16[128,3072]{1,0:T(8,128)(2,1)} %copy-done), custom_call_target="tpu_custom_call" | custom-call | flops 393216 | bytes 3538944 | tf_op jit(solution)/shard_map/add_and_halve/pallas_call | solution.py:197
  42.4 0.0 copy-start.2
  42.4 1.9 %collective-permute-start.1 = (bf16[64,3072]{1,0:T(8,128)(2,1)}, bf16[64,3072]{1,0:T(8,128)(2,1)S(1)}, u32[]{:S(2)}, u32[]{:S(2)}) collective-permute-start(bf16[64,3072]{1,0:T(8,128)(2,1)} %get-tuple-element.17), channel_id=1, source_target_pairs={{0,2},{1,3},{2,0},{3,1},{4,6},{5,7},{6,4},{7,5},{8,10},{9,11},{10,... | collective-permute-start | bytes 1179656 | tf_op jit(solution)/shard_map/ppermute | solution.py:386
  44.2 15.3 %collective-permute-done.1.got_ref = bf16[64,3072]{1,0:T(8,128)(2,1)S(1)} collective-permute-done((bf16[64,3072]{1,0:T(8,128)(2,1)}, bf16[64,3072]{1,0:T(8,128)(2,1)S(1)}, u32[]{:S(2)}, u32[]{:S(2)}) %collective-permute-start.1) | collective-permute-done | bytes 393248 | tf_op jit(solution)/shard_map/ppermute | solution.py:386
  59.6 0.0 copy-start.1
  59.6 0.7 copy-done.1
  60.3 0.0 copy-start.8
  60.3 3.4 %add_and_halve.4 = (f32[32,3072]{1,0:T(8,128)}, bf16[32,3072]{1,0:T(8,128)(2,1)}) custom-call(f32[64,3072]{1,0:T(8,128)} %get-tuple-element.16.keep_ref, bf16[64,3072]{1,0:T(8,128)(2,1)} %copy-done.1), custom_call_target="tpu_custom_call" | custom-call | flops 196608 | bytes 1769472 | tf_op jit(solution)/shard_map/add_and_halve/pallas_call | solution.py:197
  63.7 1.6 %collective-permute-start.2 = (bf16[32,3072]{1,0:T(8,128)(2,1)}, bf16[32,3072]{1,0:T(8,128)(2,1)S(1)}, u32[]{:S(2)}, u32[]{:S(2)}) collective-permute-start(bf16[32,3072]{1,0:T(8,128)(2,1)} %get-tuple-element.19), channel_id=1, source_target_pairs={{0,4},{1,5},{2,6},{3,7},{4,0},{5,1},{6,2},{7,3},{8,12},{9,13},{10,... | collective-permute-start | bytes 589832 | tf_op jit(solution)/shard_map/ppermute | solution.py:386
  65.3 5.0 %collective-permute-done.2.got_ref = bf16[32,3072]{1,0:T(8,128)(2,1)S(1)} collective-permute-done((bf16[32,3072]{1,0:T(8,128)(2,1)}, bf16[32,3072]{1,0:T(8,128)(2,1)S(1)}, u32[]{:S(2)}, u32[]{:S(2)}) %collective-permute-start.2) | collective-permute-done | bytes 196640 | tf_op jit(solution)/shard_map/ppermute | solution.py:386
  70.2 0.0 copy-start.3
  70.2 0.7 copy-done.3
  70.9 3.1 %add_and_halve.5 = (f32[16,3072]{1,0:T(8,128)}, bf16[16,3072]{1,0:T(8,128)(2,1)}) custom-call(f32[32,3072]{1,0:T(8,128)} %get-tuple-element.18.keep_ref, bf16[32,3072]{1,0:T(8,128)(2,1)} %copy-done.3), custom_call_target="tpu_custom_call" | custom-call | flops 98304 | bytes 884736 | tf_op jit(solution)/shard_map/add_and_halve/pallas_call | solution.py:197
  74.0 1.4 %collective-permute-start.3 = (bf16[16,3072]{1,0:T(8,128)(2,1)}, bf16[16,3072]{1,0:T(8,128)(2,1)S(1)}, u32[]{:S(2)}, u32[]{:S(2)}) collective-permute-start(bf16[16,3072]{1,0:T(8,128)(2,1)} %get-tuple-element.21), channel_id=1, source_target_pairs={{0,8},{1,9},{2,10},{3,11},{4,12},{5,13},{6,14},{7,15},{8,0},{9,1},... | collective-permute-start | bytes 294920 | tf_op jit(solution)/shard_map/ppermute | solution.py:386
  75.4 0.9 dynamic-slice_bitcast_fusion
  76.4 0.1 copy.20
  76.4 0.8 reshape.58.start_ref
  77.2 0.0 copy-done.2
  77.2 0.1 copy.19
  77.3 0.8 reshape.57.mom_ref
  78.1 2.6 %collective-permute-done.3.got_ref = bf16[16,3072]{1,0:T(8,128)(2,1)S(1)} collective-permute-done((bf16[16,3072]{1,0:T(8,128)(2,1)}, bf16[16,3072]{1,0:T(8,128)(2,1)S(1)}, u32[]{:S(2)}, u32[]{:S(2)}) %collective-permute-start.3) | collective-permute-done | bytes 98336 | tf_op jit(solution)/shard_map/ppermute | solution.py:386
  80.8 0.0 copy-start.4
  80.8 0.6 copy-done.4
  81.4 2.0 %update_rows.1 = (f32[16,3072]{1,0:T(8,128)}, bf16[16,3072]{1,0:T(8,128)(2,1)}) custom-call(f32[16,3072]{1,0:T(8,128)} %get-tuple-element.20.keep_ref, bf16[16,3072]{1,0:T(8,128)(2,1)} %copy-done.4, f32[16,3072]{1,0:T(8,128)} %reshape.57.mom_ref, f32[16,3072]{1,0:T(8,128)} %reshape.58.start_ref), custom_call_target="tpu_custom_call" | custom-call | flops 393216 | bytes 983040 | tf_op jit(solution)/shard_map/update_rows/pallas_call | solution.py:227
  83.4 0.4 collective-permute-start.4
  83.8 0.0 copy-done.8
  83.8 0.8 reduce-window.9
  84.5 1.1 reshape.64
  85.6 0.7 copy.21
  86.3 3.3 %collective-permute-done.4 = bf16[16,3072]{1,0:T(8,128)(2,1)S(1)} collective-permute-done((bf16[16,3072]{1,0:T(8,128)(2,1)}, bf16[16,3072]{1,0:T(8,128)(2,1)S(1)}, u32[]{:S(2)}, u32[]{:S(2)}) %collective-permute-start.4) | collective-permute-done | bytes 98336 | tf_op jit(solution)/shard_map/ppermute | solution.py:386
  89.7 0.9 pad_maximum_fusion.1
  90.6 0.1 collective-permute-start.5
  90.7 0.9 constant_dynamic-update-slice_fusion.3
  91.6 4.8 %collective-permute-done.5 = bf16[32,3072]{1,0:T(8,128)(2,1)S(1)} collective-permute-done((bf16[32,3072]{1,0:T(8,128)(2,1)S(1)}, bf16[32,3072]{1,0:T(8,128)(2,1)S(1)}, u32[]{:S(2)}, u32[]{:S(2)}) %collective-permute-start.5) | collective-permute-done | bytes 196640 | tf_op jit(solution)/shard_map/ppermute | solution.py:386
  96.3 0.9 pad_maximum_fusion
  97.2 0.2 collective-permute-start.6
  97.5 7.6 %collective-permute-done.6 = bf16[64,3072]{1,0:T(8,128)(2,1)S(1)} collective-permute-done((bf16[64,3072]{1,0:T(8,128)(2,1)S(1)}, bf16[64,3072]{1,0:T(8,128)(2,1)S(1)}, u32[]{:S(2)}, u32[]{:S(2)}) %collective-permute-start.6) | collective-permute-done | bytes 393248 | tf_op jit(solution)/shard_map/ppermute | solution.py:386
  105.1 0.0 copy-start.5
  105.1 0.1 collective-permute-start.7
  105.2 0.0 all-to-all-done
  105.2 20.8 %project_and_attend.1 = (bf16[1024,1024]{1,0:T(8,128)(2,1)}, f32[1024,1024]{1,0:T(8,128)}) custom-call(s32[3]{0:T(128)} %bitcast.21, bf16[1024,1024]{1,0:T(8,128)(2,1)} %bitcast.9.x_ref, bf16[1024,3072]{1,0:T(8,128)(2,1)} %wv_ref.3, bf16[1024,3072]{1,0:T(8,128)(2,1)} %wv_ref.3, bf16[1024,3072]{1,0:T(8,128)(2,1)} %wv_ref.3), custom_call_target="tpu_custom_call" | custom-call | flops 10737418240 | bytes 14680064 | tf_op jit(solution)/shard_map/project_and_attend/pallas_call | solution.py:270
  126.0 0.0 copy-done.5
  126.0 0.0 collective-permute-done.7.refs_1_
  126.1 0.0 copy-start.7
  126.1 0.9 copy-done.7
  126.9 9.9 %apply_fast.1 = bf16[1024,1024]{1,0:T(8,128)(2,1)} custom-call(s32[1]{0:T(128)} %bitcast.pos_ref, bf16[128,3072]{1,0:T(8,128)(2,1)} %copy-done.5, bf16[128,3072]{1,0:T(8,128)(2,1)} %copy-done.7, bf16[1024,1024]{1,0:T(8,128)(2,1)} %get-tuple-element.23.refs_2_, f32[1024,1024]{1,0:T(8,128)} %get-tuple-element.24.refs_3_, f32[4,256]{1,0:T(4,128)} %refs_4_.1, ...), custom_call_target="tpu_custom_call" | custom-call | flops 3758096384 | bytes 12058624 | tf_op jit(solution)/shard_map/apply_fast/pallas_call | solution.py:337
  (3 shorter events, 0.0 us)
Async XLA Ops:
  6.2 7.6 %copy-start.6 = (bf16[1024,4]{0,1:T(4,128)(2,1)S(1)}, bf16[1024,4]{0,1:T(4,128)(2,1)}, u32[]{:S(2)}) copy-start(bf16[1024,4]{0,1:T(4,128)(2,1)} %param.13) | copy-start | bytes 24580
  6.2 99.0 %all-to-all-start = ((bf16[16,64,1024]{2,1,0:T(8,128)(2,1)}), bf16[16,64,1024]{2,1,0:T(8,128)(2,1)}, u32[]{:S(2)}, u32[]{:S(2)}) async-start(bf16[16,64,1024]{2,1,0:T(8,128)(2,1)} %bitcast.15), calls=%async_computation | async-start | bytes 4194304 | tf_op jit(solution)/shard_map/all_to_all | solution.py:392
  35.3 2.5 %collective-permute-start = (bf16[128,3072]{1,0:T(8,128)(2,1)}, bf16[128,3072]{1,0:T(8,128)(2,1)S(1)}, u32[]{:S(2)}, u32[]{:S(2)}) collective-permute-start(bf16[128,3072]{1,0:T(8,128)(2,1)} %get-tuple-element.15), channel_id=1, source_target_pairs={{0,1},{1,0},{2,3},{3,2},{4,5},{5,4},{6,7},{7,6},{8,9},{9,8},{10,11... | collective-permute-start | bytes 2359304 | tf_op jit(solution)/shard_map/ppermute | solution.py:386
  37.8 0.9 copy-start
  42.4 34.9 %copy-start.2 = (f32[16,3,4,256]{3,2,1,0:T(4,128)S(1)}, f32[16,3,4,256]{3,2,1,0:T(4,128)}, u32[]{:S(2)}) copy-start(f32[16,3,4,256]{3,2,1,0:T(4,128)} %param.15) | copy-start | bytes 589828
  42.4 17.2 %collective-permute-start.1 = (bf16[64,3072]{1,0:T(8,128)(2,1)}, bf16[64,3072]{1,0:T(8,128)(2,1)S(1)}, u32[]{:S(2)}, u32[]{:S(2)}) collective-permute-start(bf16[64,3072]{1,0:T(8,128)(2,1)} %get-tuple-element.17), channel_id=1, source_target_pairs={{0,2},{1,3},{2,0},{3,1},{4,6},{5,7},{6,4},{7,5},{8,10},{9,11},{10,... | collective-permute-start | bytes 1179656 | tf_op jit(solution)/shard_map/ppermute | solution.py:386
  59.6 0.8 copy-start.1
  60.3 23.5 %copy-start.8 = (s32[1,3]{1,0:T(1,128)S(1)}, s32[1,3]{1,0:T(1,128)}, u32[]{:S(2)}) copy-start(s32[1,3]{1,0:T(1,128)} %param.11) | copy-start | bytes 40
  63.7 6.6 %collective-permute-start.2 = (bf16[32,3072]{1,0:T(8,128)(2,1)}, bf16[32,3072]{1,0:T(8,128)(2,1)S(1)}, u32[]{:S(2)}, u32[]{:S(2)}) collective-permute-start(bf16[32,3072]{1,0:T(8,128)(2,1)} %get-tuple-element.19), channel_id=1, source_target_pairs={{0,4},{1,5},{2,6},{3,7},{4,0},{5,1},{6,2},{7,3},{8,12},{9,13},{10,... | collective-permute-start | bytes 589832 | tf_op jit(solution)/shard_map/ppermute | solution.py:386
  70.2 0.7 copy-start.3
  74.0 6.8 %collective-permute-start.3 = (bf16[16,3072]{1,0:T(8,128)(2,1)}, bf16[16,3072]{1,0:T(8,128)(2,1)S(1)}, u32[]{:S(2)}, u32[]{:S(2)}) collective-permute-start(bf16[16,3072]{1,0:T(8,128)(2,1)} %get-tuple-element.21), channel_id=1, source_target_pairs={{0,8},{1,9},{2,10},{3,11},{4,12},{5,13},{6,14},{7,15},{8,0},{9,1},... | collective-permute-start | bytes 294920 | tf_op jit(solution)/shard_map/ppermute | solution.py:386
  80.8 0.6 copy-start.4
  83.4 6.3 %collective-permute-start.4 = (bf16[16,3072]{1,0:T(8,128)(2,1)}, bf16[16,3072]{1,0:T(8,128)(2,1)S(1)}, u32[]{:S(2)}, u32[]{:S(2)}) collective-permute-start(bf16[16,3072]{1,0:T(8,128)(2,1)} %get-tuple-element.22), channel_id=1, source_target_pairs={{0,8},{1,9},{2,10},{3,11},{4,12},{5,13},{6,14},{7,15},{8,0},{9,1},... | collective-permute-start | bytes 294920 | tf_op jit(solution)/shard_map/ppermute | solution.py:386
  90.6 5.7 %collective-permute-start.5 = (bf16[32,3072]{1,0:T(8,128)(2,1)S(1)}, bf16[32,3072]{1,0:T(8,128)(2,1)S(1)}, u32[]{:S(2)}, u32[]{:S(2)}) collective-permute-start(bf16[32,3072]{1,0:T(8,128)(2,1)S(1)} %pad_maximum_fusion.1), channel_id=1, source_target_pairs={{0,4},{1,5},{2,6},{3,7},{4,0},{5,1},{6,2},{7,3},{8,12},{9,13},{10,... | collective-permute-start | bytes 589832 | tf_op jit(solution)/shard_map/ppermute | solution.py:386
  97.2 7.8 %collective-permute-start.6 = (bf16[64,3072]{1,0:T(8,128)(2,1)S(1)}, bf16[64,3072]{1,0:T(8,128)(2,1)S(1)}, u32[]{:S(2)}, u32[]{:S(2)}) collective-permute-start(bf16[64,3072]{1,0:T(8,128)(2,1)S(1)} %pad_maximum_fusion), channel_id=1, source_target_pairs={{0,2},{1,3},{2,0},{3,1},{4,6},{5,7},{6,4},{7,5},{8,10},{9,11},{10,... | collective-permute-start | bytes 1179656 | tf_op jit(solution)/shard_map/ppermute | solution.py:386
  105.1 20.9 %copy-start.5 = (bf16[128,3072]{1,0:T(8,128)(2,1)}, bf16[128,3072]{1,0:T(8,128)(2,1)S(1)}, u32[]{:S(2)}) copy-start(bf16[128,3072]{1,0:T(8,128)(2,1)S(1)} %constant_dynamic-update-slice_fusion.refs_0_) | copy-start | bytes 2359300
  105.1 20.9 %collective-permute-start.7 = (bf16[128,3072]{1,0:T(8,128)(2,1)S(1)}, bf16[128,3072]{1,0:T(8,128)(2,1)S(1)}, u32[]{:S(2)}, u32[]{:S(2)}) collective-permute-start(bf16[128,3072]{1,0:T(8,128)(2,1)S(1)} %constant_dynamic-update-slice_fusion.refs_0_), channel_id=1, source_target_pairs={{0,1},{1,0},{2,3},{3,2},{4,5},{5,4},{6,7},{7,6},{8,9},{9,8},{10,11... | collective-permute-start | bytes 2359304 | tf_op jit(solution)/shard_map/ppermute | solution.py:386
  126.1 0.9 copy-start.7

commit v2 on v1

--- a/solution.py
+++ b/solution.py
@@ -9,7 +9,7 @@
 
 F32 = jnp.float32
 BF16 = jnp.bfloat16
-VMEM_LIMIT = 60 * 1024 * 1024
+MIB = 1024 * 1024
 
 
 def dot(a, b):
@@ -31,10 +31,14 @@
     return out
 
 
-def params(grid_rank=1):
+def params(mebibytes):
     return pltpu.CompilerParams(
-        dimension_semantics=("arbitrary",) * grid_rank, vmem_limit_bytes=VMEM_LIMIT
+        dimension_semantics=("arbitrary",), vmem_limit_bytes=mebibytes * MIB
     )
+
+
+def after(array, *others):
+    return lax.optimization_barrier((array, *others))[0]
 
 
 def cost(flops, nbytes, transcendentals=0):
@@ -81,15 +85,16 @@
         out_specs=pl.BlockSpec((tile, width), lambda i: (i, 0)),
         out_shape=jax.ShapeDtypeStruct((tok_dev, width), BF16),
         scratch_shapes=[pltpu.VMEM((1, tok_dev), jnp.int32)],
-        compiler_params=params(),
+        compiler_params=params(60),
         cost_estimate=cost(2 * tok_dev * tok_dev * width, 4 * tok_dev * width),
         name="group_by_view",
     )(view_id.reshape(1, tok_dev), activations)
 
 
-def fast_gradient(position, activations, project_weight, rate_weight, fast_round, shards):
+def fast_gradient(position, activations, project_weight, rate_weight, fast_start, shards):
     tok_dev, width = activations.shape
     heads = rate_weight.shape[1]
+    kinds = fast_start.shape[1]
     size = width // heads
     slab = size // shards
     stages = shards.bit_length() - 1
@@ -98,17 +103,33 @@
     half = size // 2
 
     def kernel(pos_ref, act_ref, wk_ref, wv_ref, rate_w_ref, fast_ref, keep_ref, send_ref,
-               rate_ref, key_ref, out_ref, hid_ref, gate_ref, grad_ref):
+               rate_ref, key_ref, out_ref, hid_ref, gate_ref, grad_ref, start_ref, sems):
         head = pl.program_id(0)
+        slot = head % 2
+
+        def fetch(which, place):
+            return [
+                pltpu.make_async_copy(
+                    fast_ref.at[:, kind, which, :], start_ref.at[place, kind], sems.at[place, kind]
+                )
+                for kind in range(kinds)
+            ]
 
         @pl.when(head == 0)
         def _():
-            raw = dot(act_ref[...], rate_w_ref[...])
+            for copy in fetch(0, 0):
+                copy.start()
+            raw = dot_nt(act_ref[...], rate_w_ref[...])
             rate_ref[...] = (jnp.maximum(raw, 0.0) + jnp.log1p(jnp.exp(-jnp.abs(raw)))) * scale
 
-        w_gate = fast_ref[:, 0:size]
-        w_up = fast_ref[:, size : 2 * size]
-        w_down = fast_ref[:, 2 * size : 3 * size]
+        @pl.when(head + 1 < heads)
+        def _():
+            for copy in fetch(head + 1, 1 - slot):
+                copy.start()
+
+        for copy in fetch(head, slot):
+            copy.wait()
+        w_gate, w_up, w_down = [start_ref[slot, kind].astype(BF16) for kind in range(kinds)]
         for start in range(0, tok_dev, tile):
             rows = slice(start, start + tile)
             act = act_ref[rows, :]
@@ -154,8 +175,8 @@
                 pl.BlockSpec((tok_dev, width), lambda h, p: (0, 0)),
                 pl.BlockSpec((width, size), lambda h, p: (0, heads + h)),
                 pl.BlockSpec((width, size), lambda h, p: (0, 2 * heads + h)),
-                pl.BlockSpec((width, heads), lambda h, p: (0, 0)),
-                pl.BlockSpec((size, 3 * size), lambda h, p: (0, h)),
+                pl.BlockSpec((heads, width), lambda h, p: (0, 0)),
+                pl.BlockSpec(memory_space=pl.ANY),
             ],
             out_specs=[
                 pl.BlockSpec((half, 3 * size), lambda h, p: (0, h)),
@@ -168,74 +189,102 @@
                 pltpu.VMEM((tok_dev, size), BF16),
                 pltpu.VMEM((tok_dev, 2 * size), BF16),
                 pltpu.VMEM((size, 3 * size), F32),
+                pltpu.VMEM((2, kinds, size, size), F32),
+                pltpu.SemaphoreType.DMA((2, kinds)),
             ],
         ),
         out_shape=[
             jax.ShapeDtypeStruct((half, 3 * width), F32),
             jax.ShapeDtypeStruct((half, 3 * width), BF16),
         ],
-        compiler_params=params(),
+        compiler_params=params(60),
         cost_estimate=cost(
             2 * tok_dev * width * (2 * width + 6 * size),
             2 * tok_dev * width + 4 * width * width + 6 * size * width + 9 * size * width,
             4 * tok_dev * width,
         ),
         name="fast_gradient",
-    )(position, activations, project_weight, project_weight, rate_weight, fast_round)
+    )(position, activations, project_weight, project_weight, rate_weight.T, fast_start)
 
 
 def add_and_halve(keep, received):
     rows, width = keep.shape
     half = rows // 2
-    cols = width // 4
 
     def kernel(keep_ref, got_ref, stay_ref, go_ref):
-        total = keep_ref[...] + got_ref[...].astype(F32)
-        stay_ref[...] = total[:half]
-        go_ref[...] = total[half:].astype(BF16)
-
-    return pl.pallas_call(
-        kernel,
-        grid=(4,),
-        in_specs=[pl.BlockSpec((rows, cols), lambda i: (0, i))] * 2,
-        out_specs=[pl.BlockSpec((half, cols), lambda i: (0, i))] * 2,
+        stay_ref[...] = keep_ref[:half, :] + got_ref[:half, :].astype(F32)
+        go_ref[...] = (keep_ref[half:, :] + got_ref[half:, :].astype(F32)).astype(BF16)
+
+    whole = pl.BlockSpec(memory_space=pltpu.VMEM)
+    return pl.pallas_call(
+        kernel,
+        in_specs=[whole, whole],
+        out_specs=[whole, whole],
         out_shape=[
             jax.ShapeDtypeStruct((half, width), F32),
             jax.ShapeDtypeStruct((half, width), BF16),
         ],
-        compiler_params=params(),
+        compiler_params=pltpu.CompilerParams(vmem_limit_bytes=6 * MIB),
         cost_estimate=cost(rows * width, 9 * rows * width),
         name="add_and_halve",
     )(keep, received)
 
 
-def update_rows(keep, received, momentum, own_start, size):
-    rows, width = keep.shape
+def join(first, second):
+    rows, width = first.shape
+
+    def kernel(first_ref, second_ref, out_ref):
+        out_ref[:rows, :] = first_ref[...]
+        out_ref[rows:, :] = second_ref[...]
+
+    whole = pl.BlockSpec(memory_space=pltpu.VMEM)
+    return pl.pallas_call(
+        kernel,
+        in_specs=[whole, whole],
+        out_specs=whole,
+        out_shape=jax.ShapeDtypeStruct((2 * rows, width), BF16),
+        compiler_params=pltpu.CompilerParams(vmem_limit_bytes=4 * MIB),
+        cost_estimate=cost(0, 8 * rows * width),
+        name="join",
+    )(first, second)
+
+
+def update_rows(keep, received, momentum, own_start):
+    rows, kinds, heads, size = momentum.shape
+    width = keep.shape[1]
 
     def kernel(keep_ref, got_ref, mom_ref, start_ref, next_ref, share_ref):
-        for low in range(0, width, size):
-            cols = slice(low, low + size)
-            moment = 0.9 * mom_ref[:, cols] + (keep_ref[:, cols] + got_ref[:, cols].astype(F32))
-            next_ref[:, cols] = moment
-            start = start_ref[:, cols]
-            moved = start - moment
-            factor = jnp.sqrt(jnp.sum(start * start, axis=-1, keepdims=True)) / jnp.sqrt(
-                jnp.sum(moved * moved, axis=-1, keepdims=True) + 1e-06
-            )
-            share_ref[:, cols] = (moved * factor).astype(BF16)
-
-    return pl.pallas_call(
-        kernel,
+        for head in range(heads):
+            for kind in range(kinds):
+                low = (head * kinds + kind) * size
+                cols = slice(low, low + size)
+                moment = 0.9 * mom_ref[:, kind, head, :] + (
+                    keep_ref[:, cols] + got_ref[:, cols].astype(F32)
+                )
+                next_ref[:, kind, head, :] = moment
+                start = start_ref[:, kind, head, :]
+                moved = start - moment
+                factor = jnp.sqrt(jnp.sum(start * start, axis=-1, keepdims=True)) / jnp.sqrt(
+                    jnp.sum(moved * moved, axis=-1, keepdims=True) + 1e-06
+                )
+                share_ref[:, cols] = (moved * factor).astype(BF16)
+
+    whole = pl.BlockSpec(memory_space=pltpu.VMEM)
+    return pl.pallas_call(
+        kernel,
+        in_specs=[whole] * 4,
+        out_specs=[whole, whole],
         out_shape=[
-            jax.ShapeDtypeStruct((rows, width), F32),
+            jax.ShapeDtypeStruct(momentum.shape, F32),
             jax.ShapeDtypeStruct((rows, width), BF16),
         ],
+        compiler_params=pltpu.CompilerParams(vmem_limit_bytes=4 * MIB),
         cost_estimate=cost(8 * rows * width, 20 * rows * width),
         name="update_rows",
     )(keep, received, momentum, own_start)
 
 
-def project_and_attend(window_ends, arrived, project_weight, heads):
+def project_and_attend(window_ends, arrived, project_weight, heads, first, count):
     tok_dev, width = arrived.shape
     size = width // heads
     windows = window_ends.shape[0]
@@ -271,12 +320,12 @@
         kernel,
         grid_spec=pltpu.PrefetchScalarGridSpec(
             num_scalar_prefetch=1,
-            grid=(heads,),
+            grid=(count,),
             in_specs=[
                 pl.BlockSpec((tok_dev, width), lambda h, e: (0, 0)),
-                pl.BlockSpec((width, size), lambda h, e: (0, h)),
-                pl.BlockSpec((width, size), lambda h, e: (0, heads + h)),
-                pl.BlockSpec((width, size), lambda h, e: (0, 2 * heads + h)),
+                pl.BlockSpec((width, size), lambda h, e: (0, first + h)),
+                pl.BlockSpec((width, size), lambda h, e: (0, heads + first + h)),
+                pl.BlockSpec((width, size), lambda h, e: (0, 2 * heads + first + h)),
             ],
             out_specs=[
                 pl.BlockSpec((tok_dev, size), lambda h, e: (0, h)),
@@ -284,31 +333,38 @@
             ],
         ),
         out_shape=[
-            jax.ShapeDtypeStruct((tok_dev, width), BF16),
-            jax.ShapeDtypeStruct((tok_dev, width), F32),
+            jax.ShapeDtypeStruct((tok_dev, count * size), BF16),
+            jax.ShapeDtypeStruct((tok_dev, count * size), F32),
         ],
-        compiler_params=params(),
+        compiler_params=params(50),
         cost_estimate=cost(
-            2 * tok_dev * width * (3 * width + 2 * tok_dev),
-            8 * tok_dev * width + 6 * width * width,
-            heads * tok_dev * tok_dev,
+            2 * tok_dev * count * size * (3 * width + 2 * tok_dev),
+            2 * tok_dev * width + 6 * tok_dev * count * size + 6 * width * count * size,
+            count * tok_dev * tok_dev,
         ),
         name="project_and_attend",
     )(window_ends, arrived, project_weight, project_weight, project_weight)
 
 
-def apply_fast(position, gathered, unit, attended, norm_gain, output_weight, shards):
-    tok_dev, width = unit.shape
+def apply_fast(position, gathered, units, attends, norm_gain, output_weight, shards):
+    tok_dev = units[0].shape[0]
+    width = output_weight.shape[0]
     heads, size = norm_gain.shape
     slab = size // shards
     stages = shards.bit_length() - 1
     tile = 256
     parts = len(gathered)
     part_rows = size // parts
+    pieces_of = len(units)
+    where = []
+    for piece, unit in enumerate(units):
+        where += [(piece, low) for low in range(0, unit.shape[1], size)]
 
     def kernel(pos_ref, *refs):
         part_refs = refs[:parts]
-        unit_ref, att_ref, gain_ref, ow_ref, mix_ref, wide_ref, fast_ref = refs[parts:]
+        unit_refs = refs[parts : parts + pieces_of]
+        att_refs = refs[parts + pieces_of : parts + 2 * pieces_of]
+        gain_ref, ow_ref, mix_ref, wide_ref, fast_ref = refs[parts + 2 * pieces_of :]
 
         @pl.when(pl.program_id(0) == 0)
         def _():
@@ -322,15 +378,16 @@
         pieces = []
         for head in range(heads):
             low = head * 3 * size
-            cols = slice(head * size, (head + 1) * size)
-            query = unit_ref[:, cols]
+            piece, col = where[head]
+            cols = slice(col, col + size)
+            query = unit_refs[piece][:, cols]
             gate = dot(query, fast_ref[:, low : low + size])
             up = dot(query, fast_ref[:, low + size : low + 2 * size])
             hidden = (gate * jax.nn.sigmoid(gate) * up).astype(BF16)
             out = dot_nt(hidden, fast_ref[:, low + 2 * size : low + 3 * size])
             out = out * lax.rsqrt(jnp.mean(out * out, axis=-1, keepdims=True) + 1e-06)
             normed = (out * gain_ref[head : head + 1, :]).astype(BF16).astype(F32)
-            pieces.append((normed + att_ref[:, cols]).astype(BF16))
+            pieces.append((normed + att_refs[piece][:, cols]).astype(BF16))
         combined = jnp.concatenate(pieces, axis=1)
         mix_ref[...] = dot(combined, ow_ref[...]).astype(BF16)
 
@@ -340,9 +397,8 @@
             num_scalar_prefetch=1,
             grid=(tok_dev // tile,),
             in_specs=[pl.BlockSpec((part_rows, 3 * width), lambda i, p: (0, 0))] * parts
+            + [pl.BlockSpec((tile, unit.shape[1]), lambda i, p: (i, 0)) for unit in units] * 2
             + [
-                pl.BlockSpec((tile, width), lambda i, p: (i, 0)),
-                pl.BlockSpec((tile, width), lambda i, p: (i, 0)),
                 pl.BlockSpec((heads, size), lambda i, p: (0, 0)),
                 pl.BlockSpec((width, width), lambda i, p: (0, 0)),
             ],
@@ -353,14 +409,14 @@
             ],
         ),
         out_shape=jax.ShapeDtypeStruct((tok_dev, width), BF16),
-        compiler_params=params(),
+        compiler_params=params(20),
         cost_estimate=cost(
             2 * tok_dev * width * (width + 3 * size),
             8 * tok_dev * width + 2 * width * width + 6 * size * width,
             tok_dev * width,
         ),
         name="apply_fast",
-    )(position, *gathered, unit, attended, norm_gain, output_weight)
+    )(position, *gathered, *units, *attends, norm_gain, output_weight)
 
 
 def body(
@@ -385,18 +441,15 @@
     def swap(array, bit):
         return lax.ppermute(array, "tok", [(i, i ^ bit) for i in range(shards)])
 
-    def flat(array):
-        return jnp.swapaxes(array, 1, 2).reshape(array.shape[0], 3 * width)
-
     sent = group_by_view(view_id, activations, shards)
     arrived = lax.all_to_all(
         sent.reshape(shards, tok_dev // shards, width), "tok", split_axis=0, concat_axis=0, tiled=True
     ).reshape(tok_dev, width)
-
-    fast_round = flat(fast_start.astype(BF16))
-    own_start = flat(lax.dynamic_slice_in_dim(fast_start, index * slab, slab, 0))
+    ends = jnp.cumsum(window_lengths[0])
+    own_start = lax.dynamic_slice_in_dim(fast_start, index * slab, slab, 0)
+
     keep, send = fast_gradient(
-        position, activations, project_weight, rate_weight, fast_round, shards
+        position, after(activations, sent), project_weight, rate_weight, fast_start, shards
     )
     bit = 1
     while bit < shards:
@@ -404,20 +457,28 @@
         bit *= 2
         if bit < shards:
             keep, send = add_and_halve(keep, received)
-    moment, share = update_rows(keep, received, flat(momentum), own_start, size)
-    momentum_next = jnp.swapaxes(moment.reshape(slab, heads, 3, size), 1, 2)
-
-    unit, attended = project_and_attend(
-        jnp.cumsum(window_lengths[0]), arrived, project_weight, heads
-    )
-
+    momentum_next, block = update_rows(keep, received, momentum, own_start)
+
+    stages = shards.bit_length() - 1
+    units, attends = [], []
     bit = shards // 2
-    block = share
-    while bit > 1:
-        block = jnp.concatenate([block, swap(block, bit)], axis=0)
-        bit //= 2
-    gathered = [block, swap(block, 1)]
-    mixed = apply_fast(position, gathered, unit, attended, norm_gain, output_weight, shards)
+    done = 0
+    for stage in range(stages - 1):
+        last = stage == stages - 2
+        count = heads - done if last else min(1, heads - done)
+        if count:
+            unit, attended = project_and_attend(
+                ends, after(arrived, block), project_weight, heads, done, count
+            )
+            units.append(unit)
+            attends.append(attended)
+            done += count
+        other = swap(block, bit)
+        if not last:
+            block = join(block, after(other, attends[-1]))
+            bit //= 2
+    gathered = [block, other, swap(block, 1), swap(after(other, attends[-1]), 1)]
+    mixed = apply_fast(position, gathered, units, attends, norm_gain, output_weight, shards)
     return (mixed[None], momentum_next)
 
 

time: 138 us -> 110 us (0.80)
  local copies, waits for them, and re-layouts: 14.8 us -> 2.37 us
  waiting for transfers between devices: 40.8 us -> 28.7 us
  Pallas kernels: 64.3 us -> 54.5 us
  starting transfers between devices: 13.6 us -> 23.1 us
  other arithmetic: 2.58 us -> 0.18 us
    ppermute x8 -> x9, waiting for transfers between devices: 40.8 us -> 28.7 us  [swap(): return lax.ppermute(array, 'tok', [(i, i ^ bit) for i in range(shards)])]
    pallas_call x4 -> x6, Pallas kernels: 12.1 us -> 1.27 us  [the longest x1 0.99 us: update_rows(): pl.pallas_call(kernel, in_specs=[whole] * 4, out_specs=[whole, whole], ou...]
    ppermute x8 -> x9, starting transfers between devices: 5.99 us -> 15.7 us  [swap(): return lax.ppermute(array, 'tok', [(i, i ^ bit) for i in range(shards)])]
    unnamed x24 -> x12, local copies, waits for them, and re-layouts: 9.3 us -> 1.43 us
    reshape x4 -> x0, local copies, waits for them, and re-layouts: 4.44 us -> none  [the longest x3 3.37 us: flat(): return jnp.swapaxes(array, 1, 2).reshape(array.shape[0], 3 * width)]
    pallas_call x1 -> x3, Pallas kernels: 20.8 us -> 24.1 us  [project_and_attend(): pl.pallas_call(kernel, grid_spec=pltpu.PrefetchScalarGridSpec(num_scalar_...]
    pallas_call x1, Pallas kernels: 9.87 us -> 7.33 us  [apply_fast(): pl.pallas_call(kernel, grid_spec=pltpu.PrefetchScalarGridSpec(num_scalar_...]
    concatenate x2 -> x0, other arithmetic: 1.82 us -> none  [body(): block = jnp.concatenate([block, swap(block, bit)], axis=0)]
  transfers between devices with their start and end apart: 9 -> 10, of which waited for: 7 -> 6; matrix products, arithmetic and copies ran while one was open for 10% -> 1% of each run, Pallas kernels for 36% -> 38%
where the time goes in v2:
time: 110 us
  Pallas kernels  54.5 us (50%)
  waiting for transfers between devices  28.7 us (26%)
  starting transfers between devices  23.1 us (21%)
  local copies, waits for them, and re-layouts  2.37 us (2%)
    ppermute x9, waiting for transfers between devices, swap(): return lax.ppermute(array, 'tok', [(i, i ^ bit) for i in range(shards)])  28.7 us
    pallas_call x3, Pallas kernels, project_and_attend(): pl.pallas_call(kernel, grid_spec=pltpu.PrefetchScalarGridSpec(num_scalar_...  24.1 us
    pallas_call x1, Pallas kernels, fast_gradient(): pl.pallas_call(kernel, grid_spec=pltpu.PrefetchScalarGridSpec(num_scalar_...  16.3 us
    ppermute x9, starting transfers between devices, swap(): return lax.ppermute(array, 'tok', [(i, i ^ bit) for i in range(shards)])  15.7 us
    all_to_all x1, starting transfers between devices, body(): lax.all_to_all(sent.reshape(shards, tok_dev // shards, width), 'tok', spl...  7.38 us
    pallas_call x1, Pallas kernels, apply_fast(): pl.pallas_call(kernel, grid_spec=pltpu.PrefetchScalarGridSpec(num_scalar_...  7.33 us
    pallas_call x1, Pallas kernels, group_by_view(): pl.pallas_call(kernel, grid=(tok_dev // tile,), in_specs=[pl.BlockSpec((1...  5.57 us
  transfers between devices with their start and end apart: 10, of which 6 were waited for; matrix products, arithmetic and copies ran while one was open for 1% of the time, Pallas kernels for 38%

profile of v2, /device:TPU:0, one launch (start us, length us, event | category | flops | bytes accessed | tf_op | source)
XLA Modules:
  0.0 109.6 jit_solution(16754277552544189472)
XLA Ops:
  0.6 5.6 %group_by_view.1 = bf16[1024,1024]{1,0:T(8,128)(2,1)} custom-call(s32[1,1024]{1,0:T(1,128)} %bitcast.16, bf16[1024,1024]{1,0:T(8,128)(2,1)} %act_ref.2), custom_call_target="tpu_custom_call" | custom-call | flops 2147483648 | bytes 4194304 | tf_op jit(solution)/shard_map/group_by_view/pallas_call | solution.py:78
  6.2 7.4 %all-to-all-start = ((bf16[16,64,1024]{2,1,0:T(8,128)(2,1)}), bf16[16,64,1024]{2,1,0:T(8,128)(2,1)S(1)}, u32[]{:S(2)}, u32[]{:S(2)}) async-start(bf16[16,64,1024]{2,1,0:T(8,128)(2,1)} %bitcast.14), calls=%async_computation | async-start | bytes 4194304 | tf_op jit(solution)/shard_map/all_to_all | solution.py:445
  13.6 16.3 %fast_gradient.1 = (f32[128,3072]{1,0:T(8,128)}, bf16[128,3072]{1,0:T(8,128)(2,1)}) custom-call(s32[1]{0:T(128)} %bitcast.pos_ref, bf16[1024,1024]{1,0:T(8,128)(2,1)} %act_ref.2, bf16[1024,3072]{1,0:T(8,128)(2,1)} %wv_ref.7, bf16[1024,3072]{1,0:T(8,128)(2,1)} %wv_ref.7, bf16[4,1024]{1,0:T(4,128)(2,1)} %bitcast.15, f32[256,3,4,256]{3,2,1,0:T(4,128)} %fast_ref.1), custom_call_target="tpu_custom_call" | custom-call | flops 7516192768 | bytes 10223616 | tf_op jit(solution)/shard_map/fast_gradient/pallas_call | solution.py:169
  29.9 0.0 copy-start.5
  29.9 0.5 collective-permute-start
  30.3 2.1 %collective-permute-done.got_ref = bf16[128,3072]{1,0:T(8,128)(2,1)S(1)} collective-permute-done((bf16[128,3072]{1,0:T(8,128)(2,1)}, bf16[128,3072]{1,0:T(8,128)(2,1)S(1)}, u32[]{:S(2)}, u32[]{:S(2)}) %collective-permute-start) | collective-permute-done | bytes 786464 | tf_op jit(solution)/shard_map/ppermute | solution.py:442
  32.5 0.0 copy-start.1
  32.5 1.4 %copy-done.1 = f32[128,3072]{1,0:T(8,128)S(1)} copy-done((f32[128,3072]{1,0:T(8,128)S(1)}, f32[128,3072]{1,0:T(8,128)}, u32[]{:S(2)}) %copy-start.1) | copy-done | bytes 1572888
  33.9 0.0 copy-start.2
  33.9 0.1 add_and_halve.3
  34.0 1.9 %collective-permute-start.1 = (bf16[64,3072]{1,0:T(8,128)(2,1)S(1)}, bf16[64,3072]{1,0:T(8,128)(2,1)S(1)}, u32[]{:S(2)}, u32[]{:S(2)}) collective-permute-start(bf16[64,3072]{1,0:T(8,128)(2,1)S(1)} %get-tuple-element.29), channel_id=1, source_target_pairs={{0,2},{1,3},{2,0},{3,1},{4,6},{5,7},{6,4},{7,5},{8,10},{9,11},{10,... | collective-permute-start | bytes 1179656 | tf_op jit(solution)/shard_map/ppermute | solution.py:442
  35.9 14.3 %collective-permute-done.1.got_ref = bf16[64,3072]{1,0:T(8,128)(2,1)S(1)} collective-permute-done((bf16[64,3072]{1,0:T(8,128)(2,1)S(1)}, bf16[64,3072]{1,0:T(8,128)(2,1)S(1)}, u32[]{:S(2)}, u32[]{:S(2)}) %collective-permute-start.1) | collective-permute-done | bytes 393248 | tf_op jit(solution)/shard_map/ppermute | solution.py:442
  50.2 0.1 add_and_halve.4
  50.3 4.3 %collective-permute-start.2 = (bf16[32,3072]{1,0:T(8,128)(2,1)S(1)}, bf16[32,3072]{1,0:T(8,128)(2,1)S(1)}, u32[]{:S(2)}, u32[]{:S(2)}) collective-permute-start(bf16[32,3072]{1,0:T(8,128)(2,1)S(1)} %get-tuple-element.31), channel_id=1, source_target_pairs={{0,4},{1,5},{2,6},{3,7},{4,0},{5,1},{6,2},{7,3},{8,12},{9,13},{10,... | collective-permute-start | bytes 589832 | tf_op jit(solution)/shard_map/ppermute | solution.py:442
  54.6 0.0 copy-done.5
  54.6 0.2 reduce-window.9
  54.8 6.5 %collective-permute-done.2.got_ref = bf16[32,3072]{1,0:T(8,128)(2,1)S(1)} collective-permute-done((bf16[32,3072]{1,0:T(8,128)(2,1)S(1)}, bf16[32,3072]{1,0:T(8,128)(2,1)S(1)}, u32[]{:S(2)}, u32[]{:S(2)}) %collective-permute-start.2) | collective-permute-done | bytes 196640 | tf_op jit(solution)/shard_map/ppermute | solution.py:442
  61.3 4.7 %collective-permute-start.3 = (bf16[16,3072]{1,0:T(8,128)(2,1)S(1)}, bf16[16,3072]{1,0:T(8,128)(2,1)S(1)}, u32[]{:S(2)}, u32[]{:S(2)}) collective-permute-start(bf16[16,3072]{1,0:T(8,128)(2,1)S(1)} %get-tuple-element.33), channel_id=1, source_target_pairs={{0,8},{1,9},{2,10},{3,11},{4,12},{5,13},{6,14},{7,15},{8,0},{9,1},... | collective-permute-start | bytes 294920 | tf_op jit(solution)/shard_map/ppermute | solution.py:442
  66.1 0.9 constant_dynamic-slice_fusion.start_ref
  67.0 3.9 %collective-permute-done.3.got_ref = bf16[16,3072]{1,0:T(8,128)(2,1)S(1)} collective-permute-done((bf16[16,3072]{1,0:T(8,128)(2,1)S(1)}, bf16[16,3072]{1,0:T(8,128)(2,1)S(1)}, u32[]{:S(2)}, u32[]{:S(2)}) %collective-permute-start.3) | collective-permute-done | bytes 98336 | tf_op jit(solution)/shard_map/ppermute | solution.py:442
  70.9 0.0 copy-done.2
  70.9 1.0 update_rows.1
  71.9 0.7 collective-permute-start.4
  72.6 0.0 all-to-all-done
  72.6 0.0 copy-start
  72.6 6.3 %project_and_attend.3 = (bf16[1024,256]{1,0:T(8,128)(2,1)S(1)}, f32[1024,256]{1,0:T(8,128)S(1)}) custom-call(s32[3]{0:T(128)S(1)} %bitcast.11, bf16[1024,1024]{1,0:T(8,128)(2,1)S(1)} %bitcast.8, bf16[1024,3072]{1,0:T(8,128)(2,1)} %wv_ref.7, bf16[1024,3072]{1,0:T(8,128)(2,1)} %wv_ref.7, bf16[1024,3072]{1,0:T(8,128)(2,1)} %wv_ref.7), custom_call_target="tpu_custom_call" | custom-call | flops 2684354560 | bytes 5242880 | tf_op jit(solution)/shard_map/project_and_attend/pallas_call | solution.py:319
  78.9 0.6 collective-permute-done.4.second_ref
  79.4 3.0 %collective-permute-start.5 = (bf16[32,3072]{1,0:T(8,128)(2,1)S(1)}, bf16[32,3072]{1,0:T(8,128)(2,1)S(1)}, u32[]{:S(2)}, u32[]{:S(2)}) collective-permute-start(bf16[32,3072]{1,0:T(8,128)(2,1)S(1)} %join.2.first_ref), channel_id=1, source_target_pairs={{0,4},{1,5},{2,6},{3,7},{4,0},{5,1},{6,2},{7,3},{8,12},{9,13},{10,... | collective-permute-start | bytes 589832 | tf_op jit(solution)/shard_map/ppermute | solution.py:442
  82.4 0.0 copy-done
  82.4 6.1 %project_and_attend.4 = (bf16[1024,256]{1,0:T(8,128)(2,1)S(1)}, f32[1024,256]{1,0:T(8,128)S(1)}) custom-call(s32[3]{0:T(128)S(1)} %bitcast.12, bf16[1024,1024]{1,0:T(8,128)(2,1)S(1)} %bitcast.9, bf16[1024,3072]{1,0:T(8,128)(2,1)} %wv_ref.7, bf16[1024,3072]{1,0:T(8,128)(2,1)} %wv_ref.7, bf16[1024,3072]{1,0:T(8,128)(2,1)} %wv_ref.7), custom_call_target="tpu_custom_call" | custom-call | flops 2684354560 | bytes 5242880 | tf_op jit(solution)/shard_map/project_and_attend/pallas_call | solution.py:319
  88.5 0.0 collective-permute-done.5.second_ref
  88.5 0.0 copy-start.3
  88.5 0.0 copy-start.4
  88.6 0.1 collective-permute-start.7
  88.6 0.1 collective-permute-start.6
  88.7 11.7 %project_and_attend.5 = (bf16[1024,512]{1,0:T(8,128)(2,1)S(1)}, f32[1024,512]{1,0:T(8,128)S(1)}) custom-call(s32[3]{0:T(128)S(1)} %bitcast.13, bf16[1024,1024]{1,0:T(8,128)(2,1)} %bitcast.10, bf16[1024,3072]{1,0:T(8,128)(2,1)} %wv_ref.7, bf16[1024,3072]{1,0:T(8,128)(2,1)} %wv_ref.7, bf16[1024,3072]{1,0:T(8,128)(2,1)} %wv_ref.7), custom_call_target="tpu_custom_call" | custom-call | flops 5368709120 | bytes 8388608 | tf_op jit(solution)/shard_map/project_and_attend/pallas_call | solution.py:319
  100.4 0.0 collective-permute-done.6.refs_1_
  100.4 0.5 collective-permute-start.8
  100.9 0.0 collective-permute-done.7.refs_2_
  100.9 1.3 %collective-permute-done.8.refs_3_ = bf16[64,3072]{1,0:T(8,128)(2,1)S(1)} collective-permute-done((bf16[64,3072]{1,0:T(8,128)(2,1)S(1)}, bf16[64,3072]{1,0:T(8,128)(2,1)S(1)}, u32[]{:S(2)}, u32[]{:S(2)}) %collective-permute-start.8) | collective-permute-done | bytes 393248 | tf_op jit(solution)/shard_map/ppermute | solution.py:442
  102.3 0.0 copy-done.3
  102.3 0.0 copy-done.4
  102.3 7.3 %apply_fast.1 = bf16[1024,1024]{1,0:T(8,128)(2,1)} custom-call(s32[1]{0:T(128)} %bitcast.pos_ref, bf16[64,3072]{1,0:T(8,128)(2,1)S(1)} %join.3.refs_0_, bf16[64,3072]{1,0:T(8,128)(2,1)S(1)} %collective-permute-done.6.refs_1_, bf16[64,3072]{1,0:T(8,128)(2,1)S(1)} %collective-permute-done.7.refs_2_, bf16[64,3072]{1,0:T(8,128)(2,1)S(1)} %collective-permute-done.8.refs_3_, ...), custom_call_target="tpu_custom_call" | custom-call | flops 3758096384 | bytes 12058624 | tf_op jit(solution)/shard_map/apply_fast/pallas_call | solution.py:394
  (3 shorter events, 0.1 us)
Async XLA Ops:
  6.2 66.4 %all-to-all-start = ((bf16[16,64,1024]{2,1,0:T(8,128)(2,1)}), bf16[16,64,1024]{2,1,0:T(8,128)(2,1)S(1)}, u32[]{:S(2)}, u32[]{:S(2)}) async-start(bf16[16,64,1024]{2,1,0:T(8,128)(2,1)} %bitcast.14), calls=%async_computation | async-start | bytes 4194304 | tf_op jit(solution)/shard_map/all_to_all | solution.py:445
  29.9 24.8 %copy-start.5 = (s32[1,3]{1,0:T(1,128)S(1)}, s32[1,3]{1,0:T(1,128)}, u32[]{:S(2)}) copy-start(s32[1,3]{1,0:T(1,128)} %param.11) | copy-start | bytes 40
  29.9 2.6 %collective-permute-start = (bf16[128,3072]{1,0:T(8,128)(2,1)}, bf16[128,3072]{1,0:T(8,128)(2,1)S(1)}, u32[]{:S(2)}, u32[]{:S(2)}) collective-permute-start(bf16[128,3072]{1,0:T(8,128)(2,1)} %get-tuple-element.27), channel_id=1, source_target_pairs={{0,1},{1,0},{2,3},{3,2},{4,5},{5,4},{6,7},{7,6},{8,9},{9,8},{10,11... | collective-permute-start | bytes 2359304 | tf_op jit(solution)/shard_map/ppermute | solution.py:442
  32.5 1.4 %copy-start.1 = (f32[128,3072]{1,0:T(8,128)S(1)}, f32[128,3072]{1,0:T(8,128)}, u32[]{:S(2)}) copy-start(f32[128,3072]{1,0:T(8,128)} %get-tuple-element.26.keep_ref) | copy-start | bytes 4718596
  33.9 37.0 %copy-start.2 = (f32[16,3,4,256]{3,2,1,0:T(4,128)S(1)}, f32[16,3,4,256]{3,2,1,0:T(4,128)}, u32[]{:S(2)}) copy-start(f32[16,3,4,256]{3,2,1,0:T(4,128)} %mom_ref.1) | copy-start | bytes 589828
  34.0 16.2 %collective-permute-start.1 = (bf16[64,3072]{1,0:T(8,128)(2,1)S(1)}, bf16[64,3072]{1,0:T(8,128)(2,1)S(1)}, u32[]{:S(2)}, u32[]{:S(2)}) collective-permute-start(bf16[64,3072]{1,0:T(8,128)(2,1)S(1)} %get-tuple-element.29), channel_id=1, source_target_pairs={{0,2},{1,3},{2,0},{3,1},{4,6},{5,7},{6,4},{7,5},{8,10},{9,11},{10,... | collective-permute-start | bytes 1179656 | tf_op jit(solution)/shard_map/ppermute | solution.py:442
  50.3 11.0 %collective-permute-start.2 = (bf16[32,3072]{1,0:T(8,128)(2,1)S(1)}, bf16[32,3072]{1,0:T(8,128)(2,1)S(1)}, u32[]{:S(2)}, u32[]{:S(2)}) collective-permute-start(bf16[32,3072]{1,0:T(8,128)(2,1)S(1)} %get-tuple-element.31), channel_id=1, source_target_pairs={{0,4},{1,5},{2,6},{3,7},{4,0},{5,1},{6,2},{7,3},{8,12},{9,13},{10,... | collective-permute-start | bytes 589832 | tf_op jit(solution)/shard_map/ppermute | solution.py:442
  61.3 9.6 %collective-permute-start.3 = (bf16[16,3072]{1,0:T(8,128)(2,1)S(1)}, bf16[16,3072]{1,0:T(8,128)(2,1)S(1)}, u32[]{:S(2)}, u32[]{:S(2)}) collective-permute-start(bf16[16,3072]{1,0:T(8,128)(2,1)S(1)} %get-tuple-element.33), channel_id=1, source_target_pairs={{0,8},{1,9},{2,10},{3,11},{4,12},{5,13},{6,14},{7,15},{8,0},{9,1},... | collective-permute-start | bytes 294920 | tf_op jit(solution)/shard_map/ppermute | solution.py:442
  71.9 7.5 %collective-permute-start.4 = (bf16[16,3072]{1,0:T(8,128)(2,1)S(1)}, bf16[16,3072]{1,0:T(8,128)(2,1)S(1)}, u32[]{:S(2)}, u32[]{:S(2)}) collective-permute-start(bf16[16,3072]{1,0:T(8,128)(2,1)S(1)} %get-tuple-element.34.first_ref), channel_id=1, source_target_pairs={{0,8},{1,9},{2,10},{3,11},{4,12},{5,13},{6,14},{7,15},{8,0},{9,1},... | collective-permute-start | bytes 294920 | tf_op jit(solution)/shard_map/ppermute | solution.py:442
  72.6 9.8 %copy-start = (bf16[16,64,1024]{2,1,0:T(8,128)(2,1)}, bf16[16,64,1024]{2,1,0:T(8,128)(2,1)S(1)}, u32[]{:S(2)}) copy-start(bf16[16,64,1024]{2,1,0:T(8,128)(2,1)S(1)} %all-to-all-done) | copy-start | bytes 6291460
  79.4 9.1 %collective-permute-start.5 = (bf16[32,3072]{1,0:T(8,128)(2,1)S(1)}, bf16[32,3072]{1,0:T(8,128)(2,1)S(1)}, u32[]{:S(2)}, u32[]{:S(2)}) collective-permute-start(bf16[32,3072]{1,0:T(8,128)(2,1)S(1)} %join.2.first_ref), channel_id=1, source_target_pairs={{0,4},{1,5},{2,6},{3,7},{4,0},{5,1},{6,2},{7,3},{8,12},{9,13},{10,... | collective-permute-start | bytes 589832 | tf_op jit(solution)/shard_map/ppermute | solution.py:442
  88.5 13.7 %copy-start.3 = (bf16[1024,1024]{1,0:T(8,128)(2,1)S(1)}, bf16[1024,1024]{1,0:T(8,128)(2,1)}, u32[]{:S(2)}) copy-start(bf16[1024,1024]{1,0:T(8,128)(2,1)} %refs_11_.1) | copy-start | bytes 6291460
  88.5 13.7 %copy-start.4 = (f32[4,256]{1,0:T(4,128)S(1)}, f32[4,256]{1,0:T(4,128)}, u32[]{:S(2)}) copy-start(f32[4,256]{1,0:T(4,128)} %refs_10_.1) | copy-start | bytes 12292
  88.6 12.4 %collective-permute-start.7 = (bf16[64,3072]{1,0:T(8,128)(2,1)S(1)}, bf16[64,3072]{1,0:T(8,128)(2,1)S(1)}, u32[]{:S(2)}, u32[]{:S(2)}) collective-permute-start(bf16[64,3072]{1,0:T(8,128)(2,1)S(1)} %join.3.refs_0_), channel_id=1, source_target_pairs={{0,1},{1,0},{2,3},{3,2},{4,5},{5,4},{6,7},{7,6},{8,9},{9,8},{10,11... | collective-permute-start | bytes 1179656 | tf_op jit(solution)/shard_map/ppermute | solution.py:442
  88.6 11.8 %collective-permute-start.6 = (bf16[64,3072]{1,0:T(8,128)(2,1)S(1)}, bf16[64,3072]{1,0:T(8,128)(2,1)S(1)}, u32[]{:S(2)}, u32[]{:S(2)}) collective-permute-start(bf16[64,3072]{1,0:T(8,128)(2,1)S(1)} %join.3.refs_0_), channel_id=1, source_target_pairs={{0,2},{1,3},{2,0},{3,1},{4,6},{5,7},{6,4},{7,5},{8,10},{9,11},{10,... | collective-permute-start | bytes 1179656 | tf_op jit(solution)/shard_map/ppermute | solution.py:442
  100.4 1.8 %collective-permute-start.8 = (bf16[64,3072]{1,0:T(8,128)(2,1)S(1)}, bf16[64,3072]{1,0:T(8,128)(2,1)S(1)}, u32[]{:S(2)}, u32[]{:S(2)}) collective-permute-start(bf16[64,3072]{1,0:T(8,128)(2,1)S(1)} %collective-permute-done.6.refs_1_), channel_id=1, source_target_pairs={{0,1},{1,0},{2,3},{3,2},{4,5},{5,4},{6,7},{7,6},{8,9},{9,8},{10,11... | collective-permute-start | bytes 1179656 | tf_op jit(solution)/shard_map/ppermute | solution.py:442

commit v3 on v2

--- a/solution.py
+++ b/solution.py
@@ -24,10 +24,11 @@
     return lax.dot_general(a, b, (((1,), (1,)), ((), ())), preferred_element_type=F32)
 
 
-def bit_reverse(value, width):
+def offset_of(place, order):
     out = 0
-    for bit in range(width):
-        out |= ((value >> bit) & 1) << (width - 1 - bit)
+    for step, bit in enumerate(order):
+        if (place >> (len(order) - 1 - step)) & 1:
+            out |= bit
     return out
 
 
@@ -91,21 +92,24 @@
     )(view_id.reshape(1, tok_dev), activations)
 
 
-def fast_gradient(position, activations, project_weight, rate_weight, fast_start, shards):
+def fast_gradient(
+    position, activations, project_weight, rate_weight, fast_start, first, count, order
+):
     tok_dev, width = activations.shape
     heads = rate_weight.shape[1]
     kinds = fast_start.shape[1]
     size = width // heads
+    shards = 1 << len(order)
     slab = size // shards
-    stages = shards.bit_length() - 1
     tile = 256
     scale = 0.1 / math.sqrt(tok_dev * shards)
     half = size // 2
 
     def kernel(pos_ref, act_ref, wk_ref, wv_ref, rate_w_ref, fast_ref, keep_ref, send_ref,
                rate_ref, key_ref, out_ref, hid_ref, gate_ref, grad_ref, start_ref, sems):
-        head = pl.program_id(0)
-        slot = head % 2
+        step = pl.program_id(0)
+        head = first + step
+        slot = step % 2
 
         def fetch(which, place):
             return [
@@ -115,14 +119,14 @@
                 for kind in range(kinds)
             ]
 
-        @pl.when(head == 0)
+        @pl.when(step == 0)
         def _():
-            for copy in fetch(0, 0):
+            for copy in fetch(first, 0):
                 copy.start()
             raw = dot_nt(act_ref[...], rate_w_ref[...])
             rate_ref[...] = (jnp.maximum(raw, 0.0) + jnp.log1p(jnp.exp(-jnp.abs(raw)))) * scale
 
-        @pl.when(head + 1 < heads)
+        @pl.when(step + 1 < count)
         def _():
             for copy in fetch(head + 1, 1 - slot):
                 copy.start()
@@ -158,7 +162,7 @@
         grad_ref[:, 0 : 2 * size] = dot_tn(key_ref[...], gate_ref[...])
         grad_ref[:, 2 * size : 3 * size] = dot_tn(out_ref[...], hid_ref[...])
         for place in range(shards):
-            owner = pos_ref[0] ^ bit_reverse(place, stages)
+            owner = pos_ref[0] ^ offset_of(place, order)
             rows = grad_ref[pl.ds(pl.multiple_of(owner * slab, slab), slab), :]
             if place < shards // 2:
                 keep_ref[place * slab : (place + 1) * slab, :] = rows
@@ -170,11 +174,11 @@
         kernel,
         grid_spec=pltpu.PrefetchScalarGridSpec(
             num_scalar_prefetch=1,
-            grid=(heads,),
+            grid=(count,),
             in_specs=[
                 pl.BlockSpec((tok_dev, width), lambda h, p: (0, 0)),
-                pl.BlockSpec((width, size), lambda h, p: (0, heads + h)),
-                pl.BlockSpec((width, size), lambda h, p: (0, 2 * heads + h)),
+                pl.BlockSpec((width, size), lambda h, p: (0, heads + first + h)),
+                pl.BlockSpec((width, size), lambda h, p: (0, 2 * heads + first + h)),
                 pl.BlockSpec((heads, width), lambda h, p: (0, 0)),
                 pl.BlockSpec(memory_space=pl.ANY),
             ],
@@ -194,14 +198,14 @@
             ],
         ),
         out_shape=[
-            jax.ShapeDtypeStruct((half, 3 * width), F32),
-            jax.ShapeDtypeStruct((half, 3 * width), BF16),
+            jax.ShapeDtypeStruct((half, 3 * size * count), F32),
+            jax.ShapeDtypeStruct((half, 3 * size * count), BF16),
         ],
         compiler_params=params(60),
         cost_estimate=cost(
-            2 * tok_dev * width * (2 * width + 6 * size),
-            2 * tok_dev * width + 4 * width * width + 6 * size * width + 9 * size * width,
-            4 * tok_dev * width,
+            2 * tok_dev * size * count * (2 * width + 6 * size),
+            2 * tok_dev * width + 4 * width * size * count + 20 * size * size * count,
+            4 * tok_dev * size * count,
         ),
         name="fast_gradient",
     )(position, activations, project_weight, project_weight, rate_weight.T, fast_start)
@@ -230,33 +234,21 @@
     )(keep, received)
 
 
-def join(first, second):
-    rows, width = first.shape
-
-    def kernel(first_ref, second_ref, out_ref):
-        out_ref[:rows, :] = first_ref[...]
-        out_ref[rows:, :] = second_ref[...]
-
-    whole = pl.BlockSpec(memory_space=pltpu.VMEM)
-    return pl.pallas_call(
-        kernel,
-        in_specs=[whole, whole],
-        out_specs=whole,
-        out_shape=jax.ShapeDtypeStruct((2 * rows, width), BF16),
-        compiler_params=pltpu.CompilerParams(vmem_limit_bytes=4 * MIB),
-        cost_estimate=cost(0, 8 * rows * width),
-        name="join",
-    )(first, second)
-
-
-def update_rows(keep, received, momentum, own_start):
+def update_rows(keeps, receiveds, momentum, own_start):
     rows, kinds, heads, size = momentum.shape
-    width = keep.shape[1]
-
-    def kernel(keep_ref, got_ref, mom_ref, start_ref, next_ref, share_ref):
+    width = heads * kinds * size
+    streams = len(keeps)
+    stream_heads = heads // streams
+
+    def kernel(*refs):
+        keep_refs = refs[:streams]
+        got_refs = refs[streams : 2 * streams]
+        mom_ref, start_ref, next_ref, share_ref = refs[2 * streams :]
         for head in range(heads):
+            keep_ref = keep_refs[head // stream_heads]
+            got_ref = got_refs[head // stream_heads]
             for kind in range(kinds):
-                low = (head * kinds + kind) * size
+                low = ((head % stream_heads) * kinds + kind) * size
                 cols = slice(low, low + size)
                 moment = 0.9 * mom_ref[:, kind, head, :] + (
                     keep_ref[:, cols] + got_ref[:, cols].astype(F32)
@@ -267,12 +259,13 @@
                 factor = jnp.sqrt(jnp.sum(start * start, axis=-1, keepdims=True)) / jnp.sqrt(
                     jnp.sum(moved * moved, axis=-1, keepdims=True) + 1e-06
                 )
-                share_ref[:, cols] = (moved * factor).astype(BF16)
+                low = (head * kinds + kind) * size
+                share_ref[:, low : low + size] = (moved * factor).astype(BF16)
 
     whole = pl.BlockSpec(memory_space=pltpu.VMEM)
     return pl.pallas_call(
         kernel,
-        in_specs=[whole] * 4,
+        in_specs=[whole] * (2 * streams + 2),
         out_specs=[whole, whole],
         out_shape=[
             jax.ShapeDtypeStruct(momentum.shape, F32),
@@ -281,7 +274,7 @@
         compiler_params=pltpu.CompilerParams(vmem_limit_bytes=4 * MIB),
         cost_estimate=cost(8 * rows * width, 20 * rows * width),
         name="update_rows",
-    )(keep, received, momentum, own_start)
+    )(*keeps, *receiveds, momentum, own_start)
 
 
 def project_and_attend(window_ends, arrived, project_weight, heads, first, count):
@@ -351,7 +344,6 @@
     width = output_weight.shape[0]
     heads, size = norm_gain.shape
     slab = size // shards
-    stages = shards.bit_length() - 1
     tile = 256
     parts = len(gathered)
     part_rows = size // parts
@@ -368,11 +360,12 @@
 
         @pl.when(pl.program_id(0) == 0)
         def _():
-            for place in range(shards):
-                owner = pos_ref[0] ^ bit_reverse(place, stages)
-                low = (place * slab) % part_rows
-                rows = part_refs[place * slab // part_rows][low : low + slab, :]
-                wide_ref[pl.ds(pl.multiple_of(owner * slab, slab), slab), :] = rows.astype(F32)
+            core = pos_ref[0] % parts
+            for part in range(parts):
+                for place in range(shards // parts):
+                    owner = place * parts + (core ^ part)
+                    rows = part_refs[part][place * slab : (place + 1) * slab, :]
+                    wide_ref[pl.ds(pl.multiple_of(owner * slab, slab), slab), :] = rows.astype(F32)
             fast_ref[...] = wide_ref[...].astype(BF16)
 
         pieces = []
@@ -448,36 +441,31 @@
     ends = jnp.cumsum(window_lengths[0])
     own_start = lax.dynamic_slice_in_dim(fast_start, index * slab, slab, 0)
 
-    keep, send = fast_gradient(
-        position, after(activations, sent), project_weight, rate_weight, fast_start, shards
-    )
-    bit = 1
-    while bit < shards:
-        received = swap(send, bit)
-        bit *= 2
-        if bit < shards:
-            keep, send = add_and_halve(keep, received)
-    momentum_next, block = update_rows(keep, received, momentum, own_start)
-
-    stages = shards.bit_length() - 1
-    units, attends = [], []
-    bit = shards // 2
-    done = 0
-    for stage in range(stages - 1):
-        last = stage == stages - 2
-        count = heads - done if last else min(1, heads - done)
-        if count:
-            unit, attended = project_and_attend(
-                ends, after(arrived, block), project_weight, heads, done, count
-            )
-            units.append(unit)
-            attends.append(attended)
-            done += count
-        other = swap(block, bit)
-        if not last:
-            block = join(block, after(other, attends[-1]))
-            bit //= 2
-    gathered = [block, other, swap(block, 1), swap(after(other, attends[-1]), 1)]
+    bits = [1 << step for step in range(shards.bit_length() - 1)]
+    orders = [bits, bits[:1] + bits[2:] + bits[1:2]]
+    count = heads // len(orders)
+    keeps, receiveds = [], []
+    for stream, order in enumerate(orders):
+        keep, send = fast_gradient(
+            position, after(activations, sent), project_weight, rate_weight, fast_start,
+            stream * count, count, order,
+        )
+        for step, bit in enumerate(order):
+            received = swap(send, bit)
+            if step + 1 < len(order):
+                keep, send = add_and_halve(keep, received)
+        keeps.append(keep)
+        receiveds.append(received)
+    momentum_next, share = update_rows(keeps, receiveds, momentum, own_start)
+
+    cores = [[i for i in range(shards) if i % 2 == core] for core in range(2)]
+    block = lax.all_to_all(
+        jnp.broadcast_to(after(share, arrived)[None], (shards // 2, *share.shape)), "tok",
+        split_axis=0, concat_axis=0, tiled=True, axis_index_groups=cores,
+    ).reshape(size // 2, 3 * width)
+    unit, attended = project_and_attend(ends, after(arrived, share), project_weight, heads, 0, heads)
+    units, attends = [unit], [attended]
+    gathered = [block, swap(after(block, attended), 1)]
     mixed = apply_fast(position, gathered, units, attends, norm_gain, output_weight, shards)
     return (mixed[None], momentum_next)
 

time: 110 us -> 115 us (1.045)
  local copies, waits for them, and re-layouts: 2.37 us -> 8.17 us
  starting transfers between devices: 23.1 us -> 21.4 us
    ppermute x9, starting transfers between devices: 15.7 us -> 10.3 us  [swap(): return lax.ppermute(array, 'tok', [(i, i ^ bit) for i in range(shards)])]
    unnamed x12 -> x18, local copies, waits for them, and re-layouts: 1.43 us -> 6.25 us
    pallas_call x1 -> x2, Pallas kernels: 16.3 us -> 20.4 us  [fast_gradient(): pl.pallas_call(kernel, grid_spec=pltpu.PrefetchScalarGridSpec(num_scalar_...]
    all_to_all x0 -> x1, starting transfers between devices: none -> 3.73 us  [body(): lax.all_to_all(jnp.broadcast_to(after(share, arrived)[None], (shards // 2...]
    pallas_call x3 -> x1, Pallas kernels: 24.1 us -> 20.9 us  [project_and_attend(): pl.pallas_call(kernel, grid_spec=pltpu.PrefetchScalarGridSpec(num_scalar_...]
  transfers between devices with their start and end apart: 10 -> 11, of which waited for: 6 -> 5; matrix products, arithmetic and copies ran while one was open for 1% -> 1% of each run, Pallas kernels for 38% -> 37%
where the time goes in v3:
time: 115 us
  Pallas kernels  55.3 us (48%)
  waiting for transfers between devices  29.1 us (25%)
  starting transfers between devices  21.4 us (19%)
  local copies, waits for them, and re-layouts  8.17 us (7%)
    ppermute x9, waiting for transfers between devices, swap(): return lax.ppermute(array, 'tok', [(i, i ^ bit) for i in range(shards)])  29.1 us
    pallas_call x1, Pallas kernels, project_and_attend(): pl.pallas_call(kernel, grid_spec=pltpu.PrefetchScalarGridSpec(num_scalar_...  20.9 us
    pallas_call x2, Pallas kernels, fast_gradient(): pl.pallas_call(kernel, grid_spec=pltpu.PrefetchScalarGridSpec(num_scalar_...  20.4 us
    ppermute x9, starting transfers between devices, swap(): return lax.ppermute(array, 'tok', [(i, i ^ bit) for i in range(shards)])  10.3 us
    all_to_all x1, starting transfers between devices, body(): lax.all_to_all(sent.reshape(shards, tok_dev // shards, width), 'tok', spl...  7.44 us
    pallas_call x1, Pallas kernels, apply_fast(): pl.pallas_call(kernel, grid_spec=pltpu.PrefetchScalarGridSpec(num_scalar_...  7.21 us
    unnamed x18, local copies, waits for them, and re-layouts  6.25 us
    pallas_call x1, Pallas kernels, group_by_view(): pl.pallas_call(kernel, grid=(tok_dev // tile,), in_specs=[pl.BlockSpec((1...  5.57 us
  transfers between devices with their start and end apart: 11, of which 5 were waited for; matrix products, arithmetic and copies ran while one was open for 1% of the time, Pallas kernels for 37%

profile of v3, /device:TPU:0, one launch (start us, length us, event | category | flops | bytes accessed | tf_op | source)
XLA Modules:
  0.0 115.0 jit_solution(6724964118862320978)
XLA Ops:
  0.6 5.6 %group_by_view.1 = bf16[1024,1024]{1,0:T(8,128)(2,1)} custom-call(s32[1,1024]{1,0:T(1,128)} %bitcast.15, bf16[1024,1024]{1,0:T(8,128)(2,1)} %act_ref.3), custom_call_target="tpu_custom_call" | custom-call | flops 2147483648 | bytes 4194304 | tf_op jit(solution)/shard_map/group_by_view/pallas_call | solution.py:79
  6.2 7.4 %all-to-all-start = ((bf16[16,64,1024]{2,1,0:T(8,128)(2,1)}), bf16[16,64,1024]{2,1,0:T(8,128)(2,1)}, u32[]{:S(2)}, u32[]{:S(2)}) async-start(bf16[16,64,1024]{2,1,0:T(8,128)(2,1)} %bitcast.12), calls=%async_computation | async-start | bytes 4194304 | tf_op jit(solution)/shard_map/all_to_all | solution.py:438
  13.6 10.3 %fast_gradient.3 = (f32[128,1536]{1,0:T(8,128)}, bf16[128,1536]{1,0:T(8,128)(2,1)}) custom-call(s32[1]{0:T(128)} %bitcast.pos_ref, bf16[1024,1024]{1,0:T(8,128)(2,1)} %act_ref.3, bf16[1024,3072]{1,0:T(8,128)(2,1)} %wv_ref.5, bf16[1024,3072]{1,0:T(8,128)(2,1)} %wv_ref.5, bf16[4,1024]{1,0:T(4,128)(2,1)} %bitcast.13, f32[256,3,4,256]{3,2,1,0:T(4,128)} %fast_ref.3), custom_call_target="tpu_custom_call" | custom-call | flops 3758096384 | bytes 6815744 | tf_op jit(solution)/shard_map/fast_gradient/pallas_call | solution.py:173
  23.9 0.0 copy-start.1
  23.9 0.4 collective-permute-start.3
  24.3 10.1 %fast_gradient.2 = (f32[128,1536]{1,0:T(8,128)}, bf16[128,1536]{1,0:T(8,128)(2,1)}) custom-call(s32[1]{0:T(128)} %bitcast.pos_ref, bf16[1024,1024]{1,0:T(8,128)(2,1)} %act_ref.3, bf16[1024,3072]{1,0:T(8,128)(2,1)} %wv_ref.5, bf16[1024,3072]{1,0:T(8,128)(2,1)} %wv_ref.5, bf16[4,1024]{1,0:T(4,128)(2,1)} %bitcast.14, f32[256,3,4,256]{3,2,1,0:T(4,128)} %fast_ref.3), custom_call_target="tpu_custom_call" | custom-call | flops 3758096384 | bytes 6815744 | tf_op jit(solution)/shard_map/fast_gradient/pallas_call | solution.py:173
  34.5 0.2 collective-permute-start
  34.7 0.0 collective-permute-done.3.got_ref
  34.7 0.0 copy-done.1
  34.7 0.0 copy-start.2
  34.7 0.1 add_and_halve.9
  34.8 1.9 %collective-permute-start.4 = (bf16[64,1536]{1,0:T(8,128)(2,1)S(1)}, bf16[64,1536]{1,0:T(8,128)(2,1)S(1)}, u32[]{:S(2)}, u32[]{:S(2)}) collective-permute-start(bf16[64,1536]{1,0:T(8,128)(2,1)S(1)} %get-tuple-element.37), channel_id=1, source_target_pairs={{0,4},{1,5},{2,6},{3,7},{4,0},{5,1},{6,2},{7,3},{8,12},{9,13},{10,... | collective-permute-start | bytes 589832 | tf_op jit(solution)/shard_map/ppermute | solution.py:435
  36.7 0.0 collective-permute-done.got_ref
  36.7 0.0 copy-start
  36.7 1.1 copy-done
  37.8 0.1 add_and_halve.6
  37.9 1.5 %collective-permute-start.1 = (bf16[64,1536]{1,0:T(8,128)(2,1)S(1)}, bf16[64,1536]{1,0:T(8,128)(2,1)S(1)}, u32[]{:S(2)}, u32[]{:S(2)}) collective-permute-start(bf16[64,1536]{1,0:T(8,128)(2,1)S(1)} %get-tuple-element.30), channel_id=1, source_target_pairs={{0,2},{1,3},{2,0},{3,1},{4,6},{5,7},{6,4},{7,5},{8,10},{9,11},{10,... | collective-permute-start | bytes 589832 | tf_op jit(solution)/shard_map/ppermute | solution.py:435
  39.4 13.3 %collective-permute-done.4.got_ref = bf16[64,1536]{1,0:T(8,128)(2,1)S(1)} collective-permute-done((bf16[64,1536]{1,0:T(8,128)(2,1)S(1)}, bf16[64,1536]{1,0:T(8,128)(2,1)S(1)}, u32[]{:S(2)}, u32[]{:S(2)}) %collective-permute-start.4) | collective-permute-done | bytes 196640 | tf_op jit(solution)/shard_map/ppermute | solution.py:435
  52.8 4.5 %collective-permute-start.5 = (bf16[32,1536]{1,0:T(8,128)(2,1)S(1)}, bf16[32,1536]{1,0:T(8,128)(2,1)S(1)}, u32[]{:S(2)}, u32[]{:S(2)}) collective-permute-start(bf16[32,1536]{1,0:T(8,128)(2,1)S(1)} %get-tuple-element.39), channel_id=1, source_target_pairs={{0,8},{1,9},{2,10},{3,11},{4,12},{5,13},{6,14},{7,15},{8,0},{9,1},... | collective-permute-start | bytes 294920 | tf_op jit(solution)/shard_map/ppermute | solution.py:435
  57.3 0.0 collective-permute-done.1.got_ref
  57.3 0.0 copy-start.8
  57.3 0.1 collective-permute-start.2
  57.4 9.5 %collective-permute-done.5.got_ref = bf16[32,1536]{1,0:T(8,128)(2,1)S(1)} collective-permute-done((bf16[32,1536]{1,0:T(8,128)(2,1)S(1)}, bf16[32,1536]{1,0:T(8,128)(2,1)S(1)}, u32[]{:S(2)}, u32[]{:S(2)}) %collective-permute-start.5) | collective-permute-done | bytes 98336 | tf_op jit(solution)/shard_map/ppermute | solution.py:435
  66.9 1.5 %collective-permute-start.7 = (bf16[16,1536]{1,0:T(8,128)(2,1)S(1)}, bf16[16,1536]{1,0:T(8,128)(2,1)S(1)}, u32[]{:S(2)}, u32[]{:S(2)}) collective-permute-start(bf16[16,1536]{1,0:T(8,128)(2,1)S(1)} %get-tuple-element.42), channel_id=1, source_target_pairs={{0,2},{1,3},{2,0},{3,1},{4,6},{5,7},{6,4},{7,5},{8,10},{9,11},{10,... | collective-permute-start | bytes 147464 | tf_op jit(solution)/shard_map/ppermute | solution.py:435
  68.5 0.0 collective-permute-done.2.got_ref
  68.5 0.1 collective-permute-start.6
  68.6 0.9 constant_dynamic-slice_fusion.refs_5_
  69.5 1.6 %collective-permute-done.7.refs_3_ = bf16[16,1536]{1,0:T(8,128)(2,1)S(1)} collective-permute-done((bf16[16,1536]{1,0:T(8,128)(2,1)S(1)}, bf16[16,1536]{1,0:T(8,128)(2,1)S(1)}, u32[]{:S(2)}, u32[]{:S(2)}) %collective-permute-start.7) | collective-permute-done | bytes 49184 | tf_op jit(solution)/shard_map/ppermute | solution.py:435
  71.1 2.5 %collective-permute-done.6.refs_2_ = bf16[16,1536]{1,0:T(8,128)(2,1)S(1)} collective-permute-done((bf16[16,1536]{1,0:T(8,128)(2,1)S(1)}, bf16[16,1536]{1,0:T(8,128)(2,1)S(1)}, u32[]{:S(2)}, u32[]{:S(2)}) %collective-permute-start.6) | collective-permute-done | bytes 49184 | tf_op jit(solution)/shard_map/ppermute | solution.py:435
  73.5 0.0 copy-done.2
  73.6 1.0 update_rows.1
  74.5 0.0 all-to-all-done
  74.6 1.0 broadcast_in_dim.4
  75.5 3.7 %all-to-all-start.1 = ((bf16[8,16,3072]{2,1,0:T(8,128)(2,1)}), bf16[8,16,3072]{2,1,0:T(8,128)(2,1)S(1)}, u32[]{:S(2)}, u32[]{:S(2)}) async-start(bf16[8,16,3072]{2,1,0:T(8,128)(2,1)} %broadcast_in_dim.4), calls=%async_computation.1 | async-start | bytes 1572864 | tf_op jit(solution)/shard_map/all_to_all | solution.py:462
  79.3 0.0 copy-done.8
  79.3 0.2 reduce-window.9
  79.4 0.0 copy-start.3
  79.4 0.0 copy-start.4
  79.4 20.9 %project_and_attend.1 = (bf16[1024,1024]{1,0:T(8,128)(2,1)S(1)}, f32[1024,1024]{1,0:T(8,128)}) custom-call(s32[3]{0:T(128)S(1)} %bitcast.11, bf16[1024,1024]{1,0:T(8,128)(2,1)} %bitcast.4.x_ref, bf16[1024,3072]{1,0:T(8,128)(2,1)} %wv_ref.5, bf16[1024,3072]{1,0:T(8,128)(2,1)} %wv_ref.5, bf16[1024,3072]{1,0:T(8,128)(2,1)} %wv_ref.5), custom_call_target="tpu_custom_call" | custom-call | flops 10737418240 | bytes 14680064 | tf_op jit(solution)/shard_map/project_and_attend/pallas_call | solution.py:312
  100.4 0.0 copy-start.6
  100.4 1.3 %copy-done.6 = bf16[1024,1024]{1,0:T(8,128)(2,1)} copy-done((bf16[1024,1024]{1,0:T(8,128)(2,1)}, bf16[1024,1024]{1,0:T(8,128)(2,1)S(1)}, u32[]{:S(2)}) %copy-start.6) | copy-done | bytes 2097176
  101.7 0.0 all-to-all-done.1
  101.7 0.0 collective-permute-start.8
  101.7 2.3 %collective-permute-done.8.refs_1_ = bf16[128,3072]{1,0:T(8,128)(2,1)S(1)} collective-permute-done((bf16[128,3072]{1,0:T(8,128)(2,1)S(1)}, bf16[128,3072]{1,0:T(8,128)(2,1)S(1)}, u32[]{:S(2)}, u32[]{:S(2)}) %collective-permute-start.8) | collective-permute-done | bytes 786464 | tf_op jit(solution)/shard_map/ppermute | solution.py:435
  104.0 0.0 copy-done.3
  104.0 0.0 copy-done.4
  104.0 0.0 copy-start.5
  104.0 2.2 %copy-done.5 = f32[1024,1024]{1,0:T(8,128)S(1)} copy-done((f32[1024,1024]{1,0:T(8,128)S(1)}, f32[1024,1024]{1,0:T(8,128)}, u32[]{:S(2)}) %copy-start.5) | copy-done | bytes 4194328
  106.2 0.0 copy-start.7
  106.2 1.6 %copy-done.7 = bf16[1024,1024]{1,0:T(8,128)(2,1)S(1)} copy-done((bf16[1024,1024]{1,0:T(8,128)(2,1)S(1)}, bf16[1024,1024]{1,0:T(8,128)(2,1)}, u32[]{:S(2)}) %copy-start.7) | copy-done | bytes 2097176
  107.8 7.2 %apply_fast.1 = bf16[1024,1024]{1,0:T(8,128)(2,1)} custom-call(s32[1]{0:T(128)} %bitcast.pos_ref, bf16[128,3072]{1,0:T(8,128)(2,1)S(1)} %bitcast.10, bf16[128,3072]{1,0:T(8,128)(2,1)S(1)} %collective-permute-done.8.refs_1_, bf16[1024,1024]{1,0:T(8,128)(2,1)S(1)} %copy-done.7, f32[1024,1024]{1,0:T(8,128)S(1)} %copy-done.5, f32[4,256]{1,0:T(4,128)S(1)} %copy-done.4, ...), custom_call_target="tpu_custom_call" | custom-call | flops 3758096384 | bytes 12058624 | tf_op jit(solution)/shard_map/apply_fast/pallas_call | solution.py:387
  (4 shorter events, 0.1 us)
Async XLA Ops:
  6.2 68.4 %all-to-all-start = ((bf16[16,64,1024]{2,1,0:T(8,128)(2,1)}), bf16[16,64,1024]{2,1,0:T(8,128)(2,1)}, u32[]{:S(2)}, u32[]{:S(2)}) async-start(bf16[16,64,1024]{2,1,0:T(8,128)(2,1)} %bitcast.12), calls=%async_computation | async-start | bytes 4194304 | tf_op jit(solution)/shard_map/all_to_all | solution.py:438
  23.9 10.8 %copy-start.1 = (f32[128,1536]{1,0:T(8,128)S(1)}, f32[128,1536]{1,0:T(8,128)}, u32[]{:S(2)}) copy-start(f32[128,1536]{1,0:T(8,128)} %get-tuple-element.34.keep_ref) | copy-start | bytes 2359300
  23.9 10.8 %collective-permute-start.3 = (bf16[128,1536]{1,0:T(8,128)(2,1)}, bf16[128,1536]{1,0:T(8,128)(2,1)S(1)}, u32[]{:S(2)}, u32[]{:S(2)}) collective-permute-start(bf16[128,1536]{1,0:T(8,128)(2,1)} %get-tuple-element.35), channel_id=1, source_target_pairs={{0,1},{1,0},{2,3},{3,2},{4,5},{5,4},{6,7},{7,6},{8,9},{9,8},{10,11... | collective-permute-start | bytes 1179656 | tf_op jit(solution)/shard_map/ppermute | solution.py:435
  34.5 2.2 %collective-permute-start = (bf16[128,1536]{1,0:T(8,128)(2,1)}, bf16[128,1536]{1,0:T(8,128)(2,1)S(1)}, u32[]{:S(2)}, u32[]{:S(2)}) collective-permute-start(bf16[128,1536]{1,0:T(8,128)(2,1)} %get-tuple-element.28), channel_id=1, source_target_pairs={{0,1},{1,0},{2,3},{3,2},{4,5},{5,4},{6,7},{7,6},{8,9},{9,8},{10,11... | collective-permute-start | bytes 1179656 | tf_op jit(solution)/shard_map/ppermute | solution.py:435
  34.7 38.9 %copy-start.2 = (f32[16,3,4,256]{3,2,1,0:T(4,128)S(1)}, f32[16,3,4,256]{3,2,1,0:T(4,128)}, u32[]{:S(2)}) copy-start(f32[16,3,4,256]{3,2,1,0:T(4,128)} %refs_4_.2) | copy-start | bytes 589828
  34.8 18.0 %collective-permute-start.4 = (bf16[64,1536]{1,0:T(8,128)(2,1)S(1)}, bf16[64,1536]{1,0:T(8,128)(2,1)S(1)}, u32[]{:S(2)}, u32[]{:S(2)}) collective-permute-start(bf16[64,1536]{1,0:T(8,128)(2,1)S(1)} %get-tuple-element.37), channel_id=1, source_target_pairs={{0,4},{1,5},{2,6},{3,7},{4,0},{5,1},{6,2},{7,3},{8,12},{9,13},{10,... | collective-permute-start | bytes 589832 | tf_op jit(solution)/shard_map/ppermute | solution.py:435
  36.7 1.1 copy-start
  37.9 19.4 %collective-permute-start.1 = (bf16[64,1536]{1,0:T(8,128)(2,1)S(1)}, bf16[64,1536]{1,0:T(8,128)(2,1)S(1)}, u32[]{:S(2)}, u32[]{:S(2)}) collective-permute-start(bf16[64,1536]{1,0:T(8,128)(2,1)S(1)} %get-tuple-element.30), channel_id=1, source_target_pairs={{0,2},{1,3},{2,0},{3,1},{4,6},{5,7},{6,4},{7,5},{8,10},{9,11},{10,... | collective-permute-start | bytes 589832 | tf_op jit(solution)/shard_map/ppermute | solution.py:435
  52.8 14.1 %collective-permute-start.5 = (bf16[32,1536]{1,0:T(8,128)(2,1)S(1)}, bf16[32,1536]{1,0:T(8,128)(2,1)S(1)}, u32[]{:S(2)}, u32[]{:S(2)}) collective-permute-start(bf16[32,1536]{1,0:T(8,128)(2,1)S(1)} %get-tuple-element.39), channel_id=1, source_target_pairs={{0,8},{1,9},{2,10},{3,11},{4,12},{5,13},{6,14},{7,15},{8,0},{9,1},... | collective-permute-start | bytes 294920 | tf_op jit(solution)/shard_map/ppermute | solution.py:435
  57.3 21.9 %copy-start.8 = (s32[1,3]{1,0:T(1,128)S(1)}, s32[1,3]{1,0:T(1,128)}, u32[]{:S(2)}) copy-start(s32[1,3]{1,0:T(1,128)} %param.11) | copy-start | bytes 40
  57.3 11.1 %collective-permute-start.2 = (bf16[32,1536]{1,0:T(8,128)(2,1)S(1)}, bf16[32,1536]{1,0:T(8,128)(2,1)S(1)}, u32[]{:S(2)}, u32[]{:S(2)}) collective-permute-start(bf16[32,1536]{1,0:T(8,128)(2,1)S(1)} %get-tuple-element.32), channel_id=1, source_target_pairs={{0,4},{1,5},{2,6},{3,7},{4,0},{5,1},{6,2},{7,3},{8,12},{9,13},{10,... | collective-permute-start | bytes 294920 | tf_op jit(solution)/shard_map/ppermute | solution.py:435
  66.9 4.2 %collective-permute-start.7 = (bf16[16,1536]{1,0:T(8,128)(2,1)S(1)}, bf16[16,1536]{1,0:T(8,128)(2,1)S(1)}, u32[]{:S(2)}, u32[]{:S(2)}) collective-permute-start(bf16[16,1536]{1,0:T(8,128)(2,1)S(1)} %get-tuple-element.42), channel_id=1, source_target_pairs={{0,2},{1,3},{2,0},{3,1},{4,6},{5,7},{6,4},{7,5},{8,10},{9,11},{10,... | collective-permute-start | bytes 147464 | tf_op jit(solution)/shard_map/ppermute | solution.py:435
  68.5 5.1 %collective-permute-start.6 = (bf16[16,1536]{1,0:T(8,128)(2,1)S(1)}, bf16[16,1536]{1,0:T(8,128)(2,1)S(1)}, u32[]{:S(2)}, u32[]{:S(2)}) collective-permute-start(bf16[16,1536]{1,0:T(8,128)(2,1)S(1)} %get-tuple-element.41), channel_id=1, source_target_pairs={{0,8},{1,9},{2,10},{3,11},{4,12},{5,13},{6,14},{7,15},{8,0},{9,1},... | collective-permute-start | bytes 147464 | tf_op jit(solution)/shard_map/ppermute | solution.py:435
  75.5 26.2 %all-to-all-start.1 = ((bf16[8,16,3072]{2,1,0:T(8,128)(2,1)}), bf16[8,16,3072]{2,1,0:T(8,128)(2,1)S(1)}, u32[]{:S(2)}, u32[]{:S(2)}) async-start(bf16[8,16,3072]{2,1,0:T(8,128)(2,1)} %broadcast_in_dim.4), calls=%async_computation.1 | async-start | bytes 1572864 | tf_op jit(solution)/shard_map/all_to_all | solution.py:462
  79.4 24.5 %copy-start.3 = (bf16[1024,1024]{1,0:T(8,128)(2,1)S(1)}, bf16[1024,1024]{1,0:T(8,128)(2,1)}, u32[]{:S(2)}) copy-start(bf16[1024,1024]{1,0:T(8,128)(2,1)} %refs_5_.1) | copy-start | bytes 6291460
  79.4 24.5 %copy-start.4 = (f32[4,256]{1,0:T(4,128)S(1)}, f32[4,256]{1,0:T(4,128)}, u32[]{:S(2)}) copy-start(f32[4,256]{1,0:T(4,128)} %refs_4_.3) | copy-start | bytes 12292
  100.4 1.3 %copy-start.6 = (bf16[1024,1024]{1,0:T(8,128)(2,1)}, bf16[1024,1024]{1,0:T(8,128)(2,1)S(1)}, u32[]{:S(2)}) copy-start(bf16[1024,1024]{1,0:T(8,128)(2,1)S(1)} %get-tuple-element.48.refs_2_) | copy-start | bytes 6291460
  101.7 2.3 %collective-permute-start.8 = (bf16[128,3072]{1,0:T(8,128)(2,1)S(1)}, bf16[128,3072]{1,0:T(8,128)(2,1)S(1)}, u32[]{:S(2)}, u32[]{:S(2)}) collective-permute-start(bf16[128,3072]{1,0:T(8,128)(2,1)S(1)} %bitcast.9), channel_id=1, source_target_pairs={{0,1},{1,0},{2,3},{3,2},{4,5},{5,4},{6,7},{7,6},{8,9},{9,8},{10,11... | collective-permute-start | bytes 2359304 | tf_op jit(solution)/shard_map/ppermute | solution.py:435
  104.0 2.2 %copy-start.5 = (f32[1024,1024]{1,0:T(8,128)S(1)}, f32[1024,1024]{1,0:T(8,128)}, u32[]{:S(2)}) copy-start(f32[1024,1024]{1,0:T(8,128)} %get-tuple-element.46.refs_3_) | copy-start | bytes 12582916
  106.2 1.6 %copy-start.7 = (bf16[1024,1024]{1,0:T(8,128)(2,1)S(1)}, bf16[1024,1024]{1,0:T(8,128)(2,1)}, u32[]{:S(2)}) copy-start(bf16[1024,1024]{1,0:T(8,128)(2,1)} %copy-done.6) | copy-start | bytes 6291460

commit v4 on v2

--- a/solution.py
+++ b/solution.py
@@ -51,7 +51,7 @@
     tok_dev, width = activations.shape
     per_view = tok_dev // shards
     chunk = 256
-    tile = 256
+    tile = 1024
 
     def kernel(view_ref, act_ref, out_ref, slot_ref):
         @pl.when(pl.program_id(0) == 0)
@@ -98,7 +98,7 @@
     size = width // heads
     slab = size // shards
     stages = shards.bit_length() - 1
-    tile = 256
+    tile = 1024
     scale = 0.1 / math.sqrt(tok_dev * shards)
     half = size // 2
 
@@ -288,7 +288,7 @@
     tok_dev, width = arrived.shape
     size = width // heads
     windows = window_ends.shape[0]
-    tile = 256
+    tile = 512
     scale = 1.0 / math.sqrt(size)
 
     def kernel(ends_ref, x_ref, wq_ref, wk_ref, wv_ref, unit_ref, att_ref):
@@ -352,7 +352,7 @@
     heads, size = norm_gain.shape
     slab = size // shards
     stages = shards.bit_length() - 1
-    tile = 256
+    tile = 1024
     parts = len(gathered)
     part_rows = size // parts
     pieces_of = len(units)
@@ -409,7 +409,7 @@
             ],
         ),
         out_shape=jax.ShapeDtypeStruct((tok_dev, width), BF16),
-        compiler_params=params(20),
+        compiler_params=params(40),
         cost_estimate=cost(
             2 * tok_dev * width * (width + 3 * size),
             8 * tok_dev * width + 2 * width * width + 6 * size * width,
@@ -451,18 +451,23 @@
     keep, send = fast_gradient(
         position, after(activations, sent), project_weight, rate_weight, fast_start, shards
     )
+    units, attends = [], []
     bit = 1
     while bit < shards:
         received = swap(send, bit)
+        if bit == 8:
+            unit, attended = project_and_attend(ends, after(arrived, send), project_weight, heads, 0, 1)
+            units.append(unit)
+            attends.append(attended)
+            done = 1
+            received = after(received, attended)
         bit *= 2
         if bit < shards:
             keep, send = add_and_halve(keep, received)
     momentum_next, block = update_rows(keep, received, momentum, own_start)
 
     stages = shards.bit_length() - 1
-    units, attends = [], []
     bit = shards // 2
-    done = 0
     for stage in range(stages - 1):
         last = stage == stages - 2
         count = heads - done if last else min(1, heads - done)

time: 110 us -> 103 us (0.936)
  Pallas kernels: 54.5 us -> 50.5 us
  starting transfers between devices: 23.1 us -> 19.9 us
    ppermute x9, starting transfers between devices: 15.7 us -> 12.5 us  [swap(): return lax.ppermute(array, 'tok', [(i, i ^ bit) for i in range(shards)])]
    pallas_call x1, Pallas kernels: 16.3 us -> 14.4 us  [fast_gradient(): pl.pallas_call(kernel, grid_spec=pltpu.PrefetchScalarGridSpec(num_scalar_...]
    pallas_call x1, Pallas kernels: 7.33 us -> 5.76 us  [apply_fast(): pl.pallas_call(kernel, grid_spec=pltpu.PrefetchScalarGridSpec(num_scalar_...]
    pallas_call x3 -> x4, Pallas kernels: 24.1 us -> 23.6 us  [project_and_attend(): pl.pallas_call(kernel, grid_spec=pltpu.PrefetchScalarGridSpec(num_scalar_...]
  transfers between devices with their start and end apart: 10 -> 10, of which waited for: 6 -> 6; matrix products, arithmetic and copies ran while one was open for 1% -> 1% of each run, Pallas kernels for 38% -> 37%
where the time goes in v4:
time: 103 us
  Pallas kernels  50.5 us (49%)
  waiting for transfers between devices  29.1 us (28%)
  starting transfers between devices  19.9 us (19%)
  local copies, waits for them, and re-layouts  2.37 us (2%)
    ppermute x9, waiting for transfers between devices, swap(): return lax.ppermute(array, 'tok', [(i, i ^ bit) for i in range(shards)])  29.1 us
    pallas_call x4, Pallas kernels, project_and_attend(): pl.pallas_call(kernel, grid_spec=pltpu.PrefetchScalarGridSpec(num_scalar_...  23.6 us
    pallas_call x1, Pallas kernels, fast_gradient(): pl.pallas_call(kernel, grid_spec=pltpu.PrefetchScalarGridSpec(num_scalar_...  14.4 us
    ppermute x9, starting transfers between devices, swap(): return lax.ppermute(array, 'tok', [(i, i ^ bit) for i in range(shards)])  12.5 us
    all_to_all x1, starting transfers between devices, body(): lax.all_to_all(sent.reshape(shards, tok_dev // shards, width), 'tok', spl...  7.39 us
    pallas_call x1, Pallas kernels, apply_fast(): pl.pallas_call(kernel, grid_spec=pltpu.PrefetchScalarGridSpec(num_scalar_...  5.76 us
    pallas_call x1, Pallas kernels, group_by_view(): pl.pallas_call(kernel, grid=(tok_dev // tile,), in_specs=[pl.BlockSpec((1...  5.41 us
  transfers between devices with their start and end apart: 10, of which 6 were waited for; matrix products, arithmetic and copies ran while one was open for 1% of the time, Pallas kernels for 37%

profile of v4, /device:TPU:0, one launch (start us, length us, event | category | flops | bytes accessed | tf_op | source)
XLA Modules:
  0.0 102.8 jit_solution(7480451727735013372)
XLA Ops:
  0.6 5.4 %group_by_view.1 = bf16[1024,1024]{1,0:T(8,128)(2,1)} custom-call(s32[1,1024]{1,0:T(1,128)} %bitcast.18, bf16[1024,1024]{1,0:T(8,128)(2,1)} %act_ref.2), custom_call_target="tpu_custom_call" | custom-call | flops 2147483648 | bytes 4194304 | tf_op jit(solution)/shard_map/group_by_view/pallas_call | solution.py:78
  6.0 7.4 %all-to-all-start = ((bf16[16,64,1024]{2,1,0:T(8,128)(2,1)}), bf16[16,64,1024]{2,1,0:T(8,128)(2,1)S(1)}, u32[]{:S(2)}, u32[]{:S(2)}) async-start(bf16[16,64,1024]{2,1,0:T(8,128)(2,1)} %bitcast.16), calls=%async_computation | async-start | bytes 4194304 | tf_op jit(solution)/shard_map/all_to_all | solution.py:445
  13.4 14.4 %fast_gradient.1 = (f32[128,3072]{1,0:T(8,128)}, bf16[128,3072]{1,0:T(8,128)(2,1)}) custom-call(s32[1]{0:T(128)} %bitcast.pos_ref, bf16[1024,1024]{1,0:T(8,128)(2,1)} %act_ref.2, bf16[1024,3072]{1,0:T(8,128)(2,1)} %wv_ref.9, bf16[1024,3072]{1,0:T(8,128)(2,1)} %wv_ref.9, bf16[4,1024]{1,0:T(4,128)(2,1)} %bitcast.17, f32[256,3,4,256]{3,2,1,0:T(4,128)} %fast_ref.1), custom_call_target="tpu_custom_call" | custom-call | flops 7516192768 | bytes 10223616 | tf_op jit(solution)/shard_map/fast_gradient/pallas_call | solution.py:169
  27.9 0.0 copy-start.4
  27.9 0.5 collective-permute-start
  28.3 2.1 %collective-permute-done.got_ref = bf16[128,3072]{1,0:T(8,128)(2,1)S(1)} collective-permute-done((bf16[128,3072]{1,0:T(8,128)(2,1)}, bf16[128,3072]{1,0:T(8,128)(2,1)S(1)}, u32[]{:S(2)}, u32[]{:S(2)}) %collective-permute-start) | collective-permute-done | bytes 786464 | tf_op jit(solution)/shard_map/ppermute | solution.py:442
  30.5 0.0 copy-start
  30.5 1.4 %copy-done = f32[128,3072]{1,0:T(8,128)S(1)} copy-done((f32[128,3072]{1,0:T(8,128)S(1)}, f32[128,3072]{1,0:T(8,128)}, u32[]{:S(2)}) %copy-start) | copy-done | bytes 1572888
  31.9 0.1 add_and_halve.3
  32.0 2.0 %collective-permute-start.1 = (bf16[64,3072]{1,0:T(8,128)(2,1)S(1)}, bf16[64,3072]{1,0:T(8,128)(2,1)S(1)}, u32[]{:S(2)}, u32[]{:S(2)}) collective-permute-start(bf16[64,3072]{1,0:T(8,128)(2,1)S(1)} %get-tuple-element.33), channel_id=1, source_target_pairs={{0,2},{1,3},{2,0},{3,1},{4,6},{5,7},{6,4},{7,5},{8,10},{9,11},{10,... | collective-permute-start | bytes 1179656 | tf_op jit(solution)/shard_map/ppermute | solution.py:442
  34.0 14.3 %collective-permute-done.1.got_ref = bf16[64,3072]{1,0:T(8,128)(2,1)S(1)} collective-permute-done((bf16[64,3072]{1,0:T(8,128)(2,1)S(1)}, bf16[64,3072]{1,0:T(8,128)(2,1)S(1)}, u32[]{:S(2)}, u32[]{:S(2)}) %collective-permute-start.1) | collective-permute-done | bytes 393248 | tf_op jit(solution)/shard_map/ppermute | solution.py:442
  48.3 0.1 add_and_halve.4
  48.3 4.3 %collective-permute-start.2 = (bf16[32,3072]{1,0:T(8,128)(2,1)S(1)}, bf16[32,3072]{1,0:T(8,128)(2,1)S(1)}, u32[]{:S(2)}, u32[]{:S(2)}) collective-permute-start(bf16[32,3072]{1,0:T(8,128)(2,1)S(1)} %get-tuple-element.35), channel_id=1, source_target_pairs={{0,4},{1,5},{2,6},{3,7},{4,0},{5,1},{6,2},{7,3},{8,12},{9,13},{10,... | collective-permute-start | bytes 589832 | tf_op jit(solution)/shard_map/ppermute | solution.py:442
  52.7 0.0 copy-done.4
  52.7 0.2 reduce-window.9
  52.8 0.9 constant_dynamic-slice_fusion.start_ref
  53.8 7.4 %collective-permute-done.2.got_ref = bf16[32,3072]{1,0:T(8,128)(2,1)S(1)} collective-permute-done((bf16[32,3072]{1,0:T(8,128)(2,1)S(1)}, bf16[32,3072]{1,0:T(8,128)(2,1)S(1)}, u32[]{:S(2)}, u32[]{:S(2)}) %collective-permute-start.2) | collective-permute-done | bytes 196640 | tf_op jit(solution)/shard_map/ppermute | solution.py:442
  61.2 3.2 %collective-permute-start.3 = (bf16[16,3072]{1,0:T(8,128)(2,1)S(1)}, bf16[16,3072]{1,0:T(8,128)(2,1)S(1)}, u32[]{:S(2)}, u32[]{:S(2)}) collective-permute-start(bf16[16,3072]{1,0:T(8,128)(2,1)S(1)} %get-tuple-element.37), channel_id=1, source_target_pairs={{0,8},{1,9},{2,10},{3,11},{4,12},{5,13},{6,14},{7,15},{8,0},{9,1},... | collective-permute-start | bytes 294920 | tf_op jit(solution)/shard_map/ppermute | solution.py:442
  64.4 0.0 all-to-all-done
  64.4 0.0 copy-start.1
  64.4 5.8 %project_and_attend.4 = (bf16[1024,256]{1,0:T(8,128)(2,1)S(1)}, f32[1024,256]{1,0:T(8,128)S(1)}) custom-call(s32[3]{0:T(128)S(1)} %bitcast.12, bf16[1024,1024]{1,0:T(8,128)(2,1)S(1)} %bitcast.8, bf16[1024,3072]{1,0:T(8,128)(2,1)} %wv_ref.9, bf16[1024,3072]{1,0:T(8,128)(2,1)} %wv_ref.9, bf16[1024,3072]{1,0:T(8,128)(2,1)} %wv_ref.9), custom_call_target="tpu_custom_call" | custom-call | flops 2684354560 | bytes 5242880 | tf_op jit(solution)/shard_map/project_and_attend/pallas_call | solution.py:319
  70.3 0.0 collective-permute-done.3.got_ref
  70.3 0.0 copy-done.1
  70.3 1.0 update_rows.1
  71.3 0.0 collective-permute-start.4
  71.3 5.9 %project_and_attend.5 = (bf16[1024,256]{1,0:T(8,128)(2,1)S(1)}, f32[1024,256]{1,0:T(8,128)S(1)}) custom-call(s32[3]{0:T(128)S(1)} %bitcast.13, bf16[1024,1024]{1,0:T(8,128)(2,1)S(1)} %bitcast.9, bf16[1024,3072]{1,0:T(8,128)(2,1)} %wv_ref.9, bf16[1024,3072]{1,0:T(8,128)(2,1)} %wv_ref.9, bf16[1024,3072]{1,0:T(8,128)(2,1)} %wv_ref.9), custom_call_target="tpu_custom_call" | custom-call | flops 2684354560 | bytes 5242880 | tf_op jit(solution)/shard_map/project_and_attend/pallas_call | solution.py:319
  77.2 0.2 collective-permute-done.4.second_ref
  77.4 2.4 %collective-permute-start.5 = (bf16[32,3072]{1,0:T(8,128)(2,1)S(1)}, bf16[32,3072]{1,0:T(8,128)(2,1)S(1)}, u32[]{:S(2)}, u32[]{:S(2)}) collective-permute-start(bf16[32,3072]{1,0:T(8,128)(2,1)S(1)} %join.2.first_ref), channel_id=1, source_target_pairs={{0,4},{1,5},{2,6},{3,7},{4,0},{5,1},{6,2},{7,3},{8,12},{9,13},{10,... | collective-permute-start | bytes 589832 | tf_op jit(solution)/shard_map/ppermute | solution.py:442
  79.7 6.1 %project_and_attend.6 = (bf16[1024,256]{1,0:T(8,128)(2,1)S(1)}, f32[1024,256]{1,0:T(8,128)S(1)}) custom-call(s32[3]{0:T(128)S(1)} %bitcast.14, bf16[1024,1024]{1,0:T(8,128)(2,1)S(1)} %bitcast.10, bf16[1024,3072]{1,0:T(8,128)(2,1)} %wv_ref.9, bf16[1024,3072]{1,0:T(8,128)(2,1)} %wv_ref.9, bf16[1024,3072]{1,0:T(8,128)(2,1)} %wv_ref.9), custom_call_target="tpu_custom_call" | custom-call | flops 2684354560 | bytes 5242880 | tf_op jit(solution)/shard_map/project_and_attend/pallas_call | solution.py:319
  85.8 0.0 collective-permute-done.5.second_ref
  85.9 0.0 copy-start.2
  85.9 0.0 copy-start.3
  85.9 0.1 collective-permute-start.6
  86.0 0.1 collective-permute-start.7
  86.0 5.9 %project_and_attend.7 = (bf16[1024,256]{1,0:T(8,128)(2,1)S(1)}, f32[1024,256]{1,0:T(8,128)S(1)}) custom-call(s32[3]{0:T(128)S(1)} %bitcast.15, bf16[1024,1024]{1,0:T(8,128)(2,1)S(1)} %bitcast.11, bf16[1024,3072]{1,0:T(8,128)(2,1)} %wv_ref.9, bf16[1024,3072]{1,0:T(8,128)(2,1)} %wv_ref.9, bf16[1024,3072]{1,0:T(8,128)(2,1)} %wv_ref.9), custom_call_target="tpu_custom_call" | custom-call | flops 2684354560 | bytes 5242880 | tf_op jit(solution)/shard_map/project_and_attend/pallas_call | solution.py:319
  91.9 3.4 %collective-permute-done.6.refs_1_ = bf16[64,3072]{1,0:T(8,128)(2,1)S(1)} collective-permute-done((bf16[64,3072]{1,0:T(8,128)(2,1)S(1)}, bf16[64,3072]{1,0:T(8,128)(2,1)S(1)}, u32[]{:S(2)}, u32[]{:S(2)}) %collective-permute-start.6) | collective-permute-done | bytes 393248 | tf_op jit(solution)/shard_map/ppermute | solution.py:442
  95.3 0.0 collective-permute-start.8
  95.3 0.0 collective-permute-done.7.refs_2_
  95.3 1.7 %collective-permute-done.8.refs_3_ = bf16[64,3072]{1,0:T(8,128)(2,1)S(1)} collective-permute-done((bf16[64,3072]{1,0:T(8,128)(2,1)S(1)}, bf16[64,3072]{1,0:T(8,128)(2,1)S(1)}, u32[]{:S(2)}, u32[]{:S(2)}) %collective-permute-start.8) | collective-permute-done | bytes 393248 | tf_op jit(solution)/shard_map/ppermute | solution.py:442
  97.0 0.0 copy-done.2
  97.0 0.0 copy-done.3
  97.0 5.8 %apply_fast.1 = bf16[1024,1024]{1,0:T(8,128)(2,1)} custom-call(s32[1]{0:T(128)} %bitcast.pos_ref, bf16[64,3072]{1,0:T(8,128)(2,1)S(1)} %join.3.refs_0_, bf16[64,3072]{1,0:T(8,128)(2,1)S(1)} %collective-permute-done.6.refs_1_, bf16[64,3072]{1,0:T(8,128)(2,1)S(1)} %collective-permute-done.7.refs_2_, bf16[64,3072]{1,0:T(8,128)(2,1)S(1)} %collective-permute-done.8.refs_3_, ...), custom_call_target="tpu_custom_call" | custom-call | flops 3758096384 | bytes 12058624 | tf_op jit(solution)/shard_map/apply_fast/pallas_call | solution.py:394
  (3 shorter events, 0.1 us)
Async XLA Ops:
  6.0 58.4 %all-to-all-start = ((bf16[16,64,1024]{2,1,0:T(8,128)(2,1)}), bf16[16,64,1024]{2,1,0:T(8,128)(2,1)S(1)}, u32[]{:S(2)}, u32[]{:S(2)}) async-start(bf16[16,64,1024]{2,1,0:T(8,128)(2,1)} %bitcast.16), calls=%async_computation | async-start | bytes 4194304 | tf_op jit(solution)/shard_map/all_to_all | solution.py:445
  27.9 24.8 %copy-start.4 = (s32[1,3]{1,0:T(1,128)S(1)}, s32[1,3]{1,0:T(1,128)}, u32[]{:S(2)}) copy-start(s32[1,3]{1,0:T(1,128)} %param.11) | copy-start | bytes 40
  27.9 2.6 %collective-permute-start = (bf16[128,3072]{1,0:T(8,128)(2,1)}, bf16[128,3072]{1,0:T(8,128)(2,1)S(1)}, u32[]{:S(2)}, u32[]{:S(2)}) collective-permute-start(bf16[128,3072]{1,0:T(8,128)(2,1)} %get-tuple-element.31), channel_id=1, source_target_pairs={{0,1},{1,0},{2,3},{3,2},{4,5},{5,4},{6,7},{7,6},{8,9},{9,8},{10,11... | collective-permute-start | bytes 2359304 | tf_op jit(solution)/shard_map/ppermute | solution.py:442
  30.5 1.4 %copy-start = (f32[128,3072]{1,0:T(8,128)S(1)}, f32[128,3072]{1,0:T(8,128)}, u32[]{:S(2)}) copy-start(f32[128,3072]{1,0:T(8,128)} %get-tuple-element.30.keep_ref) | copy-start | bytes 4718596
  32.0 16.3 %collective-permute-start.1 = (bf16[64,3072]{1,0:T(8,128)(2,1)S(1)}, bf16[64,3072]{1,0:T(8,128)(2,1)S(1)}, u32[]{:S(2)}, u32[]{:S(2)}) collective-permute-start(bf16[64,3072]{1,0:T(8,128)(2,1)S(1)} %get-tuple-element.33), channel_id=1, source_target_pairs={{0,2},{1,3},{2,0},{3,1},{4,6},{5,7},{6,4},{7,5},{8,10},{9,11},{10,... | collective-permute-start | bytes 1179656 | tf_op jit(solution)/shard_map/ppermute | solution.py:442
  48.3 12.8 %collective-permute-start.2 = (bf16[32,3072]{1,0:T(8,128)(2,1)S(1)}, bf16[32,3072]{1,0:T(8,128)(2,1)S(1)}, u32[]{:S(2)}, u32[]{:S(2)}) collective-permute-start(bf16[32,3072]{1,0:T(8,128)(2,1)S(1)} %get-tuple-element.35), channel_id=1, source_target_pairs={{0,4},{1,5},{2,6},{3,7},{4,0},{5,1},{6,2},{7,3},{8,12},{9,13},{10,... | collective-permute-start | bytes 589832 | tf_op jit(solution)/shard_map/ppermute | solution.py:442
  61.2 9.1 %collective-permute-start.3 = (bf16[16,3072]{1,0:T(8,128)(2,1)S(1)}, bf16[16,3072]{1,0:T(8,128)(2,1)S(1)}, u32[]{:S(2)}, u32[]{:S(2)}) collective-permute-start(bf16[16,3072]{1,0:T(8,128)(2,1)S(1)} %get-tuple-element.37), channel_id=1, source_target_pairs={{0,8},{1,9},{2,10},{3,11},{4,12},{5,13},{6,14},{7,15},{8,0},{9,1},... | collective-permute-start | bytes 294920 | tf_op jit(solution)/shard_map/ppermute | solution.py:442
  64.4 5.9 %copy-start.1 = (f32[16,3,4,256]{3,2,1,0:T(4,128)S(1)}, f32[16,3,4,256]{3,2,1,0:T(4,128)}, u32[]{:S(2)}) copy-start(f32[16,3,4,256]{3,2,1,0:T(4,128)} %mom_ref.1) | copy-start | bytes 589828
  71.3 6.1 %collective-permute-start.4 = (bf16[16,3072]{1,0:T(8,128)(2,1)S(1)}, bf16[16,3072]{1,0:T(8,128)(2,1)S(1)}, u32[]{:S(2)}, u32[]{:S(2)}) collective-permute-start(bf16[16,3072]{1,0:T(8,128)(2,1)S(1)} %get-tuple-element.41.first_ref), channel_id=1, source_target_pairs={{0,8},{1,9},{2,10},{3,11},{4,12},{5,13},{6,14},{7,15},{8,0},{9,1},... | collective-permute-start | bytes 294920 | tf_op jit(solution)/shard_map/ppermute | solution.py:442
  77.4 8.4 %collective-permute-start.5 = (bf16[32,3072]{1,0:T(8,128)(2,1)S(1)}, bf16[32,3072]{1,0:T(8,128)(2,1)S(1)}, u32[]{:S(2)}, u32[]{:S(2)}) collective-permute-start(bf16[32,3072]{1,0:T(8,128)(2,1)S(1)} %join.2.first_ref), channel_id=1, source_target_pairs={{0,4},{1,5},{2,6},{3,7},{4,0},{5,1},{6,2},{7,3},{8,12},{9,13},{10,... | collective-permute-start | bytes 589832 | tf_op jit(solution)/shard_map/ppermute | solution.py:442
  85.9 11.1 %copy-start.2 = (bf16[1024,1024]{1,0:T(8,128)(2,1)S(1)}, bf16[1024,1024]{1,0:T(8,128)(2,1)}, u32[]{:S(2)}) copy-start(bf16[1024,1024]{1,0:T(8,128)(2,1)} %refs_13_.1) | copy-start | bytes 6291460
  85.9 11.1 %copy-start.3 = (f32[4,256]{1,0:T(4,128)S(1)}, f32[4,256]{1,0:T(4,128)}, u32[]{:S(2)}) copy-start(f32[4,256]{1,0:T(4,128)} %refs_12_.1) | copy-start | bytes 12292
  85.9 9.4 %collective-permute-start.6 = (bf16[64,3072]{1,0:T(8,128)(2,1)S(1)}, bf16[64,3072]{1,0:T(8,128)(2,1)S(1)}, u32[]{:S(2)}, u32[]{:S(2)}) collective-permute-start(bf16[64,3072]{1,0:T(8,128)(2,1)S(1)} %join.3.refs_0_), channel_id=1, source_target_pairs={{0,2},{1,3},{2,0},{3,1},{4,6},{5,7},{6,4},{7,5},{8,10},{9,11},{10,... | collective-permute-start | bytes 1179656 | tf_op jit(solution)/shard_map/ppermute | solution.py:442
  86.0 9.3 %collective-permute-start.7 = (bf16[64,3072]{1,0:T(8,128)(2,1)S(1)}, bf16[64,3072]{1,0:T(8,128)(2,1)S(1)}, u32[]{:S(2)}, u32[]{:S(2)}) collective-permute-start(bf16[64,3072]{1,0:T(8,128)(2,1)S(1)} %join.3.refs_0_), channel_id=1, source_target_pairs={{0,1},{1,0},{2,3},{3,2},{4,5},{5,4},{6,7},{7,6},{8,9},{9,8},{10,11... | collective-permute-start | bytes 1179656 | tf_op jit(solution)/shard_map/ppermute | solution.py:442
  95.3 1.7 %collective-permute-start.8 = (bf16[64,3072]{1,0:T(8,128)(2,1)S(1)}, bf16[64,3072]{1,0:T(8,128)(2,1)S(1)}, u32[]{:S(2)}, u32[]{:S(2)}) collective-permute-start(bf16[64,3072]{1,0:T(8,128)(2,1)S(1)} %collective-permute-done.6.refs_1_), channel_id=1, source_target_pairs={{0,1},{1,0},{2,3},{3,2},{4,5},{5,4},{6,7},{7,6},{8,9},{9,8},{10,11... | collective-permute-start | bytes 1179656 | tf_op jit(solution)/shard_map/ppermute | solution.py:442

commit v5 on v4

--- a/solution.py
+++ b/solution.py
@@ -284,18 +284,39 @@
     )(keep, received, momentum, own_start)
 
 
-def project_and_attend(window_ends, arrived, project_weight, heads, first, count):
+def head_weights(project_weight, heads, head):
+    width, columns = project_weight.shape
+    kinds = 3
+    size = columns // kinds // heads
+
+    def kernel(in_ref, out_ref):
+        out_ref[...] = in_ref[...]
+
+    return pl.pallas_call(
+        kernel,
+        grid=(kinds,),
+        in_specs=[pl.BlockSpec((width, size), lambda kind: (0, kind * heads + head))],
+        out_specs=pl.BlockSpec((width, size), lambda kind: (0, kind)),
+        out_shape=jax.ShapeDtypeStruct((width, kinds * size), BF16),
+        compiler_params=params(8),
+        cost_estimate=cost(0, 4 * width * kinds * size),
+        name="head_weights",
+    )(project_weight)
+
+
+def project_and_attend(window_ends, arrived, weights):
     tok_dev, width = arrived.shape
-    size = width // heads
+    size = weights.shape[1] // 3
+    count = 1
     windows = window_ends.shape[0]
     tile = 512
-    scale = 1.0 / math.sqrt(size)
-
-    def kernel(ends_ref, x_ref, wq_ref, wk_ref, wv_ref, unit_ref, att_ref):
+    scale = math.log2(math.e) / math.sqrt(size)
+
+    def kernel(ends_ref, x_ref, weight_ref, unit_ref, att_ref):
         x = x_ref[...]
-        queries = dot(x, wq_ref[...]).astype(BF16)
-        keys = dot(x, wk_ref[...]).astype(BF16)
-        values = dot(x, wv_ref[...]).astype(BF16)
+        queries = dot(x, weight_ref[:, 0:size]).astype(BF16)
+        keys = dot(x, weight_ref[:, size : 2 * size]).astype(BF16)
+        values = dot(x, weight_ref[:, 2 * size : 3 * size]).astype(BF16)
         wide = queries.astype(F32)
         unit_ref[...] = (
             wide * lax.rsqrt(jnp.mean(wide * wide, axis=-1, keepdims=True) + 1e-06)
@@ -309,12 +330,14 @@
             window = jnp.zeros((tile, 1), jnp.int32)
             for w in range(windows):
                 window += (place >= ends_ref[w]).astype(jnp.int32)
-            scores = dot_nt(queries[start : start + tile], keys) * scale
+            scores = dot_nt(queries[start : start + tile], keys)
             scores = jnp.where(window == key_window, scores, -1e30)
             highest = jnp.max(scores, axis=-1, keepdims=True)
-            expo = jnp.exp(scores - highest)
+            expo = jnp.exp2((scores - highest) * scale)
             total = jnp.sum(expo, axis=-1, keepdims=True)
-            att_ref[start : start + tile, :] = dot(expo.astype(BF16), values) / total
+            att_ref[start : start + tile, :] = dot(expo.astype(BF16), values) * (
+                1.0 / total
+            )
 
     return pl.pallas_call(
         kernel,
@@ -323,9 +346,7 @@
             grid=(count,),
             in_specs=[
                 pl.BlockSpec((tok_dev, width), lambda h, e: (0, 0)),
-                pl.BlockSpec((width, size), lambda h, e: (0, first + h)),
-                pl.BlockSpec((width, size), lambda h, e: (0, heads + first + h)),
-                pl.BlockSpec((width, size), lambda h, e: (0, 2 * heads + first + h)),
+                pl.BlockSpec((width, 3 * size), lambda h, e: (0, 0)),
             ],
             out_specs=[
                 pl.BlockSpec((tok_dev, size), lambda h, e: (0, h)),
@@ -336,14 +357,14 @@
             jax.ShapeDtypeStruct((tok_dev, count * size), BF16),
             jax.ShapeDtypeStruct((tok_dev, count * size), F32),
         ],
-        compiler_params=params(50),
+        compiler_params=params(34),
         cost_estimate=cost(
             2 * tok_dev * count * size * (3 * width + 2 * tok_dev),
             2 * tok_dev * width + 6 * tok_dev * count * size + 6 * width * count * size,
             count * tok_dev * tok_dev,
         ),
         name="project_and_attend",
-    )(window_ends, arrived, project_weight, project_weight, project_weight)
+    )(window_ends, arrived, weights)
 
 
 def apply_fast(position, gathered, units, attends, norm_gain, output_weight, shards):
@@ -455,34 +476,42 @@
     bit = 1
     while bit < shards:
         received = swap(send, bit)
+        if bit == 2:
+            source = after(project_weight, send)
+            held = [head_weights(source, heads, head) for head in range(heads)]
+            received = after(received, *held)
         if bit == 8:
-            unit, attended = project_and_attend(ends, after(arrived, send), project_weight, heads, 0, 1)
+            unit, attended = project_and_attend(ends, after(arrived, send), held[0])
             units.append(unit)
             attends.append(attended)
-            done = 1
             received = after(received, attended)
         bit *= 2
         if bit < shards:
             keep, send = add_and_halve(keep, received)
     momentum_next, block = update_rows(keep, received, momentum, own_start)
 
-    stages = shards.bit_length() - 1
-    bit = shards // 2
-    for stage in range(stages - 1):
-        last = stage == stages - 2
-        count = heads - done if last else min(1, heads - done)
-        if count:
-            unit, attended = project_and_attend(
-                ends, after(arrived, block), project_weight, heads, done, count
-            )
+    def attend(count, *others):
+        first = len(units)
+        for head in range(first, min(first + count, heads)):
+            unit, attended = project_and_attend(ends, after(arrived, *others), held[head])
             units.append(unit)
             attends.append(attended)
-            done += count
-        other = swap(block, bit)
-        if not last:
-            block = join(block, after(other, attends[-1]))
-            bit //= 2
-    gathered = [block, other, swap(block, 1), swap(after(other, attends[-1]), 1)]
+
+    bit = shards // 2
+    while bit > 4:
+        attend(1, block)
+        block = join(block, after(swap(block, bit), attends[-1]))
+        bit //= 2
+    attend(1, block)
+    own = {0: block, 4: swap(block, 4), 2: swap(block, 2)}
+    other = {0: swap(block, 1)}
+    last = after(own[4], attends[-1])
+    own[6] = swap(last, 2)
+    other[4] = swap(last, 1)
+    other[2] = swap(after(own[2], attends[-1]), 1)
+    attend(heads, last)
+    other[6] = swap(after(own[6], attends[-1]), 1)
+    gathered = [side[place] for side in (own, other) for place in (0, 4, 2, 6)]
     mixed = apply_fast(position, gathered, units, attends, norm_gain, output_weight, shards)
     return (mixed[None], momentum_next)
 

time: 103 us -> 99.3 us (0.964)
  waiting for transfers between devices: 29.1 us -> 17.8 us
  local copies, waits for them, and re-layouts: 2.37 us -> 11.2 us
  Pallas kernels: 50.5 us -> 47 us
  starting transfers between devices: 19.9 us -> 21.9 us
    ppermute x9 -> x12, waiting for transfers between devices: 29.1 us -> 17.8 us  [swap(): return lax.ppermute(array, 'tok', [(i, i ^ bit) for i in range(shards)])]
    unnamed x10 -> x28, local copies, waits for them, and re-layouts: 1.43 us -> 10.3 us
    pallas_call x4, Pallas kernels: 23.6 us -> 18 us  [project_and_attend(): pl.pallas_call(kernel, grid_spec=pltpu.PrefetchScalarGridSpec(num_scalar_...]
    pallas_call x0 -> x4, Pallas kernels: none -> 2.14 us  [head_weights(): pl.pallas_call(kernel, grid=(kinds,), in_specs=[pl.BlockSpec((width, size...]
    ppermute x9 -> x12, starting transfers between devices: 12.5 us -> 14.5 us  [swap(): return lax.ppermute(array, 'tok', [(i, i ^ bit) for i in range(shards)])]
  transfers between devices with their start and end apart: 10 -> 13, of which waited for: 6 -> 6; matrix products, arithmetic and copies ran while one was open for 1% -> 1% of each run, Pallas kernels for 37% -> 35%
where the time goes in v5:
time: 99.3 us; the launch traced here: 98.9 us
  Pallas kernels  47 us (47%)
  starting transfers between devices  21.9 us (22%)
  waiting for transfers between devices  17.8 us (18%)
  local copies, waits for them, and re-layouts  11.2 us (11%)
    pallas_call x4, Pallas kernels, project_and_attend(): pl.pallas_call(kernel, grid_spec=pltpu.PrefetchScalarGridSpec(num_scalar_...  18 us
    ppermute x12, waiting for transfers between devices, swap(): return lax.ppermute(array, 'tok', [(i, i ^ bit) for i in range(shards)])  17.8 us
    ppermute x12, starting transfers between devices, swap(): return lax.ppermute(array, 'tok', [(i, i ^ bit) for i in range(shards)])  14.5 us
    pallas_call x1, Pallas kernels, fast_gradient(): pl.pallas_call(kernel, grid_spec=pltpu.PrefetchScalarGridSpec(num_scalar_...  14.4 us
    unnamed x28, local copies, waits for them, and re-layouts  10.3 us
    all_to_all x1, starting transfers between devices, body(): lax.all_to_all(sent.reshape(shards, tok_dev // shards, width), 'tok', spl...  7.39 us
    pallas_call x1, Pallas kernels, apply_fast(): pl.pallas_call(kernel, grid_spec=pltpu.PrefetchScalarGridSpec(num_scalar_...  5.76 us
    pallas_call x1, Pallas kernels, group_by_view(): pl.pallas_call(kernel, grid=(tok_dev // tile,), in_specs=[pl.BlockSpec((1...  5.41 us
  transfers between devices with their start and end apart: 13, of which 6 were waited for; matrix products, arithmetic and copies ran while one was open for 1% of the time, Pallas kernels for 35%

profile of v5, /device:TPU:0, one launch (start us, length us, event | category | flops | bytes accessed | tf_op | source)
XLA Modules:
  0.0 98.9 jit_solution(267019050842549859)
XLA Ops:
  0.6 5.4 %group_by_view.1 = bf16[1024,1024]{1,0:T(8,128)(2,1)} custom-call(s32[1,1024]{1,0:T(1,128)} %bitcast.18, bf16[1024,1024]{1,0:T(8,128)(2,1)} %act_ref.2), custom_call_target="tpu_custom_call" | custom-call | flops 2147483648 | bytes 4194304 | tf_op jit(solution)/shard_map/group_by_view/pallas_call | solution.py:78
  6.0 7.4 %all-to-all-start = ((bf16[16,64,1024]{2,1,0:T(8,128)(2,1)}), bf16[16,64,1024]{2,1,0:T(8,128)(2,1)S(1)}, u32[]{:S(2)}, u32[]{:S(2)}) async-start(bf16[16,64,1024]{2,1,0:T(8,128)(2,1)} %bitcast.16), calls=%async_computation | async-start | bytes 4194304 | tf_op jit(solution)/shard_map/all_to_all | solution.py:466
  13.4 14.4 %fast_gradient.1 = (f32[128,3072]{1,0:T(8,128)}, bf16[128,3072]{1,0:T(8,128)(2,1)}) custom-call(s32[1]{0:T(128)} %bitcast.pos_ref, bf16[1024,1024]{1,0:T(8,128)(2,1)} %act_ref.2, bf16[1024,3072]{1,0:T(8,128)(2,1)} %in_ref.3, bf16[1024,3072]{1,0:T(8,128)(2,1)} %in_ref.3, bf16[4,1024]{1,0:T(4,128)(2,1)} %bitcast.17, f32[256,3,4,256]{3,2,1,0:T(4,128)} %fast_ref.1), custom_call_target="tpu_custom_call" | custom-call | flops 7516192768 | bytes 10223616 | tf_op jit(solution)/shard_map/fast_gradient/pallas_call | solution.py:169
  27.9 0.5 collective-permute-start
  28.3 2.1 %collective-permute-done.got_ref = bf16[128,3072]{1,0:T(8,128)(2,1)S(1)} collective-permute-done((bf16[128,3072]{1,0:T(8,128)(2,1)}, bf16[128,3072]{1,0:T(8,128)(2,1)S(1)}, u32[]{:S(2)}, u32[]{:S(2)}) %collective-permute-start) | collective-permute-done | bytes 786464 | tf_op jit(solution)/shard_map/ppermute | solution.py:463
  30.4 0.0 copy-start.1
  30.4 1.4 %copy-done.1 = f32[128,3072]{1,0:T(8,128)S(1)} copy-done((f32[128,3072]{1,0:T(8,128)S(1)}, f32[128,3072]{1,0:T(8,128)}, u32[]{:S(2)}) %copy-start.1) | copy-done | bytes 1572888
  31.9 0.1 add_and_halve.3
  32.0 2.0 %collective-permute-start.1 = (bf16[64,3072]{1,0:T(8,128)(2,1)S(1)}, bf16[64,3072]{1,0:T(8,128)(2,1)S(1)}, u32[]{:S(2)}, u32[]{:S(2)}) collective-permute-start(bf16[64,3072]{1,0:T(8,128)(2,1)S(1)} %get-tuple-element.36), channel_id=1, source_target_pairs={{0,2},{1,3},{2,0},{3,1},{4,6},{5,7},{6,4},{7,5},{8,10},{9,11},{10,... | collective-permute-start | bytes 1179656 | tf_op jit(solution)/shard_map/ppermute | solution.py:463
  33.9 2.8 %copy-done = bf16[1024,3072]{1,0:T(8,128)(2,1)S(1)} copy-done((bf16[1024,3072]{1,0:T(8,128)(2,1)S(1)}, bf16[1024,3072]{1,0:T(8,128)(2,1)}, u32[]{:S(2)}) %copy-start) | copy-done | bytes 6291480
  36.7 0.5 head_weights.4.weight_ref
  37.2 0.0 copy-start.8
  37.2 1.2 %copy-done.8 = bf16[1024,768]{1,0:T(8,128)(2,1)} copy-done((bf16[1024,768]{1,0:T(8,128)(2,1)}, bf16[1024,768]{1,0:T(8,128)(2,1)S(1)}, u32[]{:S(2)}) %copy-start.8) | copy-done | bytes 1572888
  38.4 0.5 head_weights.5.weight_ref
  38.9 0.0 copy-start.6
  38.9 1.1 %copy-done.6 = bf16[1024,768]{1,0:T(8,128)(2,1)} copy-done((bf16[1024,768]{1,0:T(8,128)(2,1)}, bf16[1024,768]{1,0:T(8,128)(2,1)S(1)}, u32[]{:S(2)}) %copy-start.6) | copy-done | bytes 1572888
  40.1 0.5 head_weights.6.weight_ref
  40.6 0.0 copy-start.4
  40.6 1.1 %copy-done.4 = bf16[1024,768]{1,0:T(8,128)(2,1)} copy-done((bf16[1024,768]{1,0:T(8,128)(2,1)}, bf16[1024,768]{1,0:T(8,128)(2,1)S(1)}, u32[]{:S(2)}) %copy-start.4) | copy-done | bytes 1572888
  41.7 0.7 head_weights.7.weight_ref
  42.4 0.0 copy-start.2
  42.4 1.2 %copy-done.2 = bf16[1024,768]{1,0:T(8,128)(2,1)} copy-done((bf16[1024,768]{1,0:T(8,128)(2,1)}, bf16[1024,768]{1,0:T(8,128)(2,1)S(1)}, u32[]{:S(2)}) %copy-start.2) | copy-done | bytes 1572888
  43.6 4.6 %collective-permute-done.1.got_ref = bf16[64,3072]{1,0:T(8,128)(2,1)S(1)} collective-permute-done((bf16[64,3072]{1,0:T(8,128)(2,1)S(1)}, bf16[64,3072]{1,0:T(8,128)(2,1)S(1)}, u32[]{:S(2)}, u32[]{:S(2)}) %collective-permute-start.1) | collective-permute-done | bytes 393248 | tf_op jit(solution)/shard_map/ppermute | solution.py:463
  48.2 0.1 add_and_halve.4
  48.3 4.3 %collective-permute-start.2 = (bf16[32,3072]{1,0:T(8,128)(2,1)S(1)}, bf16[32,3072]{1,0:T(8,128)(2,1)S(1)}, u32[]{:S(2)}, u32[]{:S(2)}) collective-permute-start(bf16[32,3072]{1,0:T(8,128)(2,1)S(1)} %get-tuple-element.40), channel_id=1, source_target_pairs={{0,4},{1,5},{2,6},{3,7},{4,0},{5,1},{6,2},{7,3},{8,12},{9,13},{10,... | collective-permute-start | bytes 589832 | tf_op jit(solution)/shard_map/ppermute | solution.py:463
  52.6 0.0 copy-done.13
  52.6 0.2 reduce-window.9
  52.8 0.9 constant_dynamic-slice_fusion.start_ref
  53.7 7.4 %collective-permute-done.2.got_ref = bf16[32,3072]{1,0:T(8,128)(2,1)S(1)} collective-permute-done((bf16[32,3072]{1,0:T(8,128)(2,1)S(1)}, bf16[32,3072]{1,0:T(8,128)(2,1)S(1)}, u32[]{:S(2)}, u32[]{:S(2)}) %collective-permute-start.2) | collective-permute-done | bytes 196640 | tf_op jit(solution)/shard_map/ppermute | solution.py:463
  61.2 3.2 %collective-permute-start.3 = (bf16[16,3072]{1,0:T(8,128)(2,1)S(1)}, bf16[16,3072]{1,0:T(8,128)(2,1)S(1)}, u32[]{:S(2)}, u32[]{:S(2)}) collective-permute-start(bf16[16,3072]{1,0:T(8,128)(2,1)S(1)} %get-tuple-element.42), channel_id=1, source_target_pairs={{0,8},{1,9},{2,10},{3,11},{4,12},{5,13},{6,14},{7,15},{8,0},{9,1},... | collective-permute-start | bytes 294920 | tf_op jit(solution)/shard_map/ppermute | solution.py:463
  64.4 0.0 all-to-all-done
  64.4 1.4 %copy-done.9 = bf16[1024,768]{1,0:T(8,128)(2,1)S(1)} copy-done((bf16[1024,768]{1,0:T(8,128)(2,1)S(1)}, bf16[1024,768]{1,0:T(8,128)(2,1)}, u32[]{:S(2)}) %copy-start.9) | copy-done | bytes 1572888
  65.8 4.4 %project_and_attend.4 = (bf16[1024,256]{1,0:T(8,128)(2,1)S(1)}, f32[1024,256]{1,0:T(8,128)S(1)}) custom-call(s32[3]{0:T(128)S(1)} %bitcast.12, bf16[1024,1024]{1,0:T(8,128)(2,1)S(1)} %bitcast.8, bf16[1024,768]{1,0:T(8,128)(2,1)S(1)} %copy-done.9), custom_call_target="tpu_custom_call" | custom-call | flops 2684354560 | bytes 5242880 | tf_op jit(solution)/shard_map/project_and_attend/pallas_call | solution.py:342
  70.2 0.0 collective-permute-done.3.got_ref
  70.2 0.0 copy-done.10
  70.2 1.0 %update_rows.1 = (f32[16,3,4,256]{3,2,1,0:T(4,128)}, bf16[16,3072]{1,0:T(8,128)(2,1)S(1)}) custom-call(f32[16,3072]{1,0:T(8,128)S(1)} %get-tuple-element.41.keep_ref, bf16[16,3072]{1,0:T(8,128)(2,1)S(1)} %collective-permute-done.3.got_ref, f32[16,3,4,256]{3,2,1,0:T(4,128)S(1)} %copy-done.10, f32[16,3,4,256]{3,2,1,0:T(4,128)S(1)} %constant_dynamic-slice_fusion.start_ref), custom_call_target="tpu_custom_call" | custom-call | flops 393216 | bytes 983040 | tf_op jit(solution)/shard_map/update_rows/pallas_call | solution.py:273
  71.2 0.0 collective-permute-start.4
  71.3 0.0 copy-done.7
  71.3 4.5 %project_and_attend.5 = (bf16[1024,256]{1,0:T(8,128)(2,1)S(1)}, f32[1024,256]{1,0:T(8,128)S(1)}) custom-call(s32[3]{0:T(128)S(1)} %bitcast.13, bf16[1024,1024]{1,0:T(8,128)(2,1)S(1)} %bitcast.9, bf16[1024,768]{1,0:T(8,128)(2,1)S(1)} %copy-done.7), custom_call_target="tpu_custom_call" | custom-call | flops 2684354560 | bytes 5242880 | tf_op jit(solution)/shard_map/project_and_attend/pallas_call | solution.py:342
  75.7 1.6 %collective-permute-done.4.second_ref = bf16[16,3072]{1,0:T(8,128)(2,1)S(1)} collective-permute-done((bf16[16,3072]{1,0:T(8,128)(2,1)S(1)}, bf16[16,3072]{1,0:T(8,128)(2,1)S(1)}, u32[]{:S(2)}, u32[]{:S(2)}) %collective-permute-start.4) | collective-permute-done | bytes 98336 | tf_op jit(solution)/shard_map/ppermute | solution.py:463
  77.3 0.0 copy-start.3
  77.3 2.0 %collective-permute-start.5 = (bf16[32,3072]{1,0:T(8,128)(2,1)S(1)}, bf16[32,3072]{1,0:T(8,128)(2,1)S(1)}, u32[]{:S(2)}, u32[]{:S(2)}) collective-permute-start(bf16[32,3072]{1,0:T(8,128)(2,1)S(1)} %join.1.refs_0_), channel_id=1, source_target_pairs={{0,4},{1,5},{2,6},{3,7},{4,0},{5,1},{6,2},{7,3},{8,12},{9,13},{10,... | collective-permute-start | bytes 589832 | tf_op jit(solution)/shard_map/ppermute | solution.py:463
  79.3 0.0 collective-permute-start.6
  79.3 0.0 collective-permute-start.8
  79.3 0.0 copy-done.5
  79.3 4.7 %project_and_attend.6 = (bf16[1024,256]{1,0:T(8,128)(2,1)S(1)}, f32[1024,256]{1,0:T(8,128)S(1)}) custom-call(s32[3]{0:T(128)S(1)} %bitcast.14, bf16[1024,1024]{1,0:T(8,128)(2,1)S(1)} %bitcast.10, bf16[1024,768]{1,0:T(8,128)(2,1)S(1)} %copy-done.5), custom_call_target="tpu_custom_call" | custom-call | flops 2684354560 | bytes 5242880 | tf_op jit(solution)/shard_map/project_and_attend/pallas_call | solution.py:342
  84.0 0.0 collective-permute-done.5.refs_1_
  84.0 0.0 copy-start.11
  84.0 0.0 copy-start.12
  84.1 2.1 %collective-permute-start.7 = (bf16[32,3072]{1,0:T(8,128)(2,1)S(1)}, bf16[32,3072]{1,0:T(8,128)(2,1)S(1)}, u32[]{:S(2)}, u32[]{:S(2)}) collective-permute-start(bf16[32,3072]{1,0:T(8,128)(2,1)S(1)} %collective-permute-done.5.refs_1_), channel_id=1, source_target_pairs={{0,2},{1,3},{2,0},{3,1},{4,6},{5,7},{6,4},{7,5},{8,10},{9,11},{10,... | collective-permute-start | bytes 589832 | tf_op jit(solution)/shard_map/ppermute | solution.py:463
  86.1 0.2 collective-permute-start.9
  86.4 0.0 collective-permute-done.6.refs_2_
  86.4 0.3 collective-permute-start.10
  86.7 0.0 copy-done.3
  86.7 4.5 %project_and_attend.7 = (bf16[1024,256]{1,0:T(8,128)(2,1)S(1)}, f32[1024,256]{1,0:T(8,128)S(1)}) custom-call(s32[3]{0:T(128)S(1)} %bitcast.15, bf16[1024,1024]{1,0:T(8,128)(2,1)S(1)} %bitcast.11, bf16[1024,768]{1,0:T(8,128)(2,1)S(1)} %copy-done.3), custom_call_target="tpu_custom_call" | custom-call | flops 2684354560 | bytes 5242880 | tf_op jit(solution)/shard_map/project_and_attend/pallas_call | solution.py:342
  91.1 0.6 collective-permute-done.7.refs_3_
  91.7 0.0 collective-permute-start.11
  91.7 0.0 collective-permute-done.8.refs_4_
  91.7 0.0 collective-permute-done.10.refs_6_
  91.7 0.0 collective-permute-done.9.refs_5_
  91.7 1.4 %collective-permute-done.11.refs_7_ = bf16[32,3072]{1,0:T(8,128)(2,1)S(1)} collective-permute-done((bf16[32,3072]{1,0:T(8,128)(2,1)S(1)}, bf16[32,3072]{1,0:T(8,128)(2,1)S(1)}, u32[]{:S(2)}, u32[]{:S(2)}) %collective-permute-start.11) | collective-permute-done | bytes 196640 | tf_op jit(solution)/shard_map/ppermute | solution.py:463
  93.2 0.0 copy-done.11
  93.2 0.0 copy-done.12
  93.2 5.8 %apply_fast.1 = bf16[1024,1024]{1,0:T(8,128)(2,1)} custom-call(s32[1]{0:T(128)} %bitcast.pos_ref, bf16[32,3072]{1,0:T(8,128)(2,1)S(1)} %join.1.refs_0_, bf16[32,3072]{1,0:T(8,128)(2,1)S(1)} %collective-permute-done.5.refs_1_, bf16[32,3072]{1,0:T(8,128)(2,1)S(1)} %collective-permute-done.6.refs_2_, bf16[32,3072]{1,0:T(8,128)(2,1)S(1)} %collective-permute-done.7.refs_3_, ...), custom_call_target="tpu_custom_call" | custom-call | flops 3758096384 | bytes 12058624 | tf_op jit(solution)/shard_map/apply_fast/pallas_call | solution.py:415
  (8 shorter events, 0.1 us)
Async XLA Ops:
  6.0 58.3 %all-to-all-start = ((bf16[16,64,1024]{2,1,0:T(8,128)(2,1)}), bf16[16,64,1024]{2,1,0:T(8,128)(2,1)S(1)}, u32[]{:S(2)}, u32[]{:S(2)}) async-start(bf16[16,64,1024]{2,1,0:T(8,128)(2,1)} %bitcast.16), calls=%async_computation | async-start | bytes 4194304 | tf_op jit(solution)/shard_map/all_to_all | solution.py:466
  27.9 2.6 %collective-permute-start = (bf16[128,3072]{1,0:T(8,128)(2,1)}, bf16[128,3072]{1,0:T(8,128)(2,1)S(1)}, u32[]{:S(2)}, u32[]{:S(2)}) collective-permute-start(bf16[128,3072]{1,0:T(8,128)(2,1)} %get-tuple-element.34), channel_id=1, source_target_pairs={{0,1},{1,0},{2,3},{3,2},{4,5},{5,4},{6,7},{7,6},{8,9},{9,8},{10,11... | collective-permute-start | bytes 2359304 | tf_op jit(solution)/shard_map/ppermute | solution.py:463
  30.4 1.4 %copy-start.1 = (f32[128,3072]{1,0:T(8,128)S(1)}, f32[128,3072]{1,0:T(8,128)}, u32[]{:S(2)}) copy-start(f32[128,3072]{1,0:T(8,128)} %get-tuple-element.33.keep_ref) | copy-start | bytes 4718596
  32.0 16.3 %collective-permute-start.1 = (bf16[64,3072]{1,0:T(8,128)(2,1)S(1)}, bf16[64,3072]{1,0:T(8,128)(2,1)S(1)}, u32[]{:S(2)}, u32[]{:S(2)}) collective-permute-start(bf16[64,3072]{1,0:T(8,128)(2,1)S(1)} %get-tuple-element.36), channel_id=1, source_target_pairs={{0,2},{1,3},{2,0},{3,1},{4,6},{5,7},{6,4},{7,5},{8,10},{9,11},{10,... | collective-permute-start | bytes 1179656 | tf_op jit(solution)/shard_map/ppermute | solution.py:463
  33.9 2.8 %copy-start = (bf16[1024,3072]{1,0:T(8,128)(2,1)S(1)}, bf16[1024,3072]{1,0:T(8,128)(2,1)}, u32[]{:S(2)}) copy-start(bf16[1024,3072]{1,0:T(8,128)(2,1)} %in_ref.3) | copy-start | bytes 18874372
  37.2 1.2 %copy-start.8 = (bf16[1024,768]{1,0:T(8,128)(2,1)}, bf16[1024,768]{1,0:T(8,128)(2,1)S(1)}, u32[]{:S(2)}) copy-start(bf16[1024,768]{1,0:T(8,128)(2,1)S(1)} %head_weights.4.weight_ref) | copy-start | bytes 4718596
  38.9 1.2 %copy-start.6 = (bf16[1024,768]{1,0:T(8,128)(2,1)}, bf16[1024,768]{1,0:T(8,128)(2,1)S(1)}, u32[]{:S(2)}) copy-start(bf16[1024,768]{1,0:T(8,128)(2,1)S(1)} %head_weights.5.weight_ref) | copy-start | bytes 4718596
  40.6 1.2 %copy-start.4 = (bf16[1024,768]{1,0:T(8,128)(2,1)}, bf16[1024,768]{1,0:T(8,128)(2,1)S(1)}, u32[]{:S(2)}) copy-start(bf16[1024,768]{1,0:T(8,128)(2,1)S(1)} %head_weights.6.weight_ref) | copy-start | bytes 4718596
  41.7 10.9 %copy-start.13 = (s32[1,3]{1,0:T(1,128)S(1)}, s32[1,3]{1,0:T(1,128)}, u32[]{:S(2)}) copy-start(s32[1,3]{1,0:T(1,128)} %param.11) | copy-start | bytes 40
  42.4 1.2 %copy-start.2 = (bf16[1024,768]{1,0:T(8,128)(2,1)}, bf16[1024,768]{1,0:T(8,128)(2,1)S(1)}, u32[]{:S(2)}) copy-start(bf16[1024,768]{1,0:T(8,128)(2,1)S(1)} %head_weights.7.weight_ref) | copy-start | bytes 4718596
  48.3 12.8 %collective-permute-start.2 = (bf16[32,3072]{1,0:T(8,128)(2,1)S(1)}, bf16[32,3072]{1,0:T(8,128)(2,1)S(1)}, u32[]{:S(2)}, u32[]{:S(2)}) collective-permute-start(bf16[32,3072]{1,0:T(8,128)(2,1)S(1)} %get-tuple-element.40), channel_id=1, source_target_pairs={{0,4},{1,5},{2,6},{3,7},{4,0},{5,1},{6,2},{7,3},{8,12},{9,13},{10,... | collective-permute-start | bytes 589832 | tf_op jit(solution)/shard_map/ppermute | solution.py:463
  61.2 9.1 %collective-permute-start.3 = (bf16[16,3072]{1,0:T(8,128)(2,1)S(1)}, bf16[16,3072]{1,0:T(8,128)(2,1)S(1)}, u32[]{:S(2)}, u32[]{:S(2)}) collective-permute-start(bf16[16,3072]{1,0:T(8,128)(2,1)S(1)} %get-tuple-element.42), channel_id=1, source_target_pairs={{0,8},{1,9},{2,10},{3,11},{4,12},{5,13},{6,14},{7,15},{8,0},{9,1},... | collective-permute-start | bytes 294920 | tf_op jit(solution)/shard_map/ppermute | solution.py:463
  64.4 1.4 %copy-start.9 = (bf16[1024,768]{1,0:T(8,128)(2,1)S(1)}, bf16[1024,768]{1,0:T(8,128)(2,1)}, u32[]{:S(2)}) copy-start(bf16[1024,768]{1,0:T(8,128)(2,1)} %copy-done.8) | copy-start | bytes 4718596
  65.8 4.5 %copy-start.10 = (f32[16,3,4,256]{3,2,1,0:T(4,128)S(1)}, f32[16,3,4,256]{3,2,1,0:T(4,128)}, u32[]{:S(2)}) copy-start(f32[16,3,4,256]{3,2,1,0:T(4,128)} %mom_ref.1) | copy-start | bytes 589828
  65.8 5.5 %copy-start.7 = (bf16[1024,768]{1,0:T(8,128)(2,1)S(1)}, bf16[1024,768]{1,0:T(8,128)(2,1)}, u32[]{:S(2)}) copy-start(bf16[1024,768]{1,0:T(8,128)(2,1)} %copy-done.6) | copy-start | bytes 4718596
  71.2 8.1 %copy-start.5 = (bf16[1024,768]{1,0:T(8,128)(2,1)S(1)}, bf16[1024,768]{1,0:T(8,128)(2,1)}, u32[]{:S(2)}) copy-start(bf16[1024,768]{1,0:T(8,128)(2,1)} %copy-done.4) | copy-start | bytes 4718596
  71.2 6.1 %collective-permute-start.4 = (bf16[16,3072]{1,0:T(8,128)(2,1)S(1)}, bf16[16,3072]{1,0:T(8,128)(2,1)S(1)}, u32[]{:S(2)}, u32[]{:S(2)}) collective-permute-start(bf16[16,3072]{1,0:T(8,128)(2,1)S(1)} %get-tuple-element.46.first_ref), channel_id=1, source_target_pairs={{0,8},{1,9},{2,10},{3,11},{4,12},{5,13},{6,14},{7,15},{8,0},{9,1},... | collective-permute-start | bytes 294920 | tf_op jit(solution)/shard_map/ppermute | solution.py:463
  77.3 9.3 %copy-start.3 = (bf16[1024,768]{1,0:T(8,128)(2,1)S(1)}, bf16[1024,768]{1,0:T(8,128)(2,1)}, u32[]{:S(2)}) copy-start(bf16[1024,768]{1,0:T(8,128)(2,1)} %copy-done.2) | copy-start | bytes 4718596
  77.3 6.7 %collective-permute-start.5 = (bf16[32,3072]{1,0:T(8,128)(2,1)S(1)}, bf16[32,3072]{1,0:T(8,128)(2,1)S(1)}, u32[]{:S(2)}, u32[]{:S(2)}) collective-permute-start(bf16[32,3072]{1,0:T(8,128)(2,1)S(1)} %join.1.refs_0_), channel_id=1, source_target_pairs={{0,4},{1,5},{2,6},{3,7},{4,0},{5,1},{6,2},{7,3},{8,12},{9,13},{10,... | collective-permute-start | bytes 589832 | tf_op jit(solution)/shard_map/ppermute | solution.py:463
  79.3 7.0 %collective-permute-start.6 = (bf16[32,3072]{1,0:T(8,128)(2,1)S(1)}, bf16[32,3072]{1,0:T(8,128)(2,1)S(1)}, u32[]{:S(2)}, u32[]{:S(2)}) collective-permute-start(bf16[32,3072]{1,0:T(8,128)(2,1)S(1)} %join.1.refs_0_), channel_id=1, source_target_pairs={{0,2},{1,3},{2,0},{3,1},{4,6},{5,7},{6,4},{7,5},{8,10},{9,11},{10,... | collective-permute-start | bytes 589832 | tf_op jit(solution)/shard_map/ppermute | solution.py:463
  79.3 12.4 %collective-permute-start.8 = (bf16[32,3072]{1,0:T(8,128)(2,1)S(1)}, bf16[32,3072]{1,0:T(8,128)(2,1)S(1)}, u32[]{:S(2)}, u32[]{:S(2)}) collective-permute-start(bf16[32,3072]{1,0:T(8,128)(2,1)S(1)} %join.1.refs_0_), channel_id=1, source_target_pairs={{0,1},{1,0},{2,3},{3,2},{4,5},{5,4},{6,7},{7,6},{8,9},{9,8},{10,11... | collective-permute-start | bytes 589832 | tf_op jit(solution)/shard_map/ppermute | solution.py:463
  84.0 9.1 %copy-start.11 = (bf16[1024,1024]{1,0:T(8,128)(2,1)S(1)}, bf16[1024,1024]{1,0:T(8,128)(2,1)}, u32[]{:S(2)}) copy-start(bf16[1024,1024]{1,0:T(8,128)(2,1)} %refs_17_.1) | copy-start | bytes 6291460
  84.0 9.1 %copy-start.12 = (f32[4,256]{1,0:T(4,128)S(1)}, f32[4,256]{1,0:T(4,128)}, u32[]{:S(2)}) copy-start(f32[4,256]{1,0:T(4,128)} %refs_16_.1) | copy-start | bytes 12292
  84.1 7.7 %collective-permute-start.7 = (bf16[32,3072]{1,0:T(8,128)(2,1)S(1)}, bf16[32,3072]{1,0:T(8,128)(2,1)S(1)}, u32[]{:S(2)}, u32[]{:S(2)}) collective-permute-start(bf16[32,3072]{1,0:T(8,128)(2,1)S(1)} %collective-permute-done.5.refs_1_), channel_id=1, source_target_pairs={{0,2},{1,3},{2,0},{3,1},{4,6},{5,7},{6,4},{7,5},{8,10},{9,11},{10,... | collective-permute-start | bytes 589832 | tf_op jit(solution)/shard_map/ppermute | solution.py:463
  86.1 5.6 %collective-permute-start.9 = (bf16[32,3072]{1,0:T(8,128)(2,1)S(1)}, bf16[32,3072]{1,0:T(8,128)(2,1)S(1)}, u32[]{:S(2)}, u32[]{:S(2)}) collective-permute-start(bf16[32,3072]{1,0:T(8,128)(2,1)S(1)} %collective-permute-done.5.refs_1_), channel_id=1, source_target_pairs={{0,1},{1,0},{2,3},{3,2},{4,5},{5,4},{6,7},{7,6},{8,9},{9,8},{10,11... | collective-permute-start | bytes 589832 | tf_op jit(solution)/shard_map/ppermute | solution.py:463
  86.4 5.4 %collective-permute-start.10 = (bf16[32,3072]{1,0:T(8,128)(2,1)S(1)}, bf16[32,3072]{1,0:T(8,128)(2,1)S(1)}, u32[]{:S(2)}, u32[]{:S(2)}) collective-permute-start(bf16[32,3072]{1,0:T(8,128)(2,1)S(1)} %collective-permute-done.6.refs_2_), channel_id=1, source_target_pairs={{0,1},{1,0},{2,3},{3,2},{4,5},{5,4},{6,7},{7,6},{8,9},{9,8},{10,11... | collective-permute-start | bytes 589832 | tf_op jit(solution)/shard_map/ppermute | solution.py:463
  91.7 1.4 %collective-permute-start.11 = (bf16[32,3072]{1,0:T(8,128)(2,1)S(1)}, bf16[32,3072]{1,0:T(8,128)(2,1)S(1)}, u32[]{:S(2)}, u32[]{:S(2)}) collective-permute-start(bf16[32,3072]{1,0:T(8,128)(2,1)S(1)} %collective-permute-done.7.refs_3_), channel_id=1, source_target_pairs={{0,1},{1,0},{2,3},{3,2},{4,5},{5,4},{6,7},{7,6},{8,9},{9,8},{10,11... | collective-permute-start | bytes 589832 | tf_op jit(solution)/shard_map/ppermute | solution.py:463

commit v6 on v5

--- a/solution.py
+++ b/solution.py
@@ -478,8 +478,11 @@
         received = swap(send, bit)
         if bit == 2:
             source = after(project_weight, send)
-            held = [head_weights(source, heads, head) for head in range(heads)]
-            received = after(received, *held)
+            held = [None] + [head_weights(source, heads, head) for head in range(1, heads)]
+            received = after(received, *held[1:])
+        if bit == 4:
+            held[0] = head_weights(after(project_weight, send), heads, 0)
+            received = after(received, held[0])
         if bit == 8:
             unit, attended = project_and_attend(ends, after(arrived, send), held[0])
             units.append(unit)

time: 99.3 us -> 99.1 us (level)
  local copies, waits for them, and re-layouts: 11.2 us -> 14 us
  waiting for transfers between devices: 17.8 us -> 15 us
    ppermute x12, waiting for transfers between devices: 17.8 us -> 15 us  [swap(): return lax.ppermute(array, 'tok', [(i, i ^ bit) for i in range(shards)])]
    unnamed x28 -> x30, local copies, waits for them, and re-layouts: 10.3 us -> 13.1 us
where the time goes in v6:
time: 99.1 us; the launch traced here: 98.7 us
  Pallas kernels  46.8 us (47%)
  starting transfers between devices  21.9 us (22%)
  waiting for transfers between devices  15 us (15%)
  local copies, waits for them, and re-layouts  14 us (14%)
    pallas_call x4, Pallas kernels, project_and_attend(): pl.pallas_call(kernel, grid_spec=pltpu.PrefetchScalarGridSpec(num_scalar_...  17.8 us
    ppermute x12, waiting for transfers between devices, swap(): return lax.ppermute(array, 'tok', [(i, i ^ bit) for i in range(shards)])  15 us
    ppermute x12, starting transfers between devices, swap(): return lax.ppermute(array, 'tok', [(i, i ^ bit) for i in range(shards)])  14.5 us
    pallas_call x1, Pallas kernels, fast_gradient(): pl.pallas_call(kernel, grid_spec=pltpu.PrefetchScalarGridSpec(num_scalar_...  14.4 us
    unnamed x30, local copies, waits for them, and re-layouts  13.1 us
    all_to_all x1, starting transfers between devices, body(): lax.all_to_all(sent.reshape(shards, tok_dev // shards, width), 'tok', spl...  7.39 us
    pallas_call x1, Pallas kernels, apply_fast(): pl.pallas_call(kernel, grid_spec=pltpu.PrefetchScalarGridSpec(num_scalar_...  5.76 us
    pallas_call x1, Pallas kernels, group_by_view(): pl.pallas_call(kernel, grid=(tok_dev // tile,), in_specs=[pl.BlockSpec((1...  5.41 us
  transfers between devices with their start and end apart: 13, of which 6 were waited for; matrix products, arithmetic and copies ran while one was open for 1% of the time, Pallas kernels for 35%

profile of v6, /device:TPU:0, one launch (start us, length us, event | category | flops | bytes accessed | tf_op | source)
XLA Modules:
  0.0 98.7 jit_solution(17656777567192085540)
XLA Ops:
  0.6 5.4 %group_by_view.1 = bf16[1024,1024]{1,0:T(8,128)(2,1)} custom-call(s32[1,1024]{1,0:T(1,128)} %bitcast.18, bf16[1024,1024]{1,0:T(8,128)(2,1)} %act_ref.2), custom_call_target="tpu_custom_call" | custom-call | flops 2147483648 | bytes 4194304 | tf_op jit(solution)/shard_map/group_by_view/pallas_call | solution.py:78
  6.0 7.4 %all-to-all-start = ((bf16[16,64,1024]{2,1,0:T(8,128)(2,1)}), bf16[16,64,1024]{2,1,0:T(8,128)(2,1)S(1)}, u32[]{:S(2)}, u32[]{:S(2)}) async-start(bf16[16,64,1024]{2,1,0:T(8,128)(2,1)} %bitcast.16), calls=%async_computation | async-start | bytes 4194304 | tf_op jit(solution)/shard_map/all_to_all | solution.py:466
  13.4 14.4 %fast_gradient.1 = (f32[128,3072]{1,0:T(8,128)}, bf16[128,3072]{1,0:T(8,128)(2,1)}) custom-call(s32[1]{0:T(128)} %bitcast.pos_ref, bf16[1024,1024]{1,0:T(8,128)(2,1)} %act_ref.2, bf16[1024,3072]{1,0:T(8,128)(2,1)} %in_ref.3, bf16[1024,3072]{1,0:T(8,128)(2,1)} %in_ref.3, bf16[4,1024]{1,0:T(4,128)(2,1)} %bitcast.17, f32[256,3,4,256]{3,2,1,0:T(4,128)} %fast_ref.1), custom_call_target="tpu_custom_call" | custom-call | flops 7516192768 | bytes 10223616 | tf_op jit(solution)/shard_map/fast_gradient/pallas_call | solution.py:169
  27.9 0.5 collective-permute-start
  28.3 2.1 %collective-permute-done.got_ref = bf16[128,3072]{1,0:T(8,128)(2,1)S(1)} collective-permute-done((bf16[128,3072]{1,0:T(8,128)(2,1)}, bf16[128,3072]{1,0:T(8,128)(2,1)S(1)}, u32[]{:S(2)}, u32[]{:S(2)}) %collective-permute-start) | collective-permute-done | bytes 786464 | tf_op jit(solution)/shard_map/ppermute | solution.py:463
  30.5 1.4 %copy-done.2 = f32[128,3072]{1,0:T(8,128)S(1)} copy-done((f32[128,3072]{1,0:T(8,128)S(1)}, f32[128,3072]{1,0:T(8,128)}, u32[]{:S(2)}) %copy-start.2) | copy-done | bytes 1572888
  31.9 0.1 add_and_halve.3
  32.0 2.0 %collective-permute-start.1 = (bf16[64,3072]{1,0:T(8,128)(2,1)S(1)}, bf16[64,3072]{1,0:T(8,128)(2,1)S(1)}, u32[]{:S(2)}, u32[]{:S(2)}) collective-permute-start(bf16[64,3072]{1,0:T(8,128)(2,1)S(1)} %get-tuple-element.38), channel_id=1, source_target_pairs={{0,2},{1,3},{2,0},{3,1},{4,6},{5,7},{6,4},{7,5},{8,10},{9,11},{10,... | collective-permute-start | bytes 1179656 | tf_op jit(solution)/shard_map/ppermute | solution.py:463
  34.0 2.8 %copy-done = bf16[1024,3072]{1,0:T(8,128)(2,1)S(1)} copy-done((bf16[1024,3072]{1,0:T(8,128)(2,1)S(1)}, bf16[1024,3072]{1,0:T(8,128)(2,1)}, u32[]{:S(2)}) %copy-start) | copy-done | bytes 6291480
  36.7 0.5 head_weights.4.weight_ref
  37.2 0.0 copy-start.7
  37.2 1.2 %copy-done.7 = bf16[1024,768]{1,0:T(8,128)(2,1)} copy-done((bf16[1024,768]{1,0:T(8,128)(2,1)}, bf16[1024,768]{1,0:T(8,128)(2,1)S(1)}, u32[]{:S(2)}) %copy-start.7) | copy-done | bytes 1572888
  38.4 0.5 head_weights.5.weight_ref
  38.9 0.0 copy-start.5
  38.9 1.1 %copy-done.5 = bf16[1024,768]{1,0:T(8,128)(2,1)} copy-done((bf16[1024,768]{1,0:T(8,128)(2,1)}, bf16[1024,768]{1,0:T(8,128)(2,1)S(1)}, u32[]{:S(2)}) %copy-start.5) | copy-done | bytes 1572888
  40.1 0.5 head_weights.6.weight_ref
  40.6 0.0 copy-start.3
  40.6 1.1 %copy-done.3 = bf16[1024,768]{1,0:T(8,128)(2,1)} copy-done((bf16[1024,768]{1,0:T(8,128)(2,1)}, bf16[1024,768]{1,0:T(8,128)(2,1)S(1)}, u32[]{:S(2)}) %copy-start.3) | copy-done | bytes 1572888
  41.7 6.5 %collective-permute-done.1.got_ref = bf16[64,3072]{1,0:T(8,128)(2,1)S(1)} collective-permute-done((bf16[64,3072]{1,0:T(8,128)(2,1)S(1)}, bf16[64,3072]{1,0:T(8,128)(2,1)S(1)}, u32[]{:S(2)}, u32[]{:S(2)}) %collective-permute-start.1) | collective-permute-done | bytes 393248 | tf_op jit(solution)/shard_map/ppermute | solution.py:463
  48.3 0.1 add_and_halve.4
  48.3 4.3 %collective-permute-start.2 = (bf16[32,3072]{1,0:T(8,128)(2,1)S(1)}, bf16[32,3072]{1,0:T(8,128)(2,1)S(1)}, u32[]{:S(2)}, u32[]{:S(2)}) collective-permute-start(bf16[32,3072]{1,0:T(8,128)(2,1)S(1)} %get-tuple-element.42), channel_id=1, source_target_pairs={{0,4},{1,5},{2,6},{3,7},{4,0},{5,1},{6,2},{7,3},{8,12},{9,13},{10,... | collective-permute-start | bytes 589832 | tf_op jit(solution)/shard_map/ppermute | solution.py:463
  52.6 0.0 copy-done.14
  52.6 0.2 reduce-window.9
  52.8 0.9 constant_dynamic-slice_fusion.start_ref
  53.8 0.0 copy-start.1
  53.8 2.8 %copy-done.1 = bf16[1024,3072]{1,0:T(8,128)(2,1)S(1)} copy-done((bf16[1024,3072]{1,0:T(8,128)(2,1)S(1)}, bf16[1024,3072]{1,0:T(8,128)(2,1)}, u32[]{:S(2)}) %copy-start.1) | copy-done | bytes 6291480
  56.5 0.7 head_weights.7.weight_ref
  57.2 0.0 copy-start.9
  57.2 1.2 %copy-done.9 = bf16[1024,768]{1,0:T(8,128)(2,1)} copy-done((bf16[1024,768]{1,0:T(8,128)(2,1)}, bf16[1024,768]{1,0:T(8,128)(2,1)S(1)}, u32[]{:S(2)}) %copy-start.9) | copy-done | bytes 1572888
  58.4 2.7 %collective-permute-done.2.got_ref = bf16[32,3072]{1,0:T(8,128)(2,1)S(1)} collective-permute-done((bf16[32,3072]{1,0:T(8,128)(2,1)S(1)}, bf16[32,3072]{1,0:T(8,128)(2,1)S(1)}, u32[]{:S(2)}, u32[]{:S(2)}) %collective-permute-start.2) | collective-permute-done | bytes 196640 | tf_op jit(solution)/shard_map/ppermute | solution.py:463
  61.2 3.2 %collective-permute-start.3 = (bf16[16,3072]{1,0:T(8,128)(2,1)S(1)}, bf16[16,3072]{1,0:T(8,128)(2,1)S(1)}, u32[]{:S(2)}, u32[]{:S(2)}) collective-permute-start(bf16[16,3072]{1,0:T(8,128)(2,1)S(1)} %get-tuple-element.46), channel_id=1, source_target_pairs={{0,8},{1,9},{2,10},{3,11},{4,12},{5,13},{6,14},{7,15},{8,0},{9,1},... | collective-permute-start | bytes 294920 | tf_op jit(solution)/shard_map/ppermute | solution.py:463
  64.4 0.0 all-to-all-done
  64.4 1.4 %copy-done.10 = bf16[1024,768]{1,0:T(8,128)(2,1)S(1)} copy-done((bf16[1024,768]{1,0:T(8,128)(2,1)S(1)}, bf16[1024,768]{1,0:T(8,128)(2,1)}, u32[]{:S(2)}) %copy-start.10) | copy-done | bytes 1572888
  65.8 4.4 %project_and_attend.4 = (bf16[1024,256]{1,0:T(8,128)(2,1)S(1)}, f32[1024,256]{1,0:T(8,128)S(1)}) custom-call(s32[3]{0:T(128)S(1)} %bitcast.12, bf16[1024,1024]{1,0:T(8,128)(2,1)S(1)} %bitcast.8, bf16[1024,768]{1,0:T(8,128)(2,1)S(1)} %copy-done.10), custom_call_target="tpu_custom_call" | custom-call | flops 2684354560 | bytes 5242880 | tf_op jit(solution)/shard_map/project_and_attend/pallas_call | solution.py:342
  70.2 0.0 collective-permute-done.3.got_ref
  70.3 0.0 copy-done.11
  70.3 1.0 %update_rows.1 = (f32[16,3,4,256]{3,2,1,0:T(4,128)}, bf16[16,3072]{1,0:T(8,128)(2,1)S(1)}) custom-call(f32[16,3072]{1,0:T(8,128)S(1)} %get-tuple-element.45.keep_ref, bf16[16,3072]{1,0:T(8,128)(2,1)S(1)} %collective-permute-done.3.got_ref, f32[16,3,4,256]{3,2,1,0:T(4,128)S(1)} %copy-done.11, f32[16,3,4,256]{3,2,1,0:T(4,128)S(1)} %constant_dynamic-slice_fusion.start_ref), custom_call_target="tpu_custom_call" | custom-call | flops 393216 | bytes 983040 | tf_op jit(solution)/shard_map/update_rows/pallas_call | solution.py:273
  71.3 0.0 collective-permute-start.4
  71.3 0.0 copy-done.8
  71.3 4.5 %project_and_attend.5 = (bf16[1024,256]{1,0:T(8,128)(2,1)S(1)}, f32[1024,256]{1,0:T(8,128)S(1)}) custom-call(s32[3]{0:T(128)S(1)} %bitcast.13, bf16[1024,1024]{1,0:T(8,128)(2,1)S(1)} %bitcast.9, bf16[1024,768]{1,0:T(8,128)(2,1)S(1)} %copy-done.8), custom_call_target="tpu_custom_call" | custom-call | flops 2684354560 | bytes 5242880 | tf_op jit(solution)/shard_map/project_and_attend/pallas_call | solution.py:342
  75.7 1.6 %collective-permute-done.4.second_ref = bf16[16,3072]{1,0:T(8,128)(2,1)S(1)} collective-permute-done((bf16[16,3072]{1,0:T(8,128)(2,1)S(1)}, bf16[16,3072]{1,0:T(8,128)(2,1)S(1)}, u32[]{:S(2)}, u32[]{:S(2)}) %collective-permute-start.4) | collective-permute-done | bytes 98336 | tf_op jit(solution)/shard_map/ppermute | solution.py:463
  77.4 0.0 copy-start.4
  77.4 2.0 %collective-permute-start.5 = (bf16[32,3072]{1,0:T(8,128)(2,1)S(1)}, bf16[32,3072]{1,0:T(8,128)(2,1)S(1)}, u32[]{:S(2)}, u32[]{:S(2)}) collective-permute-start(bf16[32,3072]{1,0:T(8,128)(2,1)S(1)} %join.1.refs_0_), channel_id=1, source_target_pairs={{0,4},{1,5},{2,6},{3,7},{4,0},{5,1},{6,2},{7,3},{8,12},{9,13},{10,... | collective-permute-start | bytes 589832 | tf_op jit(solution)/shard_map/ppermute | solution.py:463
  79.4 0.0 collective-permute-start.6
  79.4 0.0 collective-permute-start.8
  79.4 0.0 copy-done.6
  79.4 4.5 %project_and_attend.6 = (bf16[1024,256]{1,0:T(8,128)(2,1)S(1)}, f32[1024,256]{1,0:T(8,128)S(1)}) custom-call(s32[3]{0:T(128)S(1)} %bitcast.14, bf16[1024,1024]{1,0:T(8,128)(2,1)S(1)} %bitcast.10, bf16[1024,768]{1,0:T(8,128)(2,1)S(1)} %copy-done.6), custom_call_target="tpu_custom_call" | custom-call | flops 2684354560 | bytes 5242880 | tf_op jit(solution)/shard_map/project_and_attend/pallas_call | solution.py:342
  83.8 0.0 collective-permute-done.5.refs_1_
  83.8 0.0 copy-start.12
  83.8 0.0 copy-start.13
  83.9 2.1 %collective-permute-start.7 = (bf16[32,3072]{1,0:T(8,128)(2,1)S(1)}, bf16[32,3072]{1,0:T(8,128)(2,1)S(1)}, u32[]{:S(2)}, u32[]{:S(2)}) collective-permute-start(bf16[32,3072]{1,0:T(8,128)(2,1)S(1)} %collective-permute-done.5.refs_1_), channel_id=1, source_target_pairs={{0,2},{1,3},{2,0},{3,1},{4,6},{5,7},{6,4},{7,5},{8,10},{9,11},{10,... | collective-permute-start | bytes 589832 | tf_op jit(solution)/shard_map/ppermute | solution.py:463
  85.9 0.2 collective-permute-start.9
  86.2 0.0 collective-permute-done.6.refs_2_
  86.2 0.3 collective-permute-start.10
  86.5 0.0 copy-done.4
  86.5 4.5 %project_and_attend.7 = (bf16[1024,256]{1,0:T(8,128)(2,1)S(1)}, f32[1024,256]{1,0:T(8,128)S(1)}) custom-call(s32[3]{0:T(128)S(1)} %bitcast.15, bf16[1024,1024]{1,0:T(8,128)(2,1)S(1)} %bitcast.11, bf16[1024,768]{1,0:T(8,128)(2,1)S(1)} %copy-done.4), custom_call_target="tpu_custom_call" | custom-call | flops 2684354560 | bytes 5242880 | tf_op jit(solution)/shard_map/project_and_attend/pallas_call | solution.py:342
  90.9 0.6 collective-permute-done.7.refs_3_
  91.5 0.0 collective-permute-start.11
  91.5 0.0 collective-permute-done.8.refs_4_
  91.5 0.0 collective-permute-done.10.refs_6_
  91.5 0.0 collective-permute-done.9.refs_5_
  91.5 1.4 %collective-permute-done.11.refs_7_ = bf16[32,3072]{1,0:T(8,128)(2,1)S(1)} collective-permute-done((bf16[32,3072]{1,0:T(8,128)(2,1)S(1)}, bf16[32,3072]{1,0:T(8,128)(2,1)S(1)}, u32[]{:S(2)}, u32[]{:S(2)}) %collective-permute-start.11) | collective-permute-done | bytes 196640 | tf_op jit(solution)/shard_map/ppermute | solution.py:463
  93.0 0.0 copy-done.12
  93.0 5.8 %apply_fast.1 = bf16[1024,1024]{1,0:T(8,128)(2,1)} custom-call(s32[1]{0:T(128)} %bitcast.pos_ref, bf16[32,3072]{1,0:T(8,128)(2,1)S(1)} %join.1.refs_0_, bf16[32,3072]{1,0:T(8,128)(2,1)S(1)} %collective-permute-done.5.refs_1_, bf16[32,3072]{1,0:T(8,128)(2,1)S(1)} %collective-permute-done.6.refs_2_, bf16[32,3072]{1,0:T(8,128)(2,1)S(1)} %collective-permute-done.7.refs_3_, ...), custom_call_target="tpu_custom_call" | custom-call | flops 3758096384 | bytes 12058624 | tf_op jit(solution)/shard_map/apply_fast/pallas_call | solution.py:415
  (10 shorter events, 0.1 us)
Async XLA Ops:
  6.0 58.3 %all-to-all-start = ((bf16[16,64,1024]{2,1,0:T(8,128)(2,1)}), bf16[16,64,1024]{2,1,0:T(8,128)(2,1)S(1)}, u32[]{:S(2)}, u32[]{:S(2)}) async-start(bf16[16,64,1024]{2,1,0:T(8,128)(2,1)} %bitcast.16), calls=%async_computation | async-start | bytes 4194304 | tf_op jit(solution)/shard_map/all_to_all | solution.py:466
  27.9 2.6 %collective-permute-start = (bf16[128,3072]{1,0:T(8,128)(2,1)}, bf16[128,3072]{1,0:T(8,128)(2,1)S(1)}, u32[]{:S(2)}, u32[]{:S(2)}) collective-permute-start(bf16[128,3072]{1,0:T(8,128)(2,1)} %get-tuple-element.36), channel_id=1, source_target_pairs={{0,1},{1,0},{2,3},{3,2},{4,5},{5,4},{6,7},{7,6},{8,9},{9,8},{10,11... | collective-permute-start | bytes 2359304 | tf_op jit(solution)/shard_map/ppermute | solution.py:463
  30.5 1.4 %copy-start.2 = (f32[128,3072]{1,0:T(8,128)S(1)}, f32[128,3072]{1,0:T(8,128)}, u32[]{:S(2)}) copy-start(f32[128,3072]{1,0:T(8,128)} %get-tuple-element.35.keep_ref) | copy-start | bytes 4718596
  32.0 16.3 %collective-permute-start.1 = (bf16[64,3072]{1,0:T(8,128)(2,1)S(1)}, bf16[64,3072]{1,0:T(8,128)(2,1)S(1)}, u32[]{:S(2)}, u32[]{:S(2)}) collective-permute-start(bf16[64,3072]{1,0:T(8,128)(2,1)S(1)} %get-tuple-element.38), channel_id=1, source_target_pairs={{0,2},{1,3},{2,0},{3,1},{4,6},{5,7},{6,4},{7,5},{8,10},{9,11},{10,... | collective-permute-start | bytes 1179656 | tf_op jit(solution)/shard_map/ppermute | solution.py:463
  34.0 2.8 %copy-start = (bf16[1024,3072]{1,0:T(8,128)(2,1)S(1)}, bf16[1024,3072]{1,0:T(8,128)(2,1)}, u32[]{:S(2)}) copy-start(bf16[1024,3072]{1,0:T(8,128)(2,1)} %in_ref.3) | copy-start | bytes 18874372
  37.2 1.2 %copy-start.7 = (bf16[1024,768]{1,0:T(8,128)(2,1)}, bf16[1024,768]{1,0:T(8,128)(2,1)S(1)}, u32[]{:S(2)}) copy-start(bf16[1024,768]{1,0:T(8,128)(2,1)S(1)} %head_weights.4.weight_ref) | copy-start | bytes 4718596
  38.9 1.1 %copy-start.5 = (bf16[1024,768]{1,0:T(8,128)(2,1)}, bf16[1024,768]{1,0:T(8,128)(2,1)S(1)}, u32[]{:S(2)}) copy-start(bf16[1024,768]{1,0:T(8,128)(2,1)S(1)} %head_weights.5.weight_ref) | copy-start | bytes 4718596
  40.1 12.6 %copy-start.14 = (s32[1,3]{1,0:T(1,128)S(1)}, s32[1,3]{1,0:T(1,128)}, u32[]{:S(2)}) copy-start(s32[1,3]{1,0:T(1,128)} %param.11) | copy-start | bytes 40
  40.6 1.2 %copy-start.3 = (bf16[1024,768]{1,0:T(8,128)(2,1)}, bf16[1024,768]{1,0:T(8,128)(2,1)S(1)}, u32[]{:S(2)}) copy-start(bf16[1024,768]{1,0:T(8,128)(2,1)S(1)} %head_weights.6.weight_ref) | copy-start | bytes 4718596
  48.3 12.8 %collective-permute-start.2 = (bf16[32,3072]{1,0:T(8,128)(2,1)S(1)}, bf16[32,3072]{1,0:T(8,128)(2,1)S(1)}, u32[]{:S(2)}, u32[]{:S(2)}) collective-permute-start(bf16[32,3072]{1,0:T(8,128)(2,1)S(1)} %get-tuple-element.42), channel_id=1, source_target_pairs={{0,4},{1,5},{2,6},{3,7},{4,0},{5,1},{6,2},{7,3},{8,12},{9,13},{10,... | collective-permute-start | bytes 589832 | tf_op jit(solution)/shard_map/ppermute | solution.py:463
  53.8 2.8 %copy-start.1 = (bf16[1024,3072]{1,0:T(8,128)(2,1)S(1)}, bf16[1024,3072]{1,0:T(8,128)(2,1)}, u32[]{:S(2)}) copy-start(bf16[1024,3072]{1,0:T(8,128)(2,1)} %in_ref.3) | copy-start | bytes 18874372
  57.2 1.2 %copy-start.9 = (bf16[1024,768]{1,0:T(8,128)(2,1)}, bf16[1024,768]{1,0:T(8,128)(2,1)S(1)}, u32[]{:S(2)}) copy-start(bf16[1024,768]{1,0:T(8,128)(2,1)S(1)} %head_weights.7.weight_ref) | copy-start | bytes 4718596
  61.2 9.1 %collective-permute-start.3 = (bf16[16,3072]{1,0:T(8,128)(2,1)S(1)}, bf16[16,3072]{1,0:T(8,128)(2,1)S(1)}, u32[]{:S(2)}, u32[]{:S(2)}) collective-permute-start(bf16[16,3072]{1,0:T(8,128)(2,1)S(1)} %get-tuple-element.46), channel_id=1, source_target_pairs={{0,8},{1,9},{2,10},{3,11},{4,12},{5,13},{6,14},{7,15},{8,0},{9,1},... | collective-permute-start | bytes 294920 | tf_op jit(solution)/shard_map/ppermute | solution.py:463
  64.4 1.4 %copy-start.10 = (bf16[1024,768]{1,0:T(8,128)(2,1)S(1)}, bf16[1024,768]{1,0:T(8,128)(2,1)}, u32[]{:S(2)}) copy-start(bf16[1024,768]{1,0:T(8,128)(2,1)} %copy-done.9) | copy-start | bytes 4718596
  65.8 4.5 %copy-start.11 = (f32[16,3,4,256]{3,2,1,0:T(4,128)S(1)}, f32[16,3,4,256]{3,2,1,0:T(4,128)}, u32[]{:S(2)}) copy-start(f32[16,3,4,256]{3,2,1,0:T(4,128)} %mom_ref.1) | copy-start | bytes 589828
  65.8 5.5 %copy-start.8 = (bf16[1024,768]{1,0:T(8,128)(2,1)S(1)}, bf16[1024,768]{1,0:T(8,128)(2,1)}, u32[]{:S(2)}) copy-start(bf16[1024,768]{1,0:T(8,128)(2,1)} %copy-done.7) | copy-start | bytes 4718596
  71.3 8.1 %copy-start.6 = (bf16[1024,768]{1,0:T(8,128)(2,1)S(1)}, bf16[1024,768]{1,0:T(8,128)(2,1)}, u32[]{:S(2)}) copy-start(bf16[1024,768]{1,0:T(8,128)(2,1)} %copy-done.5) | copy-start | bytes 4718596
  71.3 6.1 %collective-permute-start.4 = (bf16[16,3072]{1,0:T(8,128)(2,1)S(1)}, bf16[16,3072]{1,0:T(8,128)(2,1)S(1)}, u32[]{:S(2)}, u32[]{:S(2)}) collective-permute-start(bf16[16,3072]{1,0:T(8,128)(2,1)S(1)} %get-tuple-element.50.first_ref), channel_id=1, source_target_pairs={{0,8},{1,9},{2,10},{3,11},{4,12},{5,13},{6,14},{7,15},{8,0},{9,1},... | collective-permute-start | bytes 294920 | tf_op jit(solution)/shard_map/ppermute | solution.py:463
  77.4 9.1 %copy-start.4 = (bf16[1024,768]{1,0:T(8,128)(2,1)S(1)}, bf16[1024,768]{1,0:T(8,128)(2,1)}, u32[]{:S(2)}) copy-start(bf16[1024,768]{1,0:T(8,128)(2,1)} %copy-done.3) | copy-start | bytes 4718596
  77.4 6.5 %collective-permute-start.5 = (bf16[32,3072]{1,0:T(8,128)(2,1)S(1)}, bf16[32,3072]{1,0:T(8,128)(2,1)S(1)}, u32[]{:S(2)}, u32[]{:S(2)}) collective-permute-start(bf16[32,3072]{1,0:T(8,128)(2,1)S(1)} %join.1.refs_0_), channel_id=1, source_target_pairs={{0,4},{1,5},{2,6},{3,7},{4,0},{5,1},{6,2},{7,3},{8,12},{9,13},{10,... | collective-permute-start | bytes 589832 | tf_op jit(solution)/shard_map/ppermute | solution.py:463
  79.4 6.8 %collective-permute-start.6 = (bf16[32,3072]{1,0:T(8,128)(2,1)S(1)}, bf16[32,3072]{1,0:T(8,128)(2,1)S(1)}, u32[]{:S(2)}, u32[]{:S(2)}) collective-permute-start(bf16[32,3072]{1,0:T(8,128)(2,1)S(1)} %join.1.refs_0_), channel_id=1, source_target_pairs={{0,2},{1,3},{2,0},{3,1},{4,6},{5,7},{6,4},{7,5},{8,10},{9,11},{10,... | collective-permute-start | bytes 589832 | tf_op jit(solution)/shard_map/ppermute | solution.py:463
  79.4 12.2 %collective-permute-start.8 = (bf16[32,3072]{1,0:T(8,128)(2,1)S(1)}, bf16[32,3072]{1,0:T(8,128)(2,1)S(1)}, u32[]{:S(2)}, u32[]{:S(2)}) collective-permute-start(bf16[32,3072]{1,0:T(8,128)(2,1)S(1)} %join.1.refs_0_), channel_id=1, source_target_pairs={{0,1},{1,0},{2,3},{3,2},{4,5},{5,4},{6,7},{7,6},{8,9},{9,8},{10,11... | collective-permute-start | bytes 589832 | tf_op jit(solution)/shard_map/ppermute | solution.py:463
  83.8 9.1 %copy-start.12 = (bf16[1024,1024]{1,0:T(8,128)(2,1)S(1)}, bf16[1024,1024]{1,0:T(8,128)(2,1)}, u32[]{:S(2)}) copy-start(bf16[1024,1024]{1,0:T(8,128)(2,1)} %refs_17_.1) | copy-start | bytes 6291460
  83.8 9.1 %copy-start.13 = (f32[4,256]{1,0:T(4,128)S(1)}, f32[4,256]{1,0:T(4,128)}, u32[]{:S(2)}) copy-start(f32[4,256]{1,0:T(4,128)} %refs_16_.1) | copy-start | bytes 12292
  83.9 7.7 %collective-permute-start.7 = (bf16[32,3072]{1,0:T(8,128)(2,1)S(1)}, bf16[32,3072]{1,0:T(8,128)(2,1)S(1)}, u32[]{:S(2)}, u32[]{:S(2)}) collective-permute-start(bf16[32,3072]{1,0:T(8,128)(2,1)S(1)} %collective-permute-done.5.refs_1_), channel_id=1, source_target_pairs={{0,2},{1,3},{2,0},{3,1},{4,6},{5,7},{6,4},{7,5},{8,10},{9,11},{10,... | collective-permute-start | bytes 589832 | tf_op jit(solution)/shard_map/ppermute | solution.py:463
  85.9 5.6 %collective-permute-start.9 = (bf16[32,3072]{1,0:T(8,128)(2,1)S(1)}, bf16[32,3072]{1,0:T(8,128)(2,1)S(1)}, u32[]{:S(2)}, u32[]{:S(2)}) collective-permute-start(bf16[32,3072]{1,0:T(8,128)(2,1)S(1)} %collective-permute-done.5.refs_1_), channel_id=1, source_target_pairs={{0,1},{1,0},{2,3},{3,2},{4,5},{5,4},{6,7},{7,6},{8,9},{9,8},{10,11... | collective-permute-start | bytes 589832 | tf_op jit(solution)/shard_map/ppermute | solution.py:463
  86.2 5.4 %collective-permute-start.10 = (bf16[32,3072]{1,0:T(8,128)(2,1)S(1)}, bf16[32,3072]{1,0:T(8,128)(2,1)S(1)}, u32[]{:S(2)}, u32[]{:S(2)}) collective-permute-start(bf16[32,3072]{1,0:T(8,128)(2,1)S(1)} %collective-permute-done.6.refs_2_), channel_id=1, source_target_pairs={{0,1},{1,0},{2,3},{3,2},{4,5},{5,4},{6,7},{7,6},{8,9},{9,8},{10,11... | collective-permute-start | bytes 589832 | tf_op jit(solution)/shard_map/ppermute | solution.py:463
  91.5 1.4 %collective-permute-start.11 = (bf16[32,3072]{1,0:T(8,128)(2,1)S(1)}, bf16[32,3072]{1,0:T(8,128)(2,1)S(1)}, u32[]{:S(2)}, u32[]{:S(2)}) collective-permute-start(bf16[32,3072]{1,0:T(8,128)(2,1)S(1)} %collective-permute-done.7.refs_3_), channel_id=1, source_target_pairs={{0,1},{1,0},{2,3},{3,2},{4,5},{5,4},{6,7},{7,6},{8,9},{9,8},{10,11... | collective-permute-start | bytes 589832 | tf_op jit(solution)/shard_map/ppermute | solution.py:463
